TPU v7x, 128 devices: a whole 4x4x4 slice. The times are simulated.
128 devices in a mesh: len: 16 (over z, x), wid: 4 (over y), lay: 2 (over core).
Axes of the slice: x: 4, y: 4, z: 4, core: 2. Of those that a mesh axis runs over, the one named last changes fastest.
Arguments:
- displacement: float32 [3, 64, 32, 256], P(None, 'len', 'wid', 'lay'), may hold values from -0.1 to 0.1
- velocity: float32 [3, 64, 32, 256], P(None, 'len', 'wid', 'lay'), may hold values from -1.5 to 1.5
- lame_first: float32 [64, 32, 256], P('len', 'wid', 'lay'), may hold values from 0.5 to 2
- shear_modulus: float32 [64, 32, 256], P('len', 'wid', 'lay'), may hold values from 0.5 to 2
- nodal_mass: float32 [64, 32, 256], P('len', 'wid', 'lay'), may hold values from 1 to 4
- slave_nodes: int32 [16, 4, 2, 64, 128], P('len', 'wid', 'lay'), may hold values from 0 to 4095
- initial_gap: float32 [16, 4, 2, 64, 128], P('len', 'wid', 'lay'), may hold values from -0.15 to 0.1
- candidate: int32 [16, 4, 2, 64, 128], P('len', 'wid', 'lay'), may hold values from 0 to 127
- pair_owner: int32 [16, 4, 2, 64, 1], P('len', 'wid', 'lay'), may hold values from 0 to 63; in each aligned block of 64 rows (0 to 63, 64 to 127, ..., all dimensions but the last counted through in order) at most 2 rows name the same one
- pair_patch: int32 [16, 4, 2, 64], P('len', 'wid', 'lay'), may hold values from 0 to 31
- master_faces: int32 [16, 4, 2, 32, 128], P('len', 'wid', 'lay'), may hold values from 0 to 2943, as said below
Outputs:
- new_displacement: float32 [3, 64, 32, 256], P(None, 'len', 'wid', 'lay')
- new_velocity: float32 [3, 64, 32, 256], P(None, 'len', 'wid', 'lay')
Inputs may be any that keep to these rules, and one draw needn't show every extreme that they name: `slave_nodes`: local node numbers of the device's own block. `candidate`: a face's position within the pair's master patch. `pair_owner`: owners are numbered len index * 4 + wid index and share the device's lay index; among the rows of one device no owner is named more than 2 times, a bound that some block reaches. `pair_patch`: a master patch of the owner. `master_faces`: a face's first node is i * 8 * 128 + j * 128 + k with i < 3 and j < 7, so all 4 of its nodes lie on the owner.
All inputs are finite; a program needn't handle non-finite values.
Results may differ from a plain program's by a relative error of at most 0.00005.
Values sent between devices are 32-bit elements; how exact they have to be, the bound alone decides.
No kernel may reach another device: no remote copies, remote signals or barrier semaphores. Data moves between devices by JAX's collectives and lax.ppermute only.
A program may use at most 64 MiB of HBM per device.

v0:
```python
import jax
import jax.numpy as jnp
from jax import lax
from jax.sharding import PartitionSpec as P

STEPS = 2


penalty = 4.0
hourglass = 0.3
time_step = 0.25
corner_offsets = (
    (0, 0, 0),
    (1, 0, 0),
    (0, 1, 0),
    (1, 1, 0),
    (0, 0, 1),
    (1, 0, 1),
    (0, 1, 1),
    (1, 1, 1),
)


def padded_2(cells, sides, width):
    for axis, dim in sides:
        count = lax.axis_size(axis)
        ends = count - 1
        head = lax.slice_in_dim(cells, 0, width, axis=dim)
        tail = lax.slice_in_dim(cells, cells.shape[dim] - width, cells.shape[dim], axis=dim)
        cells = jnp.concatenate(
            [
                lax.ppermute(tail, axis, [(i, (i + 1) % count) for i in range(ends)]),
                cells,
                lax.ppermute(head, axis, [((i + 1) % count, i) for i in range(ends)]),
            ],
            axis=dim,
        )
    return cells


def element_mean(values, counts):
    summed = jnp.zeros(counts, jnp.float32)
    for along_x, along_y, along_z in corner_offsets:
        summed = (
            summed
            + values[
                along_x : along_x + counts[0],
                along_y : along_y + counts[1],
                along_z : along_z + counts[2],
            ]
        )
    return summed * 0.125


def corner_forces(points, lame_elem, shear_elem, counts):
    corners = []
    for along_x, along_y, along_z in corner_offsets:
        corners.append(
            points[
                :,
                along_x : along_x + counts[0],
                along_y : along_y + counts[1],
                along_z : along_z + counts[2],
            ]
        )
    mean_disp = corners[0]
    for corner in corners[1:]:
        mean_disp = mean_disp + corner
    mean_disp = mean_disp * 0.125
    columns = []
    for axis_pos in range(3):
        column = jnp.zeros_like(corners[0])
        for offsets, corner in zip(corner_offsets, corners):
            column = column + (2 * offsets[axis_pos] - 1) * corner
        columns.append(column * 0.25)
    gradient = jnp.stack(columns, axis=1)
    strain_trace = gradient[0, 0] + gradient[1, 1] + gradient[2, 2]
    stress = shear_elem * (gradient + jnp.swapaxes(gradient, 0, 1))
    stress = (
        stress + lame_elem * strain_trace * jnp.eye(3, dtype=jnp.float32)[:, :, None, None, None]
    )
    damping = hourglass * shear_elem
    forces = []
    for offsets, corner in zip(corner_offsets, corners):
        unit_signs = [2 * offsets[0] - 1, 2 * offsets[1] - 1, 2 * offsets[2] - 1]
        traction = (
            unit_signs[0] * stress[:, 0]
            + unit_signs[1] * stress[:, 1]
            + unit_signs[2] * stress[:, 2]
        )
        linear = (
            unit_signs[0] * gradient[:, 0]
            + unit_signs[1] * gradient[:, 1]
            + unit_signs[2] * gradient[:, 2]
        )
        forces.append(-0.25 * traction - damping * (corner - mean_disp - 0.5 * linear))
    return forces


def face_frame(u_flat, node_one, node_two, node_three, node_four):
    at_one = u_flat[:, node_one]
    at_two = u_flat[:, node_two]
    at_three = u_flat[:, node_three]
    at_four = u_flat[:, node_four]
    centroid = (at_one + at_two + at_three + at_four) * 0.25
    shape_tail = (3,) + (1,) * node_one.ndim
    diag_one = at_three - at_one + jnp.array([1.0, 1.0, 0.0], dtype=jnp.float32).reshape(shape_tail)
    diag_two = at_four - at_two + jnp.array([-1.0, 1.0, 0.0], dtype=jnp.float32).reshape(shape_tail)
    normal = jnp.stack(
        [
            diag_one[1] * diag_two[2] - diag_one[2] * diag_two[1],
            diag_one[2] * diag_two[0] - diag_one[0] * diag_two[2],
            diag_one[0] * diag_two[1] - diag_one[1] * diag_two[0],
        ]
    )
    normal = normal / jnp.sqrt(
        normal[0] * normal[0] + normal[1] * normal[1] + normal[2] * normal[2]
    )
    return (centroid, normal)


def contact_terms(centroid, normal, slave_disp, gap_start):
    gap_now = (
        gap_start
        + (slave_disp[0] - centroid[0]) * normal[0]
        + (slave_disp[1] - centroid[1]) * normal[1]
        + (slave_disp[2] - centroid[2]) * normal[2]
    )
    penetration = jnp.minimum(gap_now, 0.0)
    return -penalty * penetration * normal


def valid_rows(length, position, pieces):
    element_low = jnp.arange(length + 1, dtype=jnp.int32) + position * length - 1
    return ((element_low >= 0) & (element_low <= pieces * length - 2)).astype(jnp.float32)


def face_sums(values, chosen_faces):
    row_count, face_count = chosen_faces.shape
    flat_index = (
        jnp.arange(row_count, dtype=jnp.int32)[:, None] * face_count + chosen_faces
    ).reshape(-1)
    summed = (
        jnp.zeros((3, row_count * face_count), jnp.float32)
        .at[:, flat_index]
        .add(values.reshape(3, -1))
    )
    return summed.reshape(3, row_count, face_count).transpose(1, 0, 2)


def route_out(buffer):
    return lax.all_to_all(buffer, ("len", "wid"), split_axis=0, concat_axis=0, tiled=True)


def route_back(buffer):
    return lax.all_to_all(buffer, ("len", "wid"), split_axis=0, concat_axis=0, tiled=True)


def per_device(
    displacement,
    velocity,
    lame_first,
    shear_modulus,
    nodal_mass,
    slave_nodes,
    initial_gap,
    candidate,
    pair_owner,
    pair_patch,
    master_faces,
):
    span_x, span_y, span_z = (displacement.shape[1], displacement.shape[2], displacement.shape[3])
    n_len = lax.axis_size("len")
    n_wid = lax.axis_size("wid")
    groups = n_len * n_wid
    pairs = slave_nodes.shape[3]
    face_count = slave_nodes.shape[4]
    patches = master_faces.shape[3]
    capacity = max(2, 2 * pairs // groups)
    slots = groups * capacity
    node_count = span_x * span_y * span_z
    slaves = slave_nodes.reshape(pairs, face_count)
    gaps = initial_gap.reshape(pairs, face_count)
    chosen = candidate.reshape(pairs, face_count)
    owners = pair_owner.reshape(pairs)
    wanted = pair_patch.reshape(pairs)
    node_one = master_faces.reshape(patches, face_count)
    node_two = node_one + span_y * span_z
    node_three = node_one + span_y * span_z + span_z
    node_four = node_one + span_z
    member = (owners[:, None] == jnp.arange(groups, dtype=jnp.int32)[None, :]).astype(jnp.int32)
    before = jnp.cumsum(member, axis=0) - member
    rank_in = jnp.sum(before * member, axis=1)
    slot_index = owners * capacity + rank_in
    request = jnp.full((slots,), -1, jnp.int32).at[slot_index].set(wanted).reshape(groups, capacity)
    stacked = jnp.stack([lame_first, shear_modulus])
    rim = padded_2(stacked, (("len", 1), ("wid", 2), ("lay", 3)), 1)
    counts = (span_x + 1, span_y + 1, span_z + 1)
    mask_x = valid_rows(span_x, lax.axis_index("len"), n_len)
    mask_y = valid_rows(span_y, lax.axis_index("wid"), n_wid)
    mask_z = valid_rows(span_z, lax.axis_index("lay"), lax.axis_size("lay"))
    mask_all = mask_x[:, None, None] * mask_y[None, :, None] * mask_z[None, None, :]
    lame_elem = element_mean(rim[0], counts) * mask_all
    shear_elem = element_mean(rim[1], counts) * mask_all
    incoming = lax.all_to_all(request, ("len", "wid"), split_axis=0, concat_axis=0, tiled=True)
    incoming_flat = incoming.reshape(slots)
    live = incoming_flat >= 0
    safe_ids = jnp.maximum(incoming_flat, 0)
    patch_onehot = (
        (safe_ids[None, :] == jnp.arange(patches, dtype=jnp.int32)[:, None]) & live[None, :]
    ).astype(jnp.float32)
    for step in range(STEPS):
        padded = padded_2(displacement, (("len", 1), ("wid", 2), ("lay", 3)), 1)
        forces = corner_forces(padded, lame_elem, shear_elem, counts)
        internal = jnp.zeros((3, span_x, span_y, span_z), jnp.float32)
        for offsets, force in zip(corner_offsets, forces):
            internal = (
                internal
                + force[
                    :,
                    1 - offsets[0] : 1 - offsets[0] + span_x,
                    1 - offsets[1] : 1 - offsets[1] + span_y,
                    1 - offsets[2] : 1 - offsets[2] + span_z,
                ]
            )
        u_flat = displacement.reshape(3, -1)
        centroid, normal = face_frame(u_flat, node_one, node_two, node_three, node_four)
        table = jnp.concatenate([centroid, normal], axis=0).transpose(1, 0, 2)
        slave_disp = u_flat[:, slaves]
        tiles = table[safe_ids] * live[:, None, None].astype(jnp.float32)
        arrived = route_out(tiles.reshape(groups, capacity, 6, face_count))
        mine = arrived.reshape(slots, 6, face_count)[slot_index]
        picked = jnp.take_along_axis(
            mine, jnp.broadcast_to(chosen[:, None, :], (pairs, 6, face_count)), axis=2
        )
        slave_part = contact_terms(
            picked[:, 0:3].transpose(1, 0, 2), picked[:, 3:6].transpose(1, 0, 2), slave_disp, gaps
        )
        reaction = face_sums(-slave_part, chosen)
        back_buffer = jnp.zeros((slots, 3, face_count), jnp.float32).at[slot_index].set(reaction)
        returned = route_back(back_buffer.reshape(groups, capacity, 3, face_count)).reshape(
            slots, 3 * face_count
        )
        patch_react = jnp.dot(
            patch_onehot,
            returned,
            precision=lax.Precision.HIGHEST,
            preferred_element_type=jnp.float32,
        )
        quarter = 0.25 * patch_react.reshape(patches, 3, face_count).transpose(1, 0, 2)
        contact = jnp.zeros((3, node_count), jnp.float32).at[:, slaves].add(slave_part)
        contact = contact.at[:, node_one].add(quarter)
        contact = contact.at[:, node_two].add(quarter)
        contact = contact.at[:, node_three].add(quarter)
        contact = contact.at[:, node_four].add(quarter)
        total_force = internal + contact.reshape(3, span_x, span_y, span_z)
        velocity = velocity + time_step * total_force / nodal_mass[None]
        displacement = displacement + time_step * velocity
    return (displacement, velocity)


def solution(mesh):
    in_specs = (
        P(None, "len", "wid", "lay"),
        P(None, "len", "wid", "lay"),
        P("len", "wid", "lay"),
        P("len", "wid", "lay"),
        P("len", "wid", "lay"),
        P("len", "wid", "lay", None, None),
        P("len", "wid", "lay", None, None),
        P("len", "wid", "lay", None, None),
        P("len", "wid", "lay", None, None),
        P("len", "wid", "lay", None),
        P("len", "wid", "lay", None, None),
    )
    out_specs = (P(None, "len", "wid", "lay"), P(None, "len", "wid", "lay"))
    return jax.shard_map(
        per_device, mesh=mesh, in_specs=in_specs, out_specs=out_specs, check_vma=False
    )
```

profile of v0, /device:TPU:1, one launch (start us, length us, event | category | flops | bytes accessed | tf_op | source)
XLA Modules:
  0.0 1323.7 jit_solution(3233268751260198568)
XLA Ops:
  4.7 12.0 all-to-all-start
  23.6 4.6 collective-permute-start
  32.2 14.2 %gather_fusion.4 = f32[4096,3]{1,0:T(8,128)} fusion(f32[3,4096]{0,1:T(8,128)S(1)} %bitcast.317, s32[4096]{0:T(1024)S(1)} %get-tuple-element.130), kind=kCustom, calls=%fused_computation.6 | custom fusion | bytes 114688 | tf_op jit(solution)/shard_map/gather | solution.py:104
  48.6 14.2 %gather_fusion.3 = f32[4096,3]{1,0:T(8,128)} fusion(f32[3,4096]{0,1:T(8,128)S(1)} %bitcast.318, s32[4096]{0:T(1024)S(1)} %get-tuple-element.129), kind=kCustom, calls=%fused_computation.5 | custom fusion | bytes 114688 | tf_op jit(solution)/shard_map/gather | solution.py:103
  65.1 14.2 %gather_fusion.2 = f32[4096,3]{1,0:T(8,128)} fusion(f32[3,4096]{0,1:T(8,128)S(1)} %bitcast.319, s32[4096]{0:T(1024)S(1)} %get-tuple-element.128), kind=kCustom, calls=%fused_computation.4 | custom fusion | bytes 114688 | tf_op jit(solution)/shard_map/gather | solution.py:102
  81.5 14.2 %gather_fusion.1 = f32[4096,3]{1,0:T(8,128)} fusion(f32[3,4096]{0,1:T(8,128)S(1)} %bitcast.320, s32[4096]{0:T(1024)S(1)} %get-tuple-element.127), kind=kCustom, calls=%fused_computation.3 | custom fusion | bytes 114688 | tf_op jit(solution)/shard_map/gather | solution.py:101
  99.1 27.9 %gather_fusion = f32[8192,3]{1,0:T(8,128)} fusion(f32[3,4096]{0,1:T(8,128)S(1)} %bitcast.321, s32[8192]{0:T(1024)S(1)} %broadcast_clamp_fusion), kind=kCustom, calls=%fused_computation.2 | custom fusion | bytes 229376 | tf_op jit(solution)/shard_map/gather | solution.py:229
  132.7 12.1 all-to-all-start.1
  151.7 5.7 collective-permute-start.5
  178.4 286.1 %gather_fusion.14 = f32[49152]{0:T(1024)S(1)} fusion(f32[64,6,128]{2,1,0:T(8,128)S(1)} %gather_fusion.6, s32[49152]{0:T(1024)S(1)} %reshape.720), kind=kCustom, calls=%fused_computation.clone | custom fusion | bytes 983040 | tf_op jit(solution)/shard_map/jit(take_along_axis)/gather | solution.py:233
  467.7 46.5 %scatter_custom_fusion.2 = f32[3,8192]{0,1:T(8,128)} fusion(s32[8192]{0:T(1024)} %bitcast.375, f32[8192,3]{1,0:T(8,128)} %copy.210, f32[]{:T(128)} %constant.54.clone.1), kind=kCustom, calls=%fused_computation.33 | custom fusion | flops 24576 | bytes 98816 | tf_op jit(solution)/shard_map/scatter-add | solution.py:146
  520.3 11.4 all-to-all-start.2
  535.1 44.8 %scatter_custom_fusion.1 = f32[3,4096]{0,1:T(8,128)S(1)} fusion(s32[8192]{0:T(1024)} %fusion.134, f32[8192,3]{1,0:T(8,128)} %copy.209, f32[]{:T(128)} %constant.54.clone.1), kind=kCustom, calls=%fused_computation.41 | custom fusion | flops 24576 | bytes 49664 | tf_op jit(solution)/shard_map/scatter-add | solution.py:251
  584.0 23.6 %scatter_fusion.1 = f32[3,4096]{0,1:T(8,128)S(1)} fusion(f32[3,4096]{0,1:T(8,128)S(1)} %scatter_custom_fusion.1, s32[4096]{0:T(1024)S(1)} %copy-done.20, f32[4096,3]{1,0:T(8,128)} %bitcast.328), kind=kCustom, calls=%fused_computation.20 | custom fusion | flops 12288 | bytes 163840 | tf_op jit(solution)/shard_map/scatter-add | solution.py:252
  607.7 23.4 %scatter_fusion.2 = f32[3,4096]{0,1:T(8,128)S(1)} fusion(f32[3,4096]{0,1:T(8,128)S(1)} %scatter_fusion.1, s32[4096]{0:T(1024)S(1)} %copy-done.18, f32[4096,3]{1,0:T(8,128)} %bitcast.329), kind=kCustom, calls=%fused_computation.21 | custom fusion | flops 12288 | bytes 163840 | tf_op jit(solution)/shard_map/scatter-add | solution.py:253
  631.2 23.4 %scatter_fusion.3 = f32[3,4096]{0,1:T(8,128)S(1)} fusion(f32[3,4096]{0,1:T(8,128)S(1)} %scatter_fusion.2, s32[4096]{0:T(1024)S(1)} %copy-done.16, f32[4096,3]{1,0:T(8,128)} %bitcast.330), kind=kCustom, calls=%fused_computation.22 | custom fusion | flops 12288 | bytes 163840 | tf_op jit(solution)/shard_map/scatter-add | solution.py:254
  654.6 23.4 %scatter_fusion.4 = f32[3,4096]{0,1:T(8,128)S(1)} fusion(f32[3,4096]{0,1:T(8,128)S(1)} %scatter_fusion.3, s32[4096]{0:T(1024)S(1)} %copy-done.14, f32[4096,3]{1,0:T(8,128)} %bitcast.331), kind=kCustom, calls=%fused_computation.23 | custom fusion | flops 12288 | bytes 163840 | tf_op jit(solution)/shard_map/scatter-add | solution.py:255
  682.5 14.2 %gather_fusion.11 = f32[4096,3]{1,0:T(8,128)} fusion(f32[3,4096]{0,1:T(8,128)S(1)} %bitcast.312, s32[4096]{0:T(1024)S(1)} %copy-done.37), kind=kCustom, calls=%fused_computation.13 | custom fusion | bytes 114688 | tf_op jit(solution)/shard_map/gather | solution.py:104
  696.7 14.2 %gather_fusion.10 = f32[4096,3]{1,0:T(8,128)} fusion(f32[3,4096]{0,1:T(8,128)S(1)} %bitcast.313, s32[4096]{0:T(1024)S(1)} %copy-done.35), kind=kCustom, calls=%fused_computation.12 | custom fusion | bytes 114688 | tf_op jit(solution)/shard_map/gather | solution.py:103
  710.9 14.2 %gather_fusion.9 = f32[4096,3]{1,0:T(8,128)} fusion(f32[3,4096]{0,1:T(8,128)S(1)} %bitcast.314, s32[4096]{0:T(1024)S(1)} %copy-done.33), kind=kCustom, calls=%fused_computation.11 | custom fusion | bytes 114688 | tf_op jit(solution)/shard_map/gather | solution.py:102
  725.1 14.2 %gather_fusion.8 = f32[4096,3]{1,0:T(8,128)} fusion(f32[3,4096]{0,1:T(8,128)S(1)} %bitcast.315, s32[4096]{0:T(1024)S(1)} %copy-done.31), kind=kCustom, calls=%fused_computation.10 | custom fusion | bytes 114688 | tf_op jit(solution)/shard_map/gather | solution.py:101
  763.4 5.4 collective-permute-start.17
  769.8 27.9 %gather_fusion.7 = f32[8192,3]{1,0:T(8,128)} fusion(f32[3,4096]{0,1:T(8,128)S(1)} %bitcast.316, s32[8192]{0:T(1024)S(1)} %copy-done.8), kind=kCustom, calls=%fused_computation.9 | custom fusion | bytes 229376 | tf_op jit(solution)/shard_map/gather | solution.py:229
  797.7 13.5 %all-to-all-start.3 = ((f32[64,2,6,128]{3,1,2,0:T(2,128)}), f32[64,2,6,128]{3,1,2,0:T(2,128)S(1)}, u32[]{:S(2)}, u32[]{:S(2)}) async-start(f32[64,2,6,128]{3,1,2,0:T(2,128)} %copy_multiply_fusion), calls=%async_computation.3 | async-start | bytes 786432 | tf_op jit(solution)/shard_map/all_to_all | solution.py:152
  823.7 286.1 %gather_fusion.15 = f32[49152]{0:T(1024)S(1)} fusion(f32[64,6,128]{2,1,0:T(8,128)S(1)} %gather_fusion.13, s32[49152]{0:T(1024)S(1)} %reshape.720), kind=kCustom, calls=%fused_computation.1.clone | custom fusion | bytes 983040 | tf_op jit(solution)/shard_map/jit(take_along_axis)/gather | solution.py:233
  1113.0 46.5 %scatter_custom_fusion.9 = f32[3,8192]{0,1:T(8,128)} fusion(s32[8192]{0:T(1024)} %bitcast.376, f32[8192,3]{1,0:T(8,128)} %copy.231, f32[]{:T(128)} %constant.54.clone.1), kind=kCustom, calls=%fused_computation.31 | custom fusion | flops 24576 | bytes 98816 | tf_op jit(solution)/shard_map/scatter-add | solution.py:146
  1165.7 7.3 all-to-all-start.4
  1175.7 44.8 %scatter_custom_fusion.8 = f32[3,4096]{0,1:T(8,128)S(1)} fusion(s32[8192]{0:T(1024)} %fusion.134, f32[8192,3]{1,0:T(8,128)} %copy.230, f32[]{:T(128)} %constant.54.clone.1), kind=kCustom, calls=%fused_computation.39 | custom fusion | flops 24576 | bytes 49664 | tf_op jit(solution)/shard_map/scatter-add | solution.py:251
  1225.5 23.7 %scatter_fusion.6 = f32[3,4096]{0,1:T(8,128)S(1)} fusion(f32[3,4096]{0,1:T(8,128)S(1)} %scatter_custom_fusion.8, s32[4096]{0:T(1024)S(1)} %copy-done.21, f32[4096,3]{1,0:T(8,128)} %bitcast.324), kind=kCustom, calls=%fused_computation.27 | custom fusion | flops 12288 | bytes 163840 | tf_op jit(solution)/shard_map/scatter-add | solution.py:252
  1249.2 23.4 %scatter_fusion.7 = f32[3,4096]{0,1:T(8,128)S(1)} fusion(f32[3,4096]{0,1:T(8,128)S(1)} %scatter_fusion.6, s32[4096]{0:T(1024)S(1)} %copy-done.19, f32[4096,3]{1,0:T(8,128)} %bitcast.325), kind=kCustom, calls=%fused_computation.28 | custom fusion | flops 12288 | bytes 163840 | tf_op jit(solution)/shard_map/scatter-add | solution.py:253
  1272.7 23.4 %scatter_fusion.8 = f32[3,4096]{0,1:T(8,128)S(1)} fusion(f32[3,4096]{0,1:T(8,128)S(1)} %scatter_fusion.7, s32[4096]{0:T(1024)S(1)} %copy-done.17, f32[4096,3]{1,0:T(8,128)} %bitcast.326), kind=kCustom, calls=%fused_computation.29 | custom fusion | flops 12288 | bytes 163840 | tf_op jit(solution)/shard_map/scatter-add | solution.py:254
  1296.2 23.4 %scatter_fusion.9 = f32[3,4096]{0,1:T(8,128)S(1)} fusion(f32[3,4096]{0,1:T(8,128)S(1)} %scatter_fusion.8, s32[4096]{0:T(1024)S(1)} %copy-done.15, f32[4096,3]{1,0:T(8,128)} %bitcast.327), kind=kCustom, calls=%fused_computation.30 | custom fusion | flops 12288 | bytes 163840 | tf_op jit(solution)/shard_map/scatter-add | solution.py:255
  (298 shorter events, 137.0 us)
Async XLA Ops:
  4.7 125.2 %all-to-all-start = ((s32[64,1,2]{2,1,0:T(1,128)}), s32[64,1,2]{2,1,0:T(1,128)S(1)}, u32[]{:S(2)}, u32[]{:S(2)}) async-start(s32[64,1,2]{2,1,0:T(1,128)} %bitcast.40), calls=%async_computation | async-start | bytes 65536 | tf_op jit(solution)/shard_map/all_to_all | solution.py:205
  17.4 133.4 %collective-permute-start.6 = (f32[3,1,8,128]{3,2,1,0:T(8,128)S(1)}, f32[3,1,8,128]{3,2,1,0:T(8,128)S(1)}, u32[]{:S(2)}, u32[]{:S(2)}) collective-permute-start(f32[3,1,8,128]{3,2,1,0:T(8,128)S(1)} %get-tuple-element.118), channel_id=1, source_target_pairs={{0,8},{8,16},{16,24},{24,32},{32,40},{40,48},{48,56},{56,64},{64,7... | collective-permute-start | bytes 36872 | tf_op jit(solution)/shard_map/ppermute | solution.py:32
  20.3 130.6 %collective-permute-start.7 = (f32[3,1,8,128]{3,2,1,0:T(8,128)S(1)}, f32[3,1,8,128]{3,2,1,0:T(8,128)S(1)}, u32[]{:S(2)}, u32[]{:S(2)}) collective-permute-start(f32[3,1,8,128]{3,2,1,0:T(8,128)S(1)} %get-tuple-element.117), channel_id=1, source_target_pairs={{8,0},{16,8},{24,16},{32,24},{40,32},{48,40},{56,48},{64,56},{72,6... | collective-permute-start | bytes 36872 | tf_op jit(solution)/shard_map/ppermute | solution.py:34
  22.3 123.2 %collective-permute-start.1 = (f32[2,1,8,128]{3,2,1,0:T(8,128)S(1)}, f32[2,1,8,128]{3,2,1,0:T(8,128)S(1)}, u32[]{:S(2)}, u32[]{:S(2)}) collective-permute-start(f32[2,1,8,128]{3,2,1,0:T(8,128)S(1)} %get-tuple-element.120), channel_id=1, source_target_pairs={{8,0},{16,8},{24,16},{32,24},{40,32},{48,40},{56,48},{64,56},{72,6... | collective-permute-start | bytes 24584 | tf_op jit(solution)/shard_map/ppermute | solution.py:34
  23.6 121.9 %collective-permute-start = (f32[2,1,8,128]{3,2,1,0:T(8,128)S(1)}, f32[2,1,8,128]{3,2,1,0:T(8,128)S(1)}, u32[]{:S(2)}, u32[]{:S(2)}) collective-permute-start(f32[2,1,8,128]{3,2,1,0:T(8,128)S(1)} %get-tuple-element.119), channel_id=1, source_target_pairs={{0,8},{8,16},{16,24},{24,32},{32,40},{40,48},{48,56},{56,64},{64,7... | collective-permute-start | bytes 24584 | tf_op jit(solution)/shard_map/ppermute | solution.py:32
  30.3 68.6 %copy-start.38 = (pred[64,128]{1,0:T(8,128)(4,1)}, pred[64,128]{1,0:T(8,128)(4,1)S(1)}, u32[]{:S(2)}) copy-start(pred[64,128]{1,0:T(8,128)(4,1)S(1)} %broadcast_compare_fusion) | copy-start | bytes 24580
  30.9 68.2 %copy-start.7 = (s32[8192]{0:T(1024)}, s32[8192]{0:T(1024)S(1)}, u32[]{:S(2)}) copy-start(s32[8192]{0:T(1024)S(1)} %broadcast_clamp_fusion) | copy-start | bytes 98308
  97.9 66.9 %copy-start.58 = (f32[129]{0:T(256)}, f32[129]{0:T(256)S(1)}, u32[]{:S(2)}) copy-start(f32[129]{0:T(256)S(1)} %and_convert_fusion) | copy-start | bytes 1552
  132.7 44.9 %all-to-all-start.1 = ((f32[64,2,6,128]{3,1,2,0:T(2,128)}), f32[64,2,6,128]{3,1,2,0:T(2,128)S(1)}, u32[]{:S(2)}, u32[]{:S(2)}) async-start(f32[64,2,6,128]{3,1,2,0:T(2,128)} %copy_multiply_fusion.1), calls=%async_computation.1 | async-start | bytes 786432 | tf_op jit(solution)/shard_map/all_to_all | solution.py:152
  145.5 5.4 collective-permute-start.3
  146.8 4.8 collective-permute-start.2
  151.7 12.9 collective-permute-start.5
  157.4 7.2 collective-permute-start.4
  158.7 6.3 collective-permute-start.9
  160.0 5.3 collective-permute-start.8
  165.5 6.4 collective-permute-start.10
  166.8 5.1 collective-permute-start.11
  178.4 286.2 %copy-start.39 = (pred[64,128]{1,0:T(8,128)(4,1)S(1)}, pred[64,128]{1,0:T(8,128)(4,1)}, u32[]{:S(2)}) copy-start(pred[64,128]{1,0:T(8,128)(4,1)} %copy-done.38) | copy-start | bytes 24580
  178.4 286.3 %copy-start.42 = (f32[1,1,1,64,128]{4,3,2,1,0:T(8,128)S(1)}, f32[1,1,1,64,128]{4,3,2,1,0:T(8,128)}, u32[]{:S(2)}) copy-start(f32[1,1,1,64,128]{4,3,2,1,0:T(8,128)} %param.23) | copy-start | bytes 98308
  520.3 59.6 %all-to-all-start.2 = ((f32[64,2,3,128]{3,1,2,0:T(2,128)}), f32[64,2,3,128]{3,1,2,0:T(2,128)S(1)}, u32[]{:S(2)}, u32[]{:S(2)}) async-start(f32[64,2,3,128]{3,1,2,0:T(2,128)} %copy.212), calls=%async_computation.2 | async-start | bytes 393216 | tf_op jit(solution)/shard_map/all_to_all | solution.py:156
  584.0 70.6 %copy-start.14 = (s32[4096]{0:T(1024)S(1)}, s32[4096]{0:T(1024)}, u32[]{:S(2)}) copy-start(s32[4096]{0:T(1024)} %get-tuple-element.123) | copy-start | bytes 49156
  748.2 5.6 collective-permute-start.13
  749.6 4.8 collective-permute-start.12
  754.4 6.3 collective-permute-start.15
  755.7 5.0 collective-permute-start.14
  762.1 52.0 %collective-permute-start.16 = (f32[3,6,10,1]{3,2,1,0:T(8,128)S(1)}, f32[3,6,10,1]{3,2,1,0:T(8,128)}, u32[]{:S(2)}, u32[]{:S(2)}) collective-permute-start(f32[3,6,10,1]{3,2,1,0:T(8,128)S(1)} %get-tuple-element.85), channel_id=1, source_target_pairs={{0,1},{2,3},{4,5},{6,7},{8,9},{10,11},{12,13},{14,15},{16,17},{18,... | collective-permute-start | bytes 2168 | tf_op jit(solution)/shard_map/ppermute | solution.py:32
  763.4 50.7 %collective-permute-start.17 = (f32[3,6,10,1]{3,2,1,0:T(8,128)S(1)}, f32[3,6,10,1]{3,2,1,0:T(8,128)}, u32[]{:S(2)}, u32[]{:S(2)}) collective-permute-start(f32[3,6,10,1]{3,2,1,0:T(8,128)S(1)} %get-tuple-element.86), channel_id=1, source_target_pairs={{1,0},{3,2},{5,4},{7,6},{9,8},{11,10},{13,12},{15,14},{17,16},{19,... | collective-permute-start | bytes 2168 | tf_op jit(solution)/shard_map/ppermute | solution.py:34
  797.7 25.2 %all-to-all-start.3 = ((f32[64,2,6,128]{3,1,2,0:T(2,128)}), f32[64,2,6,128]{3,1,2,0:T(2,128)S(1)}, u32[]{:S(2)}, u32[]{:S(2)}) async-start(f32[64,2,6,128]{3,1,2,0:T(2,128)} %copy_multiply_fusion), calls=%async_computation.3 | async-start | bytes 786432 | tf_op jit(solution)/shard_map/all_to_all | solution.py:152
  823.7 286.2 %copy-start.40 = (pred[64,128]{1,0:T(8,128)(4,1)S(1)}, pred[64,128]{1,0:T(8,128)(4,1)}, u32[]{:S(2)}) copy-start(pred[64,128]{1,0:T(8,128)(4,1)} %copy-done.38) | copy-start | bytes 24580
  823.7 286.3 %copy-start.43 = (f32[1,1,1,64,128]{4,3,2,1,0:T(8,128)S(1)}, f32[1,1,1,64,128]{4,3,2,1,0:T(8,128)}, u32[]{:S(2)}) copy-start(f32[1,1,1,64,128]{4,3,2,1,0:T(8,128)} %param.23) | copy-start | bytes 98308
  1165.7 54.8 %all-to-all-start.4 = ((f32[64,2,3,128]{3,1,2,0:T(2,128)}), f32[64,2,3,128]{3,1,2,0:T(2,128)}, u32[]{:S(2)}, u32[]{:S(2)}) async-start(f32[64,2,3,128]{3,1,2,0:T(2,128)} %copy.233), calls=%async_computation.4 | async-start | bytes 393216 | tf_op jit(solution)/shard_map/all_to_all | solution.py:156
  1225.5 70.7 %copy-start.15 = (s32[4096]{0:T(1024)S(1)}, s32[4096]{0:T(1024)}, u32[]{:S(2)}) copy-start(s32[4096]{0:T(1024)} %get-tuple-element.123) | copy-start | bytes 49156
  (55 other events, 1367.0 us)
where the time goes:
time: 1330 us; the launch traced here: 1320 us
  local copies, waits for them, and re-layouts  809 us (61%)
  other arithmetic  398 us (30%)
  starting transfers between devices  107 us (8%)
    gather x5, local copies, waits for them, and re-layouts, per_device(): jnp.take_along_axis(mine, jnp.broadcast_to(chosen[:, None, :], (pairs, 6,...  572 us
    scatter-add x2, other arithmetic, face_sums(): summed = jnp.zeros((3, row_count * face_count), jnp.float32).at[:, flat_i...  93.1 us
    scatter-add x2, other arithmetic, per_device(): jnp.zeros((3, node_count), jnp.float32).at[:, slaves].add(slave_part)  89.6 us
    gather x4, local copies, waits for them, and re-layouts, per_device(): slave_disp = u_flat[:, slaves]  61.5 us
    scatter-add x2, other arithmetic, per_device(): contact = contact.at[:, node_one].add(quarter)  47.3 us
    scatter-add x2, other arithmetic, per_device(): contact = contact.at[:, node_two].add(quarter)  46.9 us
    scatter-add x2, other arithmetic, per_device(): contact = contact.at[:, node_three].add(quarter)  46.9 us
    scatter-add x2, other arithmetic, per_device(): contact = contact.at[:, node_four].add(quarter)  46.9 us
  transfers between devices with their start and end apart: 23, of which 4 were waited for; matrix products, arithmetic and copies ran while one was open for 19% of the time, Pallas kernels for 0%

commit v1 on v0

v1 whole, which is shorter than its diff:
```python
import jax
import jax.numpy as jnp
from jax import lax
from jax.experimental import pallas as pl
from jax.experimental.pallas import tpu as pltpu
from jax.sharding import PartitionSpec as P

STEPS = 2
PENALTY = 4.0
HOURGLASS = 0.3
TIME_STEP = 0.25

NI, NJ, NK = 4, 8, 128
ROWS = NI * NJ
PAIRS = 64
PATCH = 128
PATCHES = 32
GROUPS = 64
CAP = 2
SLOTS = GROUPS * CAP
F32 = jnp.float32
BF16 = jnp.bfloat16
I32 = jnp.int32


def iota(shape, axis):
    return lax.broadcasted_iota(I32, shape, axis)


def lane_pick(values, index):
    return jnp.take_along_axis(values, index, axis=1, mode="promise_in_bounds")


def parts_3(x):
    high = x.astype(BF16)
    rest = x - high.astype(F32)
    mid = rest.astype(BF16)
    low = (rest - mid.astype(F32)).astype(BF16)
    return high, mid, low


def select_dot(onehot, x):
    high, mid, low = parts_3(x)
    out = jnp.dot(onehot, low, preferred_element_type=F32)
    out = out + jnp.dot(onehot, mid, preferred_element_type=F32)
    return out + jnp.dot(onehot, high, preferred_element_type=F32)


def gather_nodes(u_ref, nodes):
    row = nodes >> 7
    lane = nodes & 127
    out = [jnp.zeros((PAIRS, PATCH), F32) for _ in range(3)]
    for r in range(ROWS):
        here = row == r
        for c in range(3):
            source = jnp.broadcast_to(u_ref[c, r : r + 1, :], (PAIRS, PATCH))
            out[c] = jnp.where(here, lane_pick(source, lane), out[c])
    return out


def up(x, amount):
    return pltpu.roll(x, x.shape[0] - amount, 0)


def patch_table(u_ref, faces):
    frames = []
    one = [u_ref[c] for c in range(3)]
    two = [up(x, 8) for x in one]
    three = [up(x, 9) for x in one]
    four = [up(x, 1) for x in one]
    centroid = [(one[c] + two[c] + three[c] + four[c]) * 0.25 for c in range(3)]
    da = [three[0] - one[0] + 1.0, three[1] - one[1] + 1.0, three[2] - one[2]]
    db = [four[0] - two[0] - 1.0, four[1] - two[1] + 1.0, four[2] - two[2]]
    normal = [
        da[1] * db[2] - da[2] * db[1],
        da[2] * db[0] - da[0] * db[2],
        da[0] * db[1] - da[1] * db[0],
    ]
    length = jnp.sqrt(normal[0] * normal[0] + normal[1] * normal[1] + normal[2] * normal[2])
    normal = [x / length for x in normal]
    offset = centroid[0] * normal[0] + centroid[1] * normal[1] + centroid[2] * normal[2]
    frames = normal + [offset]
    row = faces >> 7
    lane = faces & 127
    out = [jnp.zeros((PATCHES, PATCH), F32) for _ in range(4)]
    for r in range((NI - 1) * NJ):
        if r % NJ == NJ - 1:
            continue
        here = row == r
        for c in range(4):
            source = jnp.broadcast_to(frames[c][r : r + 1, :], (PATCHES, PATCH))
            out[c] = jnp.where(here, lane_pick(source, lane), out[c])
    table = jnp.concatenate(out, axis=1)
    high, mid, low = parts_3(table)
    return jnp.concatenate([high, mid, low, jnp.zeros_like(high)], axis=0)


def scatter_nodes(count, row_lane, forces_ref):
    acc = jnp.zeros((6 * ROWS, PATCH), F32)
    row_at = iota((ROWS, PATCH), 0)
    lane_at = iota((PATCH, PATCH), 0)

    def body(i, acc):
        start = pl.multiple_of(i * 8, 8)
        rows, lanes = row_lane(start)
        parts = [forces_ref[c, pl.ds(start, 8), :] for c in range(6)]
        left = []
        right = []
        for q in range(8):
            here = jnp.broadcast_to(rows[q : q + 1, :], (ROWS, PATCH)) == row_at
            pieces = [
                jnp.where(here, jnp.broadcast_to(part[q : q + 1, :], (ROWS, PATCH)), 0.0)
                for part in parts
            ]
            left.append(jnp.concatenate(pieces, axis=0).astype(BF16))
            chosen = jnp.broadcast_to(lanes[q : q + 1, :], (PATCH, PATCH)) == lane_at
            right.append(jnp.where(chosen, 1.0, 0.0).astype(BF16))
        left = jnp.concatenate(left, axis=1)
        right = jnp.concatenate(right, axis=1)
        return acc + lax.dot_general(
            left, right, (((1,), (1,)), ((), ())), preferred_element_type=F32
        )

    acc = lax.fori_loop(0, count // 8, body, acc)
    return [acc[c * ROWS : (c + 1) * ROWS] + acc[(c + 3) * ROWS : (c + 4) * ROWS] for c in range(3)]


def store_parts(forces_ref, c, start, force):
    high = force.astype(BF16).astype(F32)
    forces_ref[c, start : start + force.shape[0], :] = high
    forces_ref[c + 3, start : start + force.shape[0], :] = force - high


def down_rows(x, amount):
    moved = pltpu.roll(x, amount, 0)
    return jnp.where(iota(x.shape, 0) >= amount, moved, 0.0)


def pair_force(u, normal, offset, gap):
    now = gap + (u[0] * normal[0] + u[1] * normal[1] + u[2] * normal[2]) - offset
    push = -PENALTY * jnp.minimum(now, 0.0)
    return [push * normal[c] for c in range(3)]


def every(ref, start, stride):
    return ref[pl.ds(start, GROUPS, stride=stride), :]


def slabs_kernel(disp, lame, shear, five, low, high):
    for c in range(5):
        block = disp[c] if c < 3 else (lame[...] if c == 3 else shear[...])
        five[c] = block
        low[c] = block[0]
        high[c] = block[NI - 1]


def rim_kernel(block, x_low, x_high, y_low, y_high):
    for c in range(block.shape[0]):
        for out, j in ((y_low, 0), (y_high, NJ - 1)):
            out[c, 0:1, :] = x_low[c, j : j + 1, :]
            for i in range(NI):
                out[c, i + 1 : i + 2, :] = block[c, i, j : j + 1, :]
            out[c, 5:6, :] = x_high[c, j : j + 1, :]
            out[c, 6:8, :] = jnp.zeros((2, NK), F32)


def extend_kernel(block, x_low, x_high, y_low, y_high, out):
    for c in range(block.shape[0]):
        for i in range(NI + 2):
            if i == 0:
                middle = x_low[c]
            elif i == NI + 1:
                middle = x_high[c]
            else:
                middle = block[c, i - 1]
            out[c, i, 1:9, :] = middle
            out[c, i, 0:1, :] = y_low[c, i : i + 1, :]
            out[c, i, 9:10, :] = y_high[c, i : i + 1, :]
            out[c, i, 10:16, :] = jnp.zeros((6, NK), F32)


def far_plane(near, other):
    lay = lax.axis_index("lay")
    lane = iota(near.shape, 2)
    edge = jnp.where(lay == 0, 0, NK - 1)
    shift = jnp.where(lay == 0, NK - 1, 1)
    return pltpu.roll(jnp.where(lane == edge, other, near), shift, 2)


def from_far(x):
    lay = lax.axis_index("lay")
    lane = iota(x.shape, 2)
    edge = jnp.where(lay == 0, 0, NK - 1)
    shift = jnp.where(lay == 0, 1, NK - 1)
    return jnp.where(lane == edge, 0.0, pltpu.roll(x, shift, 2))


def next_row(x):
    return pltpu.roll(x, x.shape[1] - 1, 1)


def element_moduli(near, other):
    total = near + far_plane(near, other)
    total = total + next_row(total)
    total = (total[0:5] + total[1:6]) * 0.125
    plane = iota(total.shape, 0)
    row = iota(total.shape, 1)
    at_len = lax.axis_index("len")
    at_wid = lax.axis_index("wid")
    outside = (plane == 0) & (at_len == 0)
    outside |= (plane == NI) & (at_len == lax.axis_size("len") - 1)
    outside |= (row == 0) & (at_wid == 0)
    outside |= (row == NJ) & (at_wid == lax.axis_size("wid") - 1)
    return jnp.where(outside, 0.0, total)


def internal_force(near_ref, other_ref, lame, shear):
    sigma = jnp.where(lax.axis_index("lay") == 0, 1.0, -1.0)
    grad = []
    means = []
    for c in range(3):
        near = near_ref[c]
        far = far_plane(near, other_ref[c])
        both = far + near
        diff = far - near
        both_next = next_row(both)
        sums = both + both_next
        cross = both_next - both
        tall = diff + next_row(diff)
        means.append((sums[0:5] + sums[1:6]) * 0.125)
        grad.append(
            [
                (sums[1:6] - sums[0:5]) * 0.25,
                (cross[0:5] + cross[1:6]) * 0.25,
                (tall[0:5] + tall[1:6]) * (0.25 * sigma),
            ]
        )
    pressure = lame * (grad[0][0] + grad[1][1] + grad[2][2])
    damping = HOURGLASS * shear
    damp_x = damping[0:4] + damping[1:5]
    damp_y = damp_x + next_row(damp_x)
    damp = (damp_y + from_far(damp_y))[:, 0:8]
    out = []
    for c in range(3):
        flux = []
        for j in range(3):
            stress = shear * (grad[c][j] + grad[j][c])
            if c == j:
                stress = stress + pressure
            flux.append(0.5 * damping * grad[c][j] - 0.25 * stress)
        lead = damping * means[c]
        depth = flux[2] * sigma
        lead_x = (lead[0:4] + lead[1:5]) + (flux[0][0:4] - flux[0][1:5])
        side_x = flux[1][0:4] + flux[1][1:5]
        depth_x = depth[0:4] + depth[1:5]
        lead_y = (lead_x + next_row(lead_x)) + (side_x - next_row(side_x))
        depth_y = depth_x + next_row(depth_x)
        force = (lead_y - depth_y) + from_far(lead_y + depth_y)
        out.append(force[:, 0:8] - near_ref[c, 1:5, 1:9, :] * damp)
    return out


def internal_first_kernel(near, other, out, moduli):
    lame = element_moduli(near[3], other[3])
    shear = element_moduli(near[4], other[4])
    moduli[0] = lame
    moduli[1] = shear
    for c, force in enumerate(internal_force(near, other, lame, shear)):
        out[c] = force


def internal_kernel(near, other, moduli, out):
    for c, force in enumerate(internal_force(near, other, moduli[0], moduli[1])):
        out[c] = force


def column_to_row(column):
    size = column.shape[0]
    eye = iota((size, size), 0) == iota((size, size), 1)
    return jnp.sum(jnp.where(eye, column, 0.0), axis=0, keepdims=True)


def row_to_column(row):
    size = row.shape[1]
    eye = iota((size, size), 0) == iota((size, size), 1)
    return jnp.sum(jnp.where(eye, row, 0.0), axis=1, keepdims=True)


def request_kernel(u, slaves, gaps, chosen, owners, wanted, send, slot_of, at_slaves):
    owner = owners[...].astype(F32)
    owner_row = column_to_row(owner)
    same = (owner == owner_row) & (iota((PAIRS, PAIRS), 1) < iota((PAIRS, PAIRS), 0))
    rank = jnp.max(jnp.where(same, 1.0, 0.0), axis=1, keepdims=True)
    slot = rank * GROUPS + owner
    slot_row = column_to_row(slot)
    slot_of[...] = jnp.where(slot == iota((PAIRS, SLOTS), 1).astype(F32), 1.0, 0.0)
    place = jnp.where(slot_row == iota((SLOTS, PAIRS), 0).astype(F32), 1.0, 0.0).astype(BF16)
    values = gather_nodes(u, slaves[...])
    for c in range(3):
        at_slaves[c] = values[c]
    exact = jnp.concatenate(values + [gaps[...]], axis=1)
    moved = select_dot(place, exact)
    patch = jnp.broadcast_to(row_to_column(wanted[...].astype(F32) + 1.0), (PAIRS, PATCH))
    whole = jnp.concatenate([chosen[...].astype(F32), patch], axis=1).astype(BF16)
    moved_whole = jnp.dot(place, whole, preferred_element_type=F32)
    for t in range(CAP):
        part = slice(t * GROUPS, (t + 1) * GROUPS)
        for c in range(4):
            send[pl.ds(t * 4 + c, GROUPS, stride=16), :] = moved[part, c * 128 : (c + 1) * 128]
        for c in range(2):
            send[pl.ds(8 + t * 2 + c, GROUPS, stride=16), :] = moved_whole[
                part, c * 128 : (c + 1) * 128
            ]
    for c in range(12, 16):
        send[pl.ds(c, GROUPS, stride=16), :] = jnp.zeros((GROUPS, PATCH), F32)


def wanted_rows(arrived):
    patch = jnp.concatenate([every(arrived, 9, 16), every(arrived, 11, 16)], axis=0)
    cand = jnp.concatenate([every(arrived, 8, 16), every(arrived, 10, 16)], axis=0)
    at = (iota((SLOTS, PATCH), 1) % PATCHES + 1).astype(F32)
    onehot = jnp.where(patch == at, 1.0, 0.0).astype(BF16)
    return onehot, cand.astype(I32)


def table_kernel(u, faces, table):
    table[...] = patch_table(u, faces[...])


def reply_kernel(arrived, table, faces, send, face_row, face_lane):
    onehot, cand = wanted_rows(arrived)
    tiles = jnp.dot(onehot, table[...], preferred_element_type=F32)
    for c in range(4):
        picked = lane_pick(tiles[:, c * 128 : (c + 1) * 128], cand)
        for t in range(CAP):
            send[pl.ds(t * 4 + c, GROUPS, stride=8), :] = picked[t * GROUPS : (t + 1) * GROUPS]
    index = jnp.concatenate([faces[...] >> 7, faces[...] & 127], axis=1).astype(F32)
    index = jnp.concatenate(
        [index, jnp.zeros((PATCH - PATCHES, 2 * PATCH), F32)], axis=0
    ).astype(BF16)
    index = jnp.dot(onehot, index, preferred_element_type=F32)
    face_row[...] = lane_pick(index[:, 0:128], cand).astype(I32)
    face_lane[...] = lane_pick(index[:, 128:256], cand).astype(I32)


def owner_forces(values, gap_source, frames, stride, offset, frame_stride, frame_offset, scratch):
    for t in range(CAP):
        u = [every(values, t * offset + c, stride) for c in range(3)]
        gap = every(gap_source, t * 4 + 3, 16)
        frame = [every(frames, t * frame_offset[1] + frame_offset[0] + c, frame_stride) for c in range(4)]
        force = pair_force(u, frame[0:3], frame[3], gap)
        for c in range(3):
            store_parts(scratch, c, t * GROUPS, -0.25 * force[c])


def face_contact(face_row, face_lane, scratch):
    def row_lane(start):
        return face_row[pl.ds(start, 8), :], face_lane[pl.ds(start, 8), :]

    faces = scatter_nodes(SLOTS, row_lane, scratch)
    return [x + down_rows(x, 8) + down_rows(x, 9) + down_rows(x, 1) for x in faces]


def slave_contact(arrived, stride, offset, slot_of, at_slaves, gaps, slaves, scratch):
    onehot = slot_of[...].astype(BF16)
    slots = []
    for c in range(4):
        slots.append(
            jnp.concatenate(
                [every(arrived, t * offset[1] + offset[0] + c, stride) for t in range(CAP)], axis=0
            )
        )
    mine = select_dot(onehot, jnp.concatenate(slots, axis=1))
    frame = [mine[:, c * 128 : (c + 1) * 128] for c in range(4)]
    force = pair_force([at_slaves[c] for c in range(3)], frame[0:3], frame[3], gaps[...])
    for c in range(3):
        store_parts(scratch, c, 0, force[c])

    def row_lane(start):
        nodes = slaves[pl.ds(start, 8), :]
        return nodes >> 7, nodes & 127

    return scatter_nodes(PAIRS, row_lane, scratch)


def reaction_kernel(arrived, frames, face_row, face_lane, out, scratch):
    owner_forces(arrived, arrived, frames, 16, 4, 8, (0, 4), scratch)
    for c, force in enumerate(face_contact(face_row, face_lane, scratch)):
        out[c] = force


def advance(c, force, disp, vel, mass, new_disp, new_vel):
    moved = vel[c] + TIME_STEP * force / mass[...]
    new_vel[c] = moved
    place = disp[c] + TIME_STEP * moved
    new_disp[c] = place
    return place


def middle_kernel(
    arrived, slot_of, at_slaves, gaps, slaves, reaction, internal, disp, vel, mass,
    new_disp, new_vel, low, high, scratch,
):
    contact = slave_contact(arrived, 8, (0, 4), slot_of, at_slaves, gaps, slaves, scratch)
    for c in range(3):
        force = internal[c] + (contact[c] + reaction[c])
        place = advance(c, force, disp, vel, mass, new_disp, new_vel)
        low[c] = place[0:NJ]
        high[c] = place[ROWS - NJ : ROWS]


def second_kernel(u, slaves, faces, slot_of, arrived, send, at_slaves):
    values = gather_nodes(u, slaves[...])
    for c in range(3):
        at_slaves[c] = values[c]
    place = slot_of[...].astype(BF16)
    high, mid, low = parts_3(jnp.concatenate(values, axis=1))
    dims = (((0,), (0,)), ((), ()))
    moved = lax.dot_general(place, low, dims, preferred_element_type=F32)
    moved = moved + lax.dot_general(place, mid, dims, preferred_element_type=F32)
    moved = moved + lax.dot_general(place, high, dims, preferred_element_type=F32)
    table = patch_table(u, faces[...])
    onehot, cand = wanted_rows(arrived)
    tiles = jnp.dot(onehot, table, preferred_element_type=F32)
    for t in range(CAP):
        part = slice(t * GROUPS, (t + 1) * GROUPS)
        for c in range(3):
            send[pl.ds(t * 8 + c, GROUPS, stride=16), :] = moved[part, c * 128 : (c + 1) * 128]
        send[pl.ds(t * 8 + 7, GROUPS, stride=16), :] = jnp.zeros((GROUPS, PATCH), F32)
    for c in range(4):
        picked = lane_pick(tiles[:, c * 128 : (c + 1) * 128], cand)
        for t in range(CAP):
            send[pl.ds(t * 8 + 3 + c, GROUPS, stride=16), :] = picked[
                t * GROUPS : (t + 1) * GROUPS
            ]


def last_kernel(
    arrived, sent, first, face_row, face_lane, slot_of, at_slaves, gaps, slaves, internal,
    disp, vel, mass, new_disp, new_vel, scratch, slave_scratch,
):
    owner_forces(arrived, first, sent, 16, 8, 16, (3, 8), scratch)
    reaction = face_contact(face_row, face_lane, scratch)
    contact = slave_contact(arrived, 16, (3, 8), slot_of, at_slaves, gaps, slaves, slave_scratch)
    for c in range(3):
        force = internal[c] + (contact[c] + reaction[c])
        advance(c, force, disp, vel, mass, new_disp, new_vel)


def f32(*shape):
    return jax.ShapeDtypeStruct(shape, F32)


def i32(*shape):
    return jax.ShapeDtypeStruct(shape, I32)


def call(kernel, outs, *args, scratch=()):
    return pl.pallas_call(
        kernel,
        out_shape=outs,
        scratch_shapes=[pltpu.VMEM(s, F32) for s in scratch],
        name=kernel.__name__,
    )(*args)


def shift_pair(low, high, axis):
    count = lax.axis_size(axis)
    from_low = lax.ppermute(high, axis, [(i, i + 1) for i in range(count - 1)])
    from_high = lax.ppermute(low, axis, [(i + 1, i) for i in range(count - 1)])
    return from_low, from_high


def extended(block, low, high):
    parts = block.shape[0]
    x_low, x_high = shift_pair(low, high, "len")
    low, high = call(rim_kernel, (f32(parts, 8, NK), f32(parts, 8, NK)), block, x_low, x_high)
    y_low, y_high = shift_pair(low, high, "wid")
    near = call(
        extend_kernel, f32(parts, NI + 2, 16, NK), block, x_low, x_high, y_low, y_high
    )
    return near, lax.ppermute(near, "lay", [(0, 1), (1, 0)])


def exchange(buffer):
    chunk = buffer.reshape(GROUPS, -1, PATCH)
    out = lax.all_to_all(chunk, ("len", "wid"), split_axis=0, concat_axis=0, tiled=True)
    return out.reshape(buffer.shape)


def per_device(
    displacement, velocity, lame_first, shear_modulus, nodal_mass, slave_nodes, initial_gap,
    candidate, pair_owner, pair_patch, master_faces,
):
    slaves = slave_nodes.reshape(PAIRS, PATCH)
    gaps = initial_gap.reshape(PAIRS, PATCH)
    chosen = candidate.reshape(PAIRS, PATCH)
    owners = pair_owner.reshape(PAIRS, 1)
    wanted = pair_patch.reshape(1, PAIRS)
    faces = master_faces.reshape(PATCHES, PATCH)
    u = displacement.reshape(3, ROWS, NK)
    v = velocity.reshape(3, ROWS, NK)
    mass = nodal_mass.reshape(ROWS, NK)
    five, low, high = call(
        slabs_kernel,
        (f32(5, NI, NJ, NK), f32(5, NJ, NK), f32(5, NJ, NK)),
        displacement, lame_first, shear_modulus,
    )
    near, other = extended(five, low, high)
    send, slot_of, at_slaves = call(
        request_kernel,
        (f32(GROUPS * 16, PATCH), f32(PAIRS, SLOTS), f32(3, PAIRS, PATCH)),
        u, slaves, gaps, chosen, owners, wanted,
    )
    first = exchange(send)
    table = call(table_kernel, jax.ShapeDtypeStruct((128, 512), BF16), u, faces)
    reply, face_row, face_lane = call(
        reply_kernel,
        (f32(GROUPS * 8, PATCH), i32(SLOTS, PATCH), i32(SLOTS, PATCH)),
        first, table, faces,
    )
    arrived = exchange(reply)
    reaction = call(
        reaction_kernel, f32(3, ROWS, NK), first, reply, face_row, face_lane,
        scratch=[(6, SLOTS, PATCH)],
    )
    internal, moduli = call(
        internal_first_kernel, (f32(3, NI, NJ, NK), f32(2, 5, 16, NK)), near, other
    )
    u, v, low, high = call(
        middle_kernel,
        (f32(3, ROWS, NK), f32(3, ROWS, NK), f32(3, NJ, NK), f32(3, NJ, NK)),
        arrived, slot_of, at_slaves, gaps, slaves, reaction, internal.reshape(3, ROWS, NK),
        u, v, mass,
        scratch=[(6, PAIRS, PATCH)],
    )
    near, other = extended(u.reshape(3, NI, NJ, NK), low, high)
    sent, at_slaves = call(
        second_kernel,
        (f32(GROUPS * 16, PATCH), f32(3, PAIRS, PATCH)),
        u, slaves, faces, slot_of, first,
    )
    arrived = exchange(sent)
    internal = call(internal_kernel, f32(3, NI, NJ, NK), near, other, moduli)
    u, v = call(
        last_kernel,
        (f32(3, ROWS, NK), f32(3, ROWS, NK)),
        arrived, sent, first, face_row, face_lane, slot_of, at_slaves, gaps, slaves,
        internal.reshape(3, ROWS, NK), u, v, mass,
        scratch=[(6, SLOTS, PATCH), (6, PAIRS, PATCH)],
    )
    return u.reshape(displacement.shape), v.reshape(velocity.shape)


def solution(mesh):
    nodal = P("len", "wid", "lay")
    vector = P(None, "len", "wid", "lay")
    in_specs = (
        vector, vector, nodal, nodal, nodal,
        P("len", "wid", "lay", None, None),
        P("len", "wid", "lay", None, None),
        P("len", "wid", "lay", None, None),
        P("len", "wid", "lay", None, None),
        P("len", "wid", "lay", None),
        P("len", "wid", "lay", None, None),
    )
    return jax.shard_map(
        per_device, mesh=mesh, in_specs=in_specs, out_specs=(vector, vector), check_vma=False
    )
```

time: 1330 us -> 128 us (0.10)
  local copies, waits for them, and re-layouts: 809 us -> 8.02 us
  other arithmetic: 398 us -> 0 us
  starting transfers between devices: 107 us -> 58.3 us
  Pallas kernels: 0 us -> 45.5 us
    gather x29 -> x0, local copies, waits for them, and re-layouts: 768 us -> none  [the longest x5 572 us: per_device(): jnp.take_along_axis(mine, jnp.broadcast_to(chosen[:, None, :], (pairs, 6,...]
    scatter-add x12 -> x0, other arithmetic: 371 us -> none  [the longest x2 93.1 us: face_sums(): summed = jnp.zeros((3, row_count * face_count), jnp.float32).at[:, flat_i...]
    pallas_call x0 -> x14, Pallas kernels: none -> 45.5 us  [call(): pl.pallas_call(kernel, out_shape=outs, scratch_shapes=[pltpu.VMEM(s, F32)...]
    ppermute x18 -> x10, starting transfers between devices: 51.2 us -> 24 us  [the longest x4 12 us: shift_pair(): from_low = lax.ppermute(high, axis, [(i, i + 1) for i in range(count - 1)])]
    all_to_all x5 -> x3, starting transfers between devices: 56.3 us -> 34.3 us  [exchange(): lax.all_to_all(chunk, ('len', 'wid'), split_axis=0, concat_axis=0, tiled=...]
  transfers between devices with their start and end apart: 23 -> 13, of which waited for: 4 -> 6; matrix products, arithmetic and copies ran while one was open for 19% -> 0% of each run, Pallas kernels for 0% -> 18%
where the time goes in v1:
time: 128 us; the launch traced here: 126 us
  starting transfers between devices  58.3 us (46%)
  Pallas kernels  45.5 us (36%)
  waiting for transfers between devices  13.2 us (10%)
  local copies, waits for them, and re-layouts  8.02 us (6%)
    pallas_call x14, Pallas kernels, call(): pl.pallas_call(kernel, out_shape=outs, scratch_shapes=[pltpu.VMEM(s, F32)...  45.5 us
    all_to_all x3, starting transfers between devices, exchange(): lax.all_to_all(chunk, ('len', 'wid'), split_axis=0, concat_axis=0, tiled=...  34.3 us
    ppermute x4, starting transfers between devices, shift_pair(): from_low = lax.ppermute(high, axis, [(i, i + 1) for i in range(count - 1)])  12 us
    ppermute x4, waiting for transfers between devices, shift_pair(): from_high = lax.ppermute(low, axis, [(i + 1, i) for i in range(count - 1)])  9.58 us
    unnamed x32, local copies, waits for them, and re-layouts  7.31 us
    ppermute x2, starting transfers between devices, extended(): return (near, lax.ppermute(near, 'lay', [(0, 1), (1, 0)]))  6.88 us
    ppermute x4, starting transfers between devices, shift_pair(): from_high = lax.ppermute(low, axis, [(i + 1, i) for i in range(count - 1)])  5.17 us
    ppermute x2, waiting for transfers between devices, extended(): return (near, lax.ppermute(near, 'lay', [(0, 1), (1, 0)]))  2.57 us
  transfers between devices with their start and end apart: 13, of which 6 were waited for; matrix products, arithmetic and copies ran while one was open for 0% of the time, Pallas kernels for 18%

profile of v1, /device:TPU:1, one launch (start us, length us, event | category | flops | bytes accessed | tf_op | source)
XLA Modules:
  0.0 125.9 jit_solution(5604818876488855501)
XLA Ops:
  2.0 4.2 %request_kernel.1 = (f32[1024,128]{1,0:T(8,128)}, f32[64,128]{1,0:T(8,128)}, f32[3,64,128]{2,1,0:T(8,128)}) custom-call(f32[3,32,128]{2,1,0:T(8,128)} %bitcast.28, s32[64,128]{1,0:T(8,128)} %bitcast.33, f32[64,128]{1,0:T(8,128)} %bitcast.38, s32[64,128]{1,0:T(8,128)} %bitcast.49, s32[64,1]{1,0:T(8,128)} %copy.13.owners, s32[1,64]{1,0:T(1,128)} %bitcast.51), custom_call_target="tpu_custom_call" | custom-call | tf_op jit(solution)/shard_map/request_kernel/pallas_call | solution.py:459
  6.2 11.9 %all-to-all-start = ((f32[64,16,128]{2,1,0:T(8,128)}), f32[64,16,128]{2,1,0:T(8,128)S(1)}, u32[]{:S(2)}, u32[]{:S(2)}) async-start(f32[64,16,128]{2,1,0:T(8,128)} %bitcast.37), calls=%async_computation | async-start | bytes 1048576 | tf_op jit(solution)/shard_map/all_to_all | solution.py:487
  18.1 1.5 %slabs_kernel.1 = (f32[5,4,8,128]{3,2,1,0:T(8,128)}, f32[5,8,128]{2,1,0:T(8,128)}, f32[5,8,128]{2,1,0:T(8,128)}) custom-call(f32[3,4,8,128]{3,2,1,0:T(8,128)} %disp.1, f32[4,8,128]{2,1,0:T(8,128)} %lame.1, f32[4,8,128]{2,1,0:T(8,128)} %shear.1), custom_call_target="tpu_custom_call" | custom-call | tf_op jit(solution)/shard_map/slabs_kernel/pallas_call | solution.py:459
  19.6 2.9 %collective-permute-start = (f32[5,8,128]{2,1,0:T(8,128)}, f32[5,8,128]{2,1,0:T(8,128)S(1)}, u32[]{:S(2)}, u32[]{:S(2)}) collective-permute-start(f32[5,8,128]{2,1,0:T(8,128)} %get-tuple-element.32), channel_id=1, source_target_pairs={{0,8},{8,16},{16,24},{24,32},{32,40},{40,48},{48,56},{56,64},{64,7... | collective-permute-start | bytes 61448 | tf_op jit(solution)/shard_map/ppermute | solution.py:469
  22.5 1.3 %collective-permute-start.1 = (f32[5,8,128]{2,1,0:T(8,128)}, f32[5,8,128]{2,1,0:T(8,128)S(1)}, u32[]{:S(2)}, u32[]{:S(2)}) collective-permute-start(f32[5,8,128]{2,1,0:T(8,128)} %get-tuple-element.33), channel_id=1, source_target_pairs={{8,0},{16,8},{24,16},{32,24},{40,32},{48,40},{56,48},{64,56},{72,6... | collective-permute-start | bytes 61448 | tf_op jit(solution)/shard_map/ppermute | solution.py:470
  23.8 3.7 %collective-permute-done.1.x_high = f32[5,8,128]{2,1,0:T(8,128)S(1)} collective-permute-done((f32[5,8,128]{2,1,0:T(8,128)}, f32[5,8,128]{2,1,0:T(8,128)S(1)}, u32[]{:S(2)}, u32[]{:S(2)}) %collective-permute-start.1) | collective-permute-done | bytes 20512 | tf_op jit(solution)/shard_map/ppermute | solution.py:470
  28.1 1.5 %rim_kernel.2 = (f32[5,8,128]{2,1,0:T(8,128)}, f32[5,8,128]{2,1,0:T(8,128)}) custom-call(f32[5,4,8,128]{3,2,1,0:T(8,128)} %get-tuple-element.31.block, f32[5,8,128]{2,1,0:T(8,128)} %copy-done.5, f32[5,8,128]{2,1,0:T(8,128)} %copy-done.6), custom_call_target="tpu_custom_call" | custom-call | tf_op jit(solution)/shard_map/rim_kernel/pallas_call | solution.py:459
  29.7 3.1 %collective-permute-start.2 = (f32[5,8,128]{2,1,0:T(8,128)}, f32[5,8,128]{2,1,0:T(8,128)S(1)}, u32[]{:S(2)}, u32[]{:S(2)}) collective-permute-start(f32[5,8,128]{2,1,0:T(8,128)} %get-tuple-element.34), channel_id=1, source_target_pairs={{0,2},{2,4},{4,6},{1,3},{3,5},{5,7},{8,10},{10,12},{12,14},{9,11},... | collective-permute-start | bytes 61448 | tf_op jit(solution)/shard_map/ppermute | solution.py:469
  32.8 1.3 %collective-permute-start.3 = (f32[5,8,128]{2,1,0:T(8,128)}, f32[5,8,128]{2,1,0:T(8,128)S(1)}, u32[]{:S(2)}, u32[]{:S(2)}) collective-permute-start(f32[5,8,128]{2,1,0:T(8,128)} %get-tuple-element.35), channel_id=1, source_target_pairs={{2,0},{4,2},{6,4},{3,1},{5,3},{7,5},{10,8},{12,10},{14,12},{11,9},... | collective-permute-start | bytes 61448 | tf_op jit(solution)/shard_map/ppermute | solution.py:470
  34.1 2.5 %table_kernel.1.table = bf16[128,512]{1,0:T(8,128)(2,1)} custom-call(f32[3,32,128]{2,1,0:T(8,128)} %bitcast.29, s32[32,128]{1,0:T(8,128)} %bitcast.42), custom_call_target="tpu_custom_call" | custom-call | tf_op jit(solution)/shard_map/table_kernel/pallas_call | solution.py:459
  37.4 2.3 %reply_kernel.1 = (f32[512,128]{1,0:T(8,128)}, s32[128,128]{1,0:T(8,128)}, s32[128,128]{1,0:T(8,128)}) custom-call(f32[1024,128]{1,0:T(8,128)} %bitcast.20, bf16[128,512]{1,0:T(8,128)(2,1)} %table_kernel.1.table, s32[32,128]{1,0:T(8,128)} %bitcast.43), custom_call_target="tpu_custom_call" | custom-call | tf_op jit(solution)/shard_map/reply_kernel/pallas_call | solution.py:459
  39.7 12.1 %all-to-all-start.1 = ((f32[64,8,128]{2,1,0:T(8,128)}), f32[64,8,128]{2,1,0:T(8,128)S(1)}, u32[]{:S(2)}, u32[]{:S(2)}) async-start(f32[64,8,128]{2,1,0:T(8,128)} %bitcast.27), calls=%async_computation.1 | async-start | bytes 524288 | tf_op jit(solution)/shard_map/all_to_all | solution.py:487
  53.0 1.6 %extend_kernel.2.near = f32[5,6,16,128]{3,2,1,0:T(8,128)} custom-call(f32[5,4,8,128]{3,2,1,0:T(8,128)} %get-tuple-element.31.block, f32[5,8,128]{2,1,0:T(8,128)} %copy-done.5, f32[5,8,128]{2,1,0:T(8,128)} %copy-done.6, f32[5,8,128]{2,1,0:T(8,128)} %copy-done.9, f32[5,8,128]{2,1,0:T(8,128)} %copy-done.10), custom_call_target="tpu_custom_call" | custom-call | tf_op jit(solution)/shard_map/extend_kernel/pallas_call | solution.py:459
  54.7 3.5 %collective-permute-start.4 = (f32[5,6,16,128]{3,2,1,0:T(8,128)}, f32[5,6,16,128]{3,2,1,0:T(8,128)S(1)}, u32[]{:S(2)}, u32[]{:S(2)}) collective-permute-start(f32[5,6,16,128]{3,2,1,0:T(8,128)} %extend_kernel.2.near), channel_id=1, source_target_pairs={{0,1},{1,0},{2,3},{3,2},{4,5},{5,4},{6,7},{7,6},{8,9},{9,8},{10,11... | collective-permute-start | bytes 737288 | tf_op jit(solution)/shard_map/ppermute | solution.py:482
  58.2 1.3 %collective-permute-done.4.other = f32[5,6,16,128]{3,2,1,0:T(8,128)S(1)} collective-permute-done((f32[5,6,16,128]{3,2,1,0:T(8,128)}, f32[5,6,16,128]{3,2,1,0:T(8,128)S(1)}, u32[]{:S(2)}, u32[]{:S(2)}) %collective-permute-start.4) | collective-permute-done | bytes 245792 | tf_op jit(solution)/shard_map/ppermute | solution.py:482
  60.2 2.1 %internal_first_kernel.1 = (f32[3,4,8,128]{3,2,1,0:T(8,128)}, f32[2,5,16,128]{3,2,1,0:T(8,128)}) custom-call(f32[5,6,16,128]{3,2,1,0:T(8,128)} %extend_kernel.2.near, f32[5,6,16,128]{3,2,1,0:T(8,128)} %copy-done.3), custom_call_target="tpu_custom_call" | custom-call | tf_op jit(solution)/shard_map/internal_first_kernel/pallas_call | solution.py:459
  62.3 6.2 %reaction_kernel.1.reaction = f32[3,32,128]{2,1,0:T(8,128)} custom-call(f32[1024,128]{1,0:T(8,128)} %bitcast.21, f32[512,128]{1,0:T(8,128)} %get-tuple-element.26.frames, s32[128,128]{1,0:T(8,128)} %get-tuple-element.29.face_row, s32[128,128]{1,0:T(8,128)} %get-tuple-element.30.face_lane), custom_call_target="tpu_custom_call" | custom-call | tf_op jit(solution)/shard_map/reaction_kernel/pallas_call | solution.py:459
  69.2 4.2 %middle_kernel.1 = (f32[3,32,128]{2,1,0:T(8,128)}, f32[3,32,128]{2,1,0:T(8,128)}, f32[3,8,128]{2,1,0:T(8,128)}, f32[3,8,128]{2,1,0:T(8,128)}) custom-call(f32[512,128]{1,0:T(8,128)} %bitcast.26, f32[64,128]{1,0:T(8,128)} %get-tuple-element.27.slot_of, f32[3,64,128]{2,1,0:T(8,128)} %get-tuple-element.28.at_slaves, f32[64,128]{1,0:T(8,128)} %bitcast.39, ...), custom_call_target="tpu_custom_call" | custom-call | tf_op jit(solution)/shard_map/middle_kernel/pallas_call | solution.py:459
  73.4 5.5 %second_kernel.1 = (f32[1024,128]{1,0:T(8,128)}, f32[3,64,128]{2,1,0:T(8,128)}) custom-call(f32[3,32,128]{2,1,0:T(8,128)} %get-tuple-element.37.u.disp, s32[64,128]{1,0:T(8,128)} %bitcast.35, s32[32,128]{1,0:T(8,128)} %bitcast.44, f32[64,128]{1,0:T(8,128)} %get-tuple-element.27.slot_of, f32[1024,128]{1,0:T(8,128)} %bitcast.22), custom_call_target="tpu_custom_call" | custom-call | tf_op jit(solution)/shard_map/second_kernel/pallas_call | solution.py:459
  78.8 10.2 %all-to-all-start.2 = ((f32[64,16,128]{2,1,0:T(8,128)}), f32[64,16,128]{2,1,0:T(8,128)S(1)}, u32[]{:S(2)}, u32[]{:S(2)}) async-start(f32[64,16,128]{2,1,0:T(8,128)} %bitcast.24), calls=%async_computation.2 | async-start | bytes 1048576 | tf_op jit(solution)/shard_map/all_to_all | solution.py:487
  89.0 2.9 %collective-permute-start.5 = (f32[3,8,128]{2,1,0:T(8,128)S(1)}, f32[3,8,128]{2,1,0:T(8,128)S(1)}, u32[]{:S(2)}, u32[]{:S(2)}) collective-permute-start(f32[3,8,128]{2,1,0:T(8,128)S(1)} %copy-done.15), channel_id=1, source_target_pairs={{0,8},{8,16},{16,24},{24,32},{32,40},{40,48},{48,56},{56,64},{64,7... | collective-permute-start | bytes 36872 | tf_op jit(solution)/shard_map/ppermute | solution.py:469
  92.0 1.3 %collective-permute-start.6 = (f32[3,8,128]{2,1,0:T(8,128)S(1)}, f32[3,8,128]{2,1,0:T(8,128)S(1)}, u32[]{:S(2)}, u32[]{:S(2)}) collective-permute-start(f32[3,8,128]{2,1,0:T(8,128)S(1)} %copy-done.14), channel_id=1, source_target_pairs={{8,0},{16,8},{24,16},{32,24},{40,32},{48,40},{56,48},{64,56},{72,6... | collective-permute-start | bytes 36872 | tf_op jit(solution)/shard_map/ppermute | solution.py:470
  94.3 2.5 %collective-permute-done.6.x_high = f32[3,8,128]{2,1,0:T(8,128)S(1)} collective-permute-done((f32[3,8,128]{2,1,0:T(8,128)S(1)}, f32[3,8,128]{2,1,0:T(8,128)S(1)}, u32[]{:S(2)}, u32[]{:S(2)}) %collective-permute-start.6) | collective-permute-done | bytes 12320 | tf_op jit(solution)/shard_map/ppermute | solution.py:470
  97.4 1.4 %rim_kernel.3 = (f32[3,8,128]{2,1,0:T(8,128)}, f32[3,8,128]{2,1,0:T(8,128)}) custom-call(f32[3,4,8,128]{3,2,1,0:T(8,128)} %bitcast.31, f32[3,8,128]{2,1,0:T(8,128)} %copy-done.7, f32[3,8,128]{2,1,0:T(8,128)} %copy-done.8), custom_call_target="tpu_custom_call" | custom-call | tf_op jit(solution)/shard_map/rim_kernel/pallas_call | solution.py:459
  98.9 3.1 %collective-permute-start.7 = (f32[3,8,128]{2,1,0:T(8,128)}, f32[3,8,128]{2,1,0:T(8,128)S(1)}, u32[]{:S(2)}, u32[]{:S(2)}) collective-permute-start(f32[3,8,128]{2,1,0:T(8,128)} %get-tuple-element.42), channel_id=1, source_target_pairs={{0,2},{2,4},{4,6},{1,3},{3,5},{5,7},{8,10},{10,12},{12,14},{9,11},... | collective-permute-start | bytes 36872 | tf_op jit(solution)/shard_map/ppermute | solution.py:469
  102.0 1.3 %collective-permute-start.8 = (f32[3,8,128]{2,1,0:T(8,128)}, f32[3,8,128]{2,1,0:T(8,128)S(1)}, u32[]{:S(2)}, u32[]{:S(2)}) collective-permute-start(f32[3,8,128]{2,1,0:T(8,128)} %get-tuple-element.43), channel_id=1, source_target_pairs={{2,0},{4,2},{6,4},{3,1},{5,3},{7,5},{10,8},{12,10},{14,12},{11,9},... | collective-permute-start | bytes 36872 | tf_op jit(solution)/shard_map/ppermute | solution.py:470
  103.3 3.3 %collective-permute-done.8.y_high = f32[3,8,128]{2,1,0:T(8,128)S(1)} collective-permute-done((f32[3,8,128]{2,1,0:T(8,128)}, f32[3,8,128]{2,1,0:T(8,128)S(1)}, u32[]{:S(2)}, u32[]{:S(2)}) %collective-permute-start.8) | collective-permute-done | bytes 12320 | tf_op jit(solution)/shard_map/ppermute | solution.py:470
  107.2 1.5 %extend_kernel.3.near = f32[3,6,16,128]{3,2,1,0:T(8,128)} custom-call(f32[3,4,8,128]{3,2,1,0:T(8,128)} %bitcast.32, f32[3,8,128]{2,1,0:T(8,128)} %copy-done.7, f32[3,8,128]{2,1,0:T(8,128)} %copy-done.8, f32[3,8,128]{2,1,0:T(8,128)} %copy-done.11, f32[3,8,128]{2,1,0:T(8,128)} %copy-done.12), custom_call_target="tpu_custom_call" | custom-call | tf_op jit(solution)/shard_map/extend_kernel/pallas_call | solution.py:459
  108.7 3.4 %collective-permute-start.9 = (f32[3,6,16,128]{3,2,1,0:T(8,128)}, f32[3,6,16,128]{3,2,1,0:T(8,128)S(1)}, u32[]{:S(2)}, u32[]{:S(2)}) collective-permute-start(f32[3,6,16,128]{3,2,1,0:T(8,128)} %extend_kernel.3.near), channel_id=1, source_target_pairs={{0,1},{1,0},{2,3},{3,2},{4,5},{5,4},{6,7},{7,6},{8,9},{9,8},{10,11... | collective-permute-start | bytes 442376 | tf_op jit(solution)/shard_map/ppermute | solution.py:482
  112.1 1.2 collective-permute-done.9.other
  114.0 2.0 %internal_kernel.1 = f32[3,4,8,128]{3,2,1,0:T(8,128)} custom-call(f32[3,6,16,128]{3,2,1,0:T(8,128)} %extend_kernel.3.near, f32[3,6,16,128]{3,2,1,0:T(8,128)} %copy-done.4, f32[2,5,16,128]{3,2,1,0:T(8,128)} %get-tuple-element.44.moduli), custom_call_target="tpu_custom_call" | custom-call | tf_op jit(solution)/shard_map/internal_kernel/pallas_call | solution.py:459
  116.8 9.1 %last_kernel.1 = (f32[3,32,128]{2,1,0:T(8,128)}, f32[3,32,128]{2,1,0:T(8,128)}) custom-call(f32[1024,128]{1,0:T(8,128)} %bitcast.25, f32[1024,128]{1,0:T(8,128)} %get-tuple-element.38.sent, f32[1024,128]{1,0:T(8,128)} %bitcast.23, s32[128,128]{1,0:T(8,128)} %get-tuple-element.29.face_row, s32[128,128]{1,0:T(8,128)} %get-tuple-element.30.face_lane, ...), custom_call_target="tpu_custom_call" | custom-call | tf_op jit(solution)/shard_map/last_kernel/pallas_call | solution.py:459
  (41 shorter events, 9.1 us)
Async XLA Ops:
  0.6 0.7 copy-start.13
  6.2 30.4 %all-to-all-start = ((f32[64,16,128]{2,1,0:T(8,128)}), f32[64,16,128]{2,1,0:T(8,128)S(1)}, u32[]{:S(2)}, u32[]{:S(2)}) async-start(f32[64,16,128]{2,1,0:T(8,128)} %bitcast.37), calls=%async_computation | async-start | bytes 1048576 | tf_op jit(solution)/shard_map/all_to_all | solution.py:487
  19.6 4.2 %collective-permute-start = (f32[5,8,128]{2,1,0:T(8,128)}, f32[5,8,128]{2,1,0:T(8,128)S(1)}, u32[]{:S(2)}, u32[]{:S(2)}) collective-permute-start(f32[5,8,128]{2,1,0:T(8,128)} %get-tuple-element.32), channel_id=1, source_target_pairs={{0,8},{8,16},{16,24},{24,32},{32,40},{40,48},{48,56},{56,64},{64,7... | collective-permute-start | bytes 61448 | tf_op jit(solution)/shard_map/ppermute | solution.py:469
  22.5 5.0 %collective-permute-start.1 = (f32[5,8,128]{2,1,0:T(8,128)}, f32[5,8,128]{2,1,0:T(8,128)S(1)}, u32[]{:S(2)}, u32[]{:S(2)}) collective-permute-start(f32[5,8,128]{2,1,0:T(8,128)} %get-tuple-element.33), channel_id=1, source_target_pairs={{8,0},{16,8},{24,16},{32,24},{40,32},{48,40},{56,48},{64,56},{72,6... | collective-permute-start | bytes 61448 | tf_op jit(solution)/shard_map/ppermute | solution.py:470
  23.8 3.7 %copy-start.5 = (f32[5,8,128]{2,1,0:T(8,128)}, f32[5,8,128]{2,1,0:T(8,128)S(1)}, u32[]{:S(2)}) copy-start(f32[5,8,128]{2,1,0:T(8,128)S(1)} %collective-permute-done.x_low) | copy-start | bytes 61444
  27.5 0.6 copy-start.6
  29.7 22.1 %collective-permute-start.2 = (f32[5,8,128]{2,1,0:T(8,128)}, f32[5,8,128]{2,1,0:T(8,128)S(1)}, u32[]{:S(2)}, u32[]{:S(2)}) collective-permute-start(f32[5,8,128]{2,1,0:T(8,128)} %get-tuple-element.34), channel_id=1, source_target_pairs={{0,2},{2,4},{4,6},{1,3},{3,5},{5,7},{8,10},{10,12},{12,14},{9,11},... | collective-permute-start | bytes 61448 | tf_op jit(solution)/shard_map/ppermute | solution.py:469
  32.8 19.0 %collective-permute-start.3 = (f32[5,8,128]{2,1,0:T(8,128)}, f32[5,8,128]{2,1,0:T(8,128)S(1)}, u32[]{:S(2)}, u32[]{:S(2)}) collective-permute-start(f32[5,8,128]{2,1,0:T(8,128)} %get-tuple-element.35), channel_id=1, source_target_pairs={{2,0},{4,2},{6,4},{3,1},{5,3},{7,5},{10,8},{12,10},{14,12},{11,9},... | collective-permute-start | bytes 61448 | tf_op jit(solution)/shard_map/ppermute | solution.py:470
  36.6 0.8 copy-start
  39.7 28.8 %all-to-all-start.1 = ((f32[64,8,128]{2,1,0:T(8,128)}), f32[64,8,128]{2,1,0:T(8,128)S(1)}, u32[]{:S(2)}, u32[]{:S(2)}) async-start(f32[64,8,128]{2,1,0:T(8,128)} %bitcast.27), calls=%async_computation.1 | async-start | bytes 524288 | tf_op jit(solution)/shard_map/all_to_all | solution.py:487
  51.8 0.6 copy-start.9
  52.4 0.6 copy-start.10
  54.7 4.9 %collective-permute-start.4 = (f32[5,6,16,128]{3,2,1,0:T(8,128)}, f32[5,6,16,128]{3,2,1,0:T(8,128)S(1)}, u32[]{:S(2)}, u32[]{:S(2)}) collective-permute-start(f32[5,6,16,128]{3,2,1,0:T(8,128)} %extend_kernel.2.near), channel_id=1, source_target_pairs={{0,1},{1,0},{2,3},{3,2},{4,5},{5,4},{6,7},{7,6},{8,9},{9,8},{10,11... | collective-permute-start | bytes 737288 | tf_op jit(solution)/shard_map/ppermute | solution.py:482
  59.5 0.7 copy-start.3
  68.5 0.7 copy-start.2
  78.8 10.2 %copy-start.15 = (f32[3,8,128]{2,1,0:T(8,128)S(1)}, f32[3,8,128]{2,1,0:T(8,128)}, u32[]{:S(2)}) copy-start(f32[3,8,128]{2,1,0:T(8,128)} %get-tuple-element.40) | copy-start | bytes 36868
  78.8 13.1 %copy-start.14 = (f32[3,8,128]{2,1,0:T(8,128)S(1)}, f32[3,8,128]{2,1,0:T(8,128)}, u32[]{:S(2)}) copy-start(f32[3,8,128]{2,1,0:T(8,128)} %get-tuple-element.41) | copy-start | bytes 36868
  78.8 37.1 %all-to-all-start.2 = ((f32[64,16,128]{2,1,0:T(8,128)}), f32[64,16,128]{2,1,0:T(8,128)S(1)}, u32[]{:S(2)}, u32[]{:S(2)}) async-start(f32[64,16,128]{2,1,0:T(8,128)} %bitcast.24), calls=%async_computation.2 | async-start | bytes 1048576 | tf_op jit(solution)/shard_map/all_to_all | solution.py:487
  89.0 5.3 %collective-permute-start.5 = (f32[3,8,128]{2,1,0:T(8,128)S(1)}, f32[3,8,128]{2,1,0:T(8,128)S(1)}, u32[]{:S(2)}, u32[]{:S(2)}) collective-permute-start(f32[3,8,128]{2,1,0:T(8,128)S(1)} %copy-done.15), channel_id=1, source_target_pairs={{0,8},{8,16},{16,24},{24,32},{32,40},{40,48},{48,56},{56,64},{64,7... | collective-permute-start | bytes 36872 | tf_op jit(solution)/shard_map/ppermute | solution.py:469
  92.0 4.9 %collective-permute-start.6 = (f32[3,8,128]{2,1,0:T(8,128)S(1)}, f32[3,8,128]{2,1,0:T(8,128)S(1)}, u32[]{:S(2)}, u32[]{:S(2)}) collective-permute-start(f32[3,8,128]{2,1,0:T(8,128)S(1)} %copy-done.14), channel_id=1, source_target_pairs={{8,0},{16,8},{24,16},{32,24},{40,32},{48,40},{56,48},{64,56},{72,6... | collective-permute-start | bytes 36872 | tf_op jit(solution)/shard_map/ppermute | solution.py:470
  94.3 2.5 %copy-start.7 = (f32[3,8,128]{2,1,0:T(8,128)}, f32[3,8,128]{2,1,0:T(8,128)S(1)}, u32[]{:S(2)}) copy-start(f32[3,8,128]{2,1,0:T(8,128)S(1)} %collective-permute-done.5.x_low) | copy-start | bytes 36868
  96.8 0.6 copy-start.8
  98.9 4.4 %collective-permute-start.7 = (f32[3,8,128]{2,1,0:T(8,128)}, f32[3,8,128]{2,1,0:T(8,128)S(1)}, u32[]{:S(2)}, u32[]{:S(2)}) collective-permute-start(f32[3,8,128]{2,1,0:T(8,128)} %get-tuple-element.42), channel_id=1, source_target_pairs={{0,2},{2,4},{4,6},{1,3},{3,5},{5,7},{8,10},{10,12},{12,14},{9,11},... | collective-permute-start | bytes 36872 | tf_op jit(solution)/shard_map/ppermute | solution.py:469
  102.0 4.6 %collective-permute-start.8 = (f32[3,8,128]{2,1,0:T(8,128)}, f32[3,8,128]{2,1,0:T(8,128)S(1)}, u32[]{:S(2)}, u32[]{:S(2)}) collective-permute-start(f32[3,8,128]{2,1,0:T(8,128)} %get-tuple-element.43), channel_id=1, source_target_pairs={{2,0},{4,2},{6,4},{3,1},{5,3},{7,5},{10,8},{12,10},{14,12},{11,9},... | collective-permute-start | bytes 36872 | tf_op jit(solution)/shard_map/ppermute | solution.py:470
  103.3 3.3 %copy-start.11 = (f32[3,8,128]{2,1,0:T(8,128)}, f32[3,8,128]{2,1,0:T(8,128)S(1)}, u32[]{:S(2)}) copy-start(f32[3,8,128]{2,1,0:T(8,128)S(1)} %collective-permute-done.7.y_low) | copy-start | bytes 36868
  106.6 0.6 copy-start.12
  108.7 4.6 %collective-permute-start.9 = (f32[3,6,16,128]{3,2,1,0:T(8,128)}, f32[3,6,16,128]{3,2,1,0:T(8,128)S(1)}, u32[]{:S(2)}, u32[]{:S(2)}) collective-permute-start(f32[3,6,16,128]{3,2,1,0:T(8,128)} %extend_kernel.3.near), channel_id=1, source_target_pairs={{0,1},{1,0},{2,3},{3,2},{4,5},{5,4},{6,7},{7,6},{8,9},{9,8},{10,11... | collective-permute-start | bytes 442376 | tf_op jit(solution)/shard_map/ppermute | solution.py:482
  113.3 0.7 copy-start.4
  116.0 0.8 copy-start.1

commit v2 on v1

--- a/solution.py
+++ b/solution.py
@@ -5,7 +5,7 @@
 from jax.experimental.pallas import tpu as pltpu
 from jax.sharding import PartitionSpec as P
 
-STEPS = 2
+
 PENALTY = 4.0
 HOURGLASS = 0.3
 TIME_STEP = 0.25
@@ -95,34 +95,43 @@
     return jnp.concatenate([high, mid, low, jnp.zeros_like(high)], axis=0)
 
 
+def packed_row(x, q):
+    return jnp.broadcast_to(x[q : q + 1, :], (16, PATCH)).astype(BF16)
+
+
 def scatter_nodes(count, row_lane, forces_ref):
-    acc = jnp.zeros((6 * ROWS, PATCH), F32)
-    row_at = iota((ROWS, PATCH), 0)
-    lane_at = iota((PATCH, PATCH), 0)
+    half = ROWS // 2
+    row_at = iota((half, PATCH), 0).astype(F32).astype(BF16)
+    lane_at = iota((2 * PATCH, PATCH), 0).astype(F32).astype(BF16)
+    none = jnp.zeros((half, PATCH), BF16)
 
     def body(i, acc):
-        start = pl.multiple_of(i * 8, 8)
+        start = pl.multiple_of(i * 32, 32)
         rows, lanes = row_lane(start)
-        parts = [forces_ref[c, pl.ds(start, 8), :] for c in range(6)]
+        lanes = (lanes + (rows >> 4) * PATCH).astype(F32)
+        rows = (rows & (half - 1)).astype(F32)
+        parts = [forces_ref[c, pl.ds(start, 32), :] for c in range(6)]
         left = []
         right = []
-        for q in range(8):
-            here = jnp.broadcast_to(rows[q : q + 1, :], (ROWS, PATCH)) == row_at
-            pieces = [
-                jnp.where(here, jnp.broadcast_to(part[q : q + 1, :], (ROWS, PATCH)), 0.0)
-                for part in parts
-            ]
-            left.append(jnp.concatenate(pieces, axis=0).astype(BF16))
-            chosen = jnp.broadcast_to(lanes[q : q + 1, :], (PATCH, PATCH)) == lane_at
-            right.append(jnp.where(chosen, 1.0, 0.0).astype(BF16))
+        for q in range(32):
+            here = packed_row(rows, q) == row_at
+            pieces = [jnp.where(here, packed_row(part, q), none) for part in parts]
+            left.append(jnp.concatenate(pieces, axis=0))
+            chosen = jnp.concatenate([packed_row(lanes, q)] * 16, axis=0) == lane_at
+            right.append(jnp.where(chosen, jnp.ones_like(lane_at), jnp.zeros_like(lane_at)))
         left = jnp.concatenate(left, axis=1)
         right = jnp.concatenate(right, axis=1)
         return acc + lax.dot_general(
             left, right, (((1,), (1,)), ((), ())), preferred_element_type=F32
         )
 
-    acc = lax.fori_loop(0, count // 8, body, acc)
-    return [acc[c * ROWS : (c + 1) * ROWS] + acc[(c + 3) * ROWS : (c + 4) * ROWS] for c in range(3)]
+    acc = lax.fori_loop(0, count // 32, body, jnp.zeros((6 * half, 2 * PATCH), F32))
+    acc = acc[0 : 3 * half] + acc[3 * half : 6 * half]
+    out = []
+    for c in range(3):
+        part = acc[c * half : (c + 1) * half]
+        out.append(jnp.concatenate([part[:, 0:PATCH], part[:, PATCH:]], axis=0))
+    return out
 
 
 def store_parts(forces_ref, c, start, force):
@@ -287,8 +296,8 @@
 
 
 def request_kernel(u, slaves, gaps, chosen, owners, wanted, send, slot_of, at_slaves):
-    owner = owners[...].astype(F32)
-    owner_row = column_to_row(owner)
+    owner_row = owners[...].astype(F32)
+    owner = row_to_column(owner_row)
     same = (owner == owner_row) & (iota((PAIRS, PAIRS), 1) < iota((PAIRS, PAIRS), 0))
     rank = jnp.max(jnp.where(same, 1.0, 0.0), axis=1, keepdims=True)
     slot = rank * GROUPS + owner
@@ -306,18 +315,16 @@
     for t in range(CAP):
         part = slice(t * GROUPS, (t + 1) * GROUPS)
         for c in range(4):
-            send[pl.ds(t * 4 + c, GROUPS, stride=16), :] = moved[part, c * 128 : (c + 1) * 128]
+            send[pl.ds(t * 4 + c, GROUPS, stride=12), :] = moved[part, c * 128 : (c + 1) * 128]
         for c in range(2):
-            send[pl.ds(8 + t * 2 + c, GROUPS, stride=16), :] = moved_whole[
+            send[pl.ds(8 + t * 2 + c, GROUPS, stride=12), :] = moved_whole[
                 part, c * 128 : (c + 1) * 128
             ]
-    for c in range(12, 16):
-        send[pl.ds(c, GROUPS, stride=16), :] = jnp.zeros((GROUPS, PATCH), F32)
 
 
 def wanted_rows(arrived):
-    patch = jnp.concatenate([every(arrived, 9, 16), every(arrived, 11, 16)], axis=0)
-    cand = jnp.concatenate([every(arrived, 8, 16), every(arrived, 10, 16)], axis=0)
+    patch = jnp.concatenate([every(arrived, 9, 12), every(arrived, 11, 12)], axis=0)
+    cand = jnp.concatenate([every(arrived, 8, 12), every(arrived, 10, 12)], axis=0)
     at = (iota((SLOTS, PATCH), 1) % PATCHES + 1).astype(F32)
     onehot = jnp.where(patch == at, 1.0, 0.0).astype(BF16)
     return onehot, cand.astype(I32)
@@ -346,7 +353,7 @@
 def owner_forces(values, gap_source, frames, stride, offset, frame_stride, frame_offset, scratch):
     for t in range(CAP):
         u = [every(values, t * offset + c, stride) for c in range(3)]
-        gap = every(gap_source, t * 4 + 3, 16)
+        gap = every(gap_source, t * 4 + 3, 12)
         frame = [every(frames, t * frame_offset[1] + frame_offset[0] + c, frame_stride) for c in range(4)]
         force = pair_force(u, frame[0:3], frame[3], gap)
         for c in range(3):
@@ -355,7 +362,7 @@
 
 def face_contact(face_row, face_lane, scratch):
     def row_lane(start):
-        return face_row[pl.ds(start, 8), :], face_lane[pl.ds(start, 8), :]
+        return face_row[pl.ds(start, 32), :], face_lane[pl.ds(start, 32), :]
 
     faces = scatter_nodes(SLOTS, row_lane, scratch)
     return [x + down_rows(x, 8) + down_rows(x, 9) + down_rows(x, 1) for x in faces]
@@ -377,14 +384,14 @@
         store_parts(scratch, c, 0, force[c])
 
     def row_lane(start):
-        nodes = slaves[pl.ds(start, 8), :]
+        nodes = slaves[pl.ds(start, 32), :]
         return nodes >> 7, nodes & 127
 
     return scatter_nodes(PAIRS, row_lane, scratch)
 
 
 def reaction_kernel(arrived, frames, face_row, face_lane, out, scratch):
-    owner_forces(arrived, arrived, frames, 16, 4, 8, (0, 4), scratch)
+    owner_forces(arrived, arrived, frames, 12, 4, 8, (0, 4), scratch)
     for c, force in enumerate(face_contact(face_row, face_lane, scratch)):
         out[c] = force
 
@@ -425,12 +432,11 @@
     for t in range(CAP):
         part = slice(t * GROUPS, (t + 1) * GROUPS)
         for c in range(3):
-            send[pl.ds(t * 8 + c, GROUPS, stride=16), :] = moved[part, c * 128 : (c + 1) * 128]
-        send[pl.ds(t * 8 + 7, GROUPS, stride=16), :] = jnp.zeros((GROUPS, PATCH), F32)
+            send[pl.ds(t * 7 + c, GROUPS, stride=14), :] = moved[part, c * 128 : (c + 1) * 128]
     for c in range(4):
         picked = lane_pick(tiles[:, c * 128 : (c + 1) * 128], cand)
         for t in range(CAP):
-            send[pl.ds(t * 8 + 3 + c, GROUPS, stride=16), :] = picked[
+            send[pl.ds(t * 7 + 3 + c, GROUPS, stride=14), :] = picked[
                 t * GROUPS : (t + 1) * GROUPS
             ]
 
@@ -439,35 +445,48 @@
     arrived, sent, first, face_row, face_lane, slot_of, at_slaves, gaps, slaves, internal,
     disp, vel, mass, new_disp, new_vel, scratch, slave_scratch,
 ):
-    owner_forces(arrived, first, sent, 16, 8, 16, (3, 8), scratch)
+    owner_forces(arrived, first, sent, 14, 7, 14, (3, 7), scratch)
     reaction = face_contact(face_row, face_lane, scratch)
-    contact = slave_contact(arrived, 16, (3, 8), slot_of, at_slaves, gaps, slaves, slave_scratch)
+    contact = slave_contact(arrived, 14, (3, 7), slot_of, at_slaves, gaps, slaves, slave_scratch)
     for c in range(3):
         force = internal[c] + (contact[c] + reaction[c])
         advance(c, force, disp, vel, mass, new_disp, new_vel)
 
 
 def f32(*shape):
+    return pltpu.VMEM(shape, F32)
+
+
+def i32(*shape):
+    return pltpu.VMEM(shape, I32)
+
+
+def plain(*shape):
     return jax.ShapeDtypeStruct(shape, F32)
 
 
-def i32(*shape):
-    return jax.ShapeDtypeStruct(shape, I32)
-
-
-def call(kernel, outs, *args, scratch=()):
+def call(kernel, outs, *args, scratch=(), raw=0):
+    local = pl.BlockSpec(memory_space=pltpu.VMEM)
+    whole = pl.BlockSpec()
+    inputs = [
+        x if i < raw else pltpu.with_memory_space_constraint(x, pltpu.VMEM)
+        for i, x in enumerate(args)
+    ]
     return pl.pallas_call(
         kernel,
         out_shape=outs,
+        in_specs=[whole if i < raw else local for i in range(len(args))],
+        out_specs=jax.tree.map(
+            lambda x: whole if isinstance(x, jax.ShapeDtypeStruct) else local, outs
+        ),
         scratch_shapes=[pltpu.VMEM(s, F32) for s in scratch],
-        name=kernel.__name__,
-    )(*args)
+    )(*inputs)
 
 
 def shift_pair(low, high, axis):
     count = lax.axis_size(axis)
-    from_low = lax.ppermute(high, axis, [(i, i + 1) for i in range(count - 1)])
-    from_high = lax.ppermute(low, axis, [(i + 1, i) for i in range(count - 1)])
+    from_low = lax.ppermute(high, axis, [(i, (i + 1) % count) for i in range(count)])
+    from_high = lax.ppermute(low, axis, [((i + 1) % count, i) for i in range(count)])
     return from_low, from_high
 
 
@@ -479,23 +498,24 @@
     near = call(
         extend_kernel, f32(parts, NI + 2, 16, NK), block, x_low, x_high, y_low, y_high
     )
-    return near, lax.ppermute(near, "lay", [(0, 1), (1, 0)])
+    other = lax.ppermute(near, "lay", [(0, 1), (1, 0)])
+    return near, other
 
 
 def exchange(buffer):
-    chunk = buffer.reshape(GROUPS, -1, PATCH)
+    chunk = buffer.reshape(GROUPS, 1, -1)
     out = lax.all_to_all(chunk, ("len", "wid"), split_axis=0, concat_axis=0, tiled=True)
     return out.reshape(buffer.shape)
 
 
-def per_device(
+def program(
     displacement, velocity, lame_first, shear_modulus, nodal_mass, slave_nodes, initial_gap,
     candidate, pair_owner, pair_patch, master_faces,
 ):
     slaves = slave_nodes.reshape(PAIRS, PATCH)
     gaps = initial_gap.reshape(PAIRS, PATCH)
     chosen = candidate.reshape(PAIRS, PATCH)
-    owners = pair_owner.reshape(PAIRS, 1)
+    owners = pair_owner.reshape(1, PAIRS)
     wanted = pair_patch.reshape(1, PAIRS)
     faces = master_faces.reshape(PATCHES, PATCH)
     u = displacement.reshape(3, ROWS, NK)
@@ -504,19 +524,19 @@
     five, low, high = call(
         slabs_kernel,
         (f32(5, NI, NJ, NK), f32(5, NJ, NK), f32(5, NJ, NK)),
-        displacement, lame_first, shear_modulus,
+        displacement, lame_first, shear_modulus, raw=3,
     )
     near, other = extended(five, low, high)
     send, slot_of, at_slaves = call(
         request_kernel,
-        (f32(GROUPS * 16, PATCH), f32(PAIRS, SLOTS), f32(3, PAIRS, PATCH)),
-        u, slaves, gaps, chosen, owners, wanted,
+        (plain(GROUPS * 12, PATCH), f32(PAIRS, SLOTS), f32(3, PAIRS, PATCH)),
+        u, slaves, gaps, chosen, owners, wanted, raw=6,
     )
     first = exchange(send)
-    table = call(table_kernel, jax.ShapeDtypeStruct((128, 512), BF16), u, faces)
+    table = call(table_kernel, pltpu.VMEM((128, 512), BF16), u, faces)
     reply, face_row, face_lane = call(
         reply_kernel,
-        (f32(GROUPS * 8, PATCH), i32(SLOTS, PATCH), i32(SLOTS, PATCH)),
+        (plain(GROUPS * 8, PATCH), i32(SLOTS, PATCH), i32(SLOTS, PATCH)),
         first, table, faces,
     )
     arrived = exchange(reply)
@@ -537,14 +557,14 @@
     near, other = extended(u.reshape(3, NI, NJ, NK), low, high)
     sent, at_slaves = call(
         second_kernel,
-        (f32(GROUPS * 16, PATCH), f32(3, PAIRS, PATCH)),
+        (plain(GROUPS * 14, PATCH), f32(3, PAIRS, PATCH)),
         u, slaves, faces, slot_of, first,
     )
     arrived = exchange(sent)
     internal = call(internal_kernel, f32(3, NI, NJ, NK), near, other, moduli)
     u, v = call(
         last_kernel,
-        (f32(3, ROWS, NK), f32(3, ROWS, NK)),
+        (plain(3, ROWS, NK), plain(3, ROWS, NK)),
         arrived, sent, first, face_row, face_lane, slot_of, at_slaves, gaps, slaves,
         internal.reshape(3, ROWS, NK), u, v, mass,
         scratch=[(6, SLOTS, PATCH), (6, PAIRS, PATCH)],
@@ -565,5 +585,5 @@
         P("len", "wid", "lay", None, None),
     )
     return jax.shard_map(
-        per_device, mesh=mesh, in_specs=in_specs, out_specs=(vector, vector), check_vma=False
-    )
+        program, mesh=mesh, in_specs=in_specs, out_specs=(vector, vector), check_vma=False
+    )

time: 128 us -> 85.4 us (0.67); the launches traced: 126 us -> 85 us
  Pallas kernels: 45.5 us -> 23 us
  starting transfers between devices: 58.3 us -> 48.7 us
  local copies, waits for them, and re-layouts: 8.02 us -> 0.04 us
    pallas_call x14, Pallas kernels: 45.5 us -> 23 us  [call(): pl.pallas_call(kernel, out_shape=outs, in_specs=[whole if i < raw else lo...]
    unnamed x32 -> x16, local copies, waits for them, and re-layouts: 7.31 us -> 0.04 us
    all_to_all x3, starting transfers between devices: 34.3 us -> 27.1 us  [exchange(): lax.all_to_all(chunk, ('len', 'wid'), split_axis=0, concat_axis=0, tiled=...]
    ppermute x10, starting transfers between devices: 24 us -> 21.6 us  [the longest x4 10.3 us: shift_pair(): lax.ppermute(low, axis, [((i + 1) % count, i) for i in range(count)])]
    ppermute x10, waiting for transfers between devices: 13.2 us -> 11 us  [the longest x4 8.8 us: shift_pair(): lax.ppermute(high, axis, [(i, (i + 1) % count) for i in range(count)])]
    all_to_all x3, waiting for transfers between devices: 0.01 us -> 1.49 us  [exchange(): lax.all_to_all(chunk, ('len', 'wid'), split_axis=0, concat_axis=0, tiled=...]
  transfers between devices with their start and end apart: 13 -> 13, of which waited for: 6 -> 7; matrix products, arithmetic and copies ran while one was open for 0% -> 0% of each run, Pallas kernels for 18% -> 8%
where the time goes in v2:
time: 85.4 us; the launch traced here: 85 us
  starting transfers between devices  48.7 us (57%)
  Pallas kernels  23 us (27%)
  waiting for transfers between devices  12.5 us (15%)
    all_to_all x3, starting transfers between devices, exchange(): lax.all_to_all(chunk, ('len', 'wid'), split_axis=0, concat_axis=0, tiled=...  27.1 us
    pallas_call x14, Pallas kernels, call(): pl.pallas_call(kernel, out_shape=outs, in_specs=[whole if i < raw else lo...  23 us
    ppermute x4, starting transfers between devices, shift_pair(): lax.ppermute(low, axis, [((i + 1) % count, i) for i in range(count)])  10.3 us
    ppermute x4, waiting for transfers between devices, shift_pair(): lax.ppermute(high, axis, [(i, (i + 1) % count) for i in range(count)])  8.8 us
    ppermute x2, starting transfers between devices, extended(): other = lax.ppermute(near, 'lay', [(0, 1), (1, 0)])  6.36 us
    ppermute x4, starting transfers between devices, shift_pair(): lax.ppermute(high, axis, [(i, (i + 1) % count) for i in range(count)])  4.92 us
    ppermute x2, waiting for transfers between devices, extended(): other = lax.ppermute(near, 'lay', [(0, 1), (1, 0)])  2.15 us
  transfers between devices with their start and end apart: 13, of which 7 were waited for; matrix products, arithmetic and copies ran while one was open for 0% of the time, Pallas kernels for 8%

profile of v2, /device:TPU:1, one launch (start us, length us, event | category | flops | bytes accessed | tf_op | source)
XLA Modules:
  0.0 85.0 jit_solution(8510013836128384882)
XLA Ops:
  0.6 4.1 %shard_map.122 = (f32[768,128]{1,0:T(8,128)}, f32[64,128]{1,0:T(8,128)S(1)}, f32[3,64,128]{2,1,0:T(8,128)S(1)}) custom-call(f32[3,32,128]{2,1,0:T(8,128)} %bitcast.30, s32[64,128]{1,0:T(8,128)} %bitcast.33, f32[64,128]{1,0:T(8,128)} %bitcast.37, s32[64,128]{1,0:T(8,128)} %bitcast.49, s32[1,64]{1,0:T(1,128)} %bitcast.50, s32[1,64]{1,0:T(1,128)} %bitcast.51), custom_call_target="tpu_custom_call" | custom-call | tf_op jit(solution)/shard_map/pallas_call | solution.py:475
  4.8 12.0 %all-to-all-start = ((f32[64,1,1536]{2,1,0:T(1,128)}), f32[64,1,1536]{2,1,0:T(1,128)S(1)}, u32[]{:S(2)}, u32[]{:S(2)}) async-start(f32[64,1,1536]{2,1,0:T(1,128)} %bitcast.48), calls=%async_computation | async-start | bytes 786432 | tf_op jit(solution)/shard_map/all_to_all | solution.py:507
  16.7 0.8 shard_map.126
  17.6 1.1 %collective-permute-start = (f32[5,8,128]{2,1,0:T(8,128)S(1)}, f32[5,8,128]{2,1,0:T(8,128)S(1)}, u32[]{:S(2)}, u32[]{:S(2)}) collective-permute-start(f32[5,8,128]{2,1,0:T(8,128)S(1)} %get-tuple-element.32), channel_id=1, source_target_pairs={{0,8},{8,16},{16,24},{24,32},{32,40},{40,48},{48,56},{56,64},{64,7... | collective-permute-start | bytes 61448 | tf_op jit(solution)/shard_map/ppermute | solution.py:488
  18.6 3.8 %collective-permute-start.1 = (f32[5,8,128]{2,1,0:T(8,128)S(1)}, f32[5,8,128]{2,1,0:T(8,128)S(1)}, u32[]{:S(2)}, u32[]{:S(2)}) collective-permute-start(f32[5,8,128]{2,1,0:T(8,128)S(1)} %get-tuple-element.33), channel_id=1, source_target_pairs={{8,0},{16,8},{24,16},{32,24},{40,32},{48,40},{56,48},{64,56},{72,6... | collective-permute-start | bytes 61448 | tf_op jit(solution)/shard_map/ppermute | solution.py:489
  22.4 3.1 %collective-permute-done.x_low = f32[5,8,128]{2,1,0:T(8,128)S(1)} collective-permute-done((f32[5,8,128]{2,1,0:T(8,128)S(1)}, f32[5,8,128]{2,1,0:T(8,128)S(1)}, u32[]{:S(2)}, u32[]{:S(2)}) %collective-permute-start) | collective-permute-done | bytes 20512 | tf_op jit(solution)/shard_map/ppermute | solution.py:488
  25.6 1.4 %collective-permute-start.2 = (f32[5,8,128]{2,1,0:T(8,128)S(1)}, f32[5,8,128]{2,1,0:T(8,128)S(1)}, u32[]{:S(2)}, u32[]{:S(2)}) collective-permute-start(f32[5,8,128]{2,1,0:T(8,128)S(1)} %get-tuple-element.34), channel_id=1, source_target_pairs={{0,2},{2,4},{4,6},{6,0},{1,3},{3,5},{5,7},{7,1},{8,10},{10,12},{12... | collective-permute-start | bytes 61448 | tf_op jit(solution)/shard_map/ppermute | solution.py:488
  27.0 1.3 %collective-permute-start.3 = (f32[5,8,128]{2,1,0:T(8,128)S(1)}, f32[5,8,128]{2,1,0:T(8,128)S(1)}, u32[]{:S(2)}, u32[]{:S(2)}) collective-permute-start(f32[5,8,128]{2,1,0:T(8,128)S(1)} %get-tuple-element.35), channel_id=1, source_target_pairs={{2,0},{4,2},{6,4},{0,6},{3,1},{5,3},{7,5},{1,7},{10,8},{12,10},{14... | collective-permute-start | bytes 61448 | tf_op jit(solution)/shard_map/ppermute | solution.py:489
  28.3 1.0 %shard_map.123.table = bf16[128,512]{1,0:T(8,128)(2,1)S(1)} custom-call(f32[3,32,128]{2,1,0:T(8,128)S(1)} %bitcast.31, s32[32,128]{1,0:T(8,128)S(1)} %bitcast.41), custom_call_target="tpu_custom_call" | custom-call | tf_op jit(solution)/shard_map/pallas_call | solution.py:475
  29.4 1.1 %shard_map.124 = (f32[512,128]{1,0:T(8,128)}, s32[128,128]{1,0:T(8,128)S(1)}, s32[128,128]{1,0:T(8,128)S(1)}) custom-call(f32[768,128]{1,0:T(8,128)S(1)} %bitcast.20, bf16[128,512]{1,0:T(8,128)(2,1)S(1)} %shard_map.123.table, s32[32,128]{1,0:T(8,128)S(1)} %bitcast.42), custom_call_target="tpu_custom_call" | custom-call | tf_op jit(solution)/shard_map/pallas_call | solution.py:475
  30.5 6.5 %all-to-all-start.1 = ((f32[64,1,1024]{2,1,0:T(1,128)}), f32[64,1,1024]{2,1,0:T(1,128)S(1)}, u32[]{:S(2)}, u32[]{:S(2)}) async-start(f32[64,1,1024]{2,1,0:T(1,128)} %bitcast.26), calls=%async_computation.1 | async-start | bytes 524288 | tf_op jit(solution)/shard_map/all_to_all | solution.py:507
  37.1 3.2 %collective-permute-start.4 = (f32[5,6,16,128]{3,2,1,0:T(8,128)S(1)}, f32[5,6,16,128]{3,2,1,0:T(8,128)S(1)}, u32[]{:S(2)}, u32[]{:S(2)}) collective-permute-start(f32[5,6,16,128]{3,2,1,0:T(8,128)S(1)} %shard_map.128.near), channel_id=1, source_target_pairs={{0,1},{1,0},{2,3},{3,2},{4,5},{5,4},{6,7},{7,6},{8,9},{9,8},{10,11... | collective-permute-start | bytes 737288 | tf_op jit(solution)/shard_map/ppermute | solution.py:501
  40.3 1.1 %collective-permute-done.4.other = f32[5,6,16,128]{3,2,1,0:T(8,128)S(1)} collective-permute-done((f32[5,6,16,128]{3,2,1,0:T(8,128)S(1)}, f32[5,6,16,128]{3,2,1,0:T(8,128)S(1)}, u32[]{:S(2)}, u32[]{:S(2)}) %collective-permute-start.4) | collective-permute-done | bytes 245792 | tf_op jit(solution)/shard_map/ppermute | solution.py:501
  41.4 0.4 shard_map.129
  41.8 0.0 copy-start.6
  41.8 0.0 copy-start.7
  41.8 3.2 %shard_map.125.reaction = f32[3,32,128]{2,1,0:T(8,128)S(1)} custom-call(f32[768,128]{1,0:T(8,128)S(1)} %bitcast.21, f32[512,128]{1,0:T(8,128)S(1)} %copy-done.1, s32[128,128]{1,0:T(8,128)S(1)} %get-tuple-element.29.face_row, s32[128,128]{1,0:T(8,128)S(1)} %get-tuple-element.30.face_lane), custom_call_target="tpu_custom_call" | custom-call | tf_op jit(solution)/shard_map/pallas_call | solution.py:475
  45.1 1.5 %all-to-all-done.1 = f32[64,1,1024]{2,1,0:T(1,128)S(1)} async-done(((f32[64,1,1024]{2,1,0:T(1,128)}), f32[64,1,1024]{2,1,0:T(1,128)S(1)}, u32[]{:S(2)}, u32[]{:S(2)}) %all-to-all-start.1) | async-done | bytes 262176 | tf_op jit(solution)/shard_map/all_to_all | solution.py:507
  46.6 1.8 %shard_map.130 = (f32[3,32,128]{2,1,0:T(8,128)S(1)}, f32[3,32,128]{2,1,0:T(8,128)S(1)}, f32[3,8,128]{2,1,0:T(8,128)S(1)}, f32[3,8,128]{2,1,0:T(8,128)S(1)}) custom-call(f32[512,128]{1,0:T(8,128)S(1)} %bitcast.27, f32[64,128]{1,0:T(8,128)S(1)} %get-tuple-element.27.slot_of, f32[3,64,128]{2,1,0:T(8,128)S(1)} %get-tuple-element.28.at_slaves, ...), custom_call_target="tpu_custom_call" | custom-call | tf_op jit(solution)/shard_map/pallas_call | solution.py:475
  48.4 4.3 %shard_map.131 = (f32[896,128]{1,0:T(8,128)}, f32[3,64,128]{2,1,0:T(8,128)S(1)}) custom-call(f32[3,32,128]{2,1,0:T(8,128)S(1)} %get-tuple-element.37.u.disp, s32[64,128]{1,0:T(8,128)S(1)} %bitcast.35, s32[32,128]{1,0:T(8,128)S(1)} %bitcast.43, f32[64,128]{1,0:T(8,128)S(1)} %get-tuple-element.27.slot_of, f32[768,128]{1,0:T(8,128)S(1)} %bitcast.22), custom_call_target="tpu_custom_call" | custom-call | tf_op jit(solution)/shard_map/pallas_call | solution.py:475
  52.7 8.6 %all-to-all-start.2 = ((f32[64,1,1792]{2,1,0:T(1,128)}), f32[64,1,1792]{2,1,0:T(1,128)S(1)}, u32[]{:S(2)}, u32[]{:S(2)}) async-start(f32[64,1,1792]{2,1,0:T(1,128)} %bitcast.24), calls=%async_computation.2 | async-start | bytes 917504 | tf_op jit(solution)/shard_map/all_to_all | solution.py:507
  61.3 1.1 %collective-permute-start.5 = (f32[3,8,128]{2,1,0:T(8,128)S(1)}, f32[3,8,128]{2,1,0:T(8,128)S(1)}, u32[]{:S(2)}, u32[]{:S(2)}) collective-permute-start(f32[3,8,128]{2,1,0:T(8,128)S(1)} %get-tuple-element.40), channel_id=1, source_target_pairs={{0,8},{8,16},{16,24},{24,32},{32,40},{40,48},{48,56},{56,64},{64,7... | collective-permute-start | bytes 36872 | tf_op jit(solution)/shard_map/ppermute | solution.py:488
  62.4 3.8 %collective-permute-start.6 = (f32[3,8,128]{2,1,0:T(8,128)S(1)}, f32[3,8,128]{2,1,0:T(8,128)S(1)}, u32[]{:S(2)}, u32[]{:S(2)}) collective-permute-start(f32[3,8,128]{2,1,0:T(8,128)S(1)} %get-tuple-element.41), channel_id=1, source_target_pairs={{8,0},{16,8},{24,16},{32,24},{40,32},{48,40},{56,48},{64,56},{72,6... | collective-permute-start | bytes 36872 | tf_op jit(solution)/shard_map/ppermute | solution.py:489
  66.2 4.6 %collective-permute-done.5.x_low = f32[3,8,128]{2,1,0:T(8,128)S(1)} collective-permute-done((f32[3,8,128]{2,1,0:T(8,128)S(1)}, f32[3,8,128]{2,1,0:T(8,128)S(1)}, u32[]{:S(2)}, u32[]{:S(2)}) %collective-permute-start.5) | collective-permute-done | bytes 12320 | tf_op jit(solution)/shard_map/ppermute | solution.py:488
  70.8 1.3 %collective-permute-start.7 = (f32[3,8,128]{2,1,0:T(8,128)S(1)}, f32[3,8,128]{2,1,0:T(8,128)S(1)}, u32[]{:S(2)}, u32[]{:S(2)}) collective-permute-start(f32[3,8,128]{2,1,0:T(8,128)S(1)} %get-tuple-element.42), channel_id=1, source_target_pairs={{0,2},{2,4},{4,6},{6,0},{1,3},{3,5},{5,7},{7,1},{8,10},{10,12},{12... | collective-permute-start | bytes 36872 | tf_op jit(solution)/shard_map/ppermute | solution.py:488
  72.1 1.4 %collective-permute-start.8 = (f32[3,8,128]{2,1,0:T(8,128)S(1)}, f32[3,8,128]{2,1,0:T(8,128)S(1)}, u32[]{:S(2)}, u32[]{:S(2)}) collective-permute-start(f32[3,8,128]{2,1,0:T(8,128)S(1)} %get-tuple-element.43), channel_id=1, source_target_pairs={{2,0},{4,2},{6,4},{0,6},{3,1},{5,3},{7,5},{1,7},{10,8},{12,10},{14... | collective-permute-start | bytes 36872 | tf_op jit(solution)/shard_map/ppermute | solution.py:489
  73.5 1.1 %collective-permute-done.7.y_low = f32[3,8,128]{2,1,0:T(8,128)S(1)} collective-permute-done((f32[3,8,128]{2,1,0:T(8,128)S(1)}, f32[3,8,128]{2,1,0:T(8,128)S(1)}, u32[]{:S(2)}, u32[]{:S(2)}) %collective-permute-start.7) | collective-permute-done | bytes 12320 | tf_op jit(solution)/shard_map/ppermute | solution.py:488
  74.6 0.1 collective-permute-done.8.y_high
  74.7 3.2 %collective-permute-start.9 = (f32[3,6,16,128]{3,2,1,0:T(8,128)S(1)}, f32[3,6,16,128]{3,2,1,0:T(8,128)S(1)}, u32[]{:S(2)}, u32[]{:S(2)}) collective-permute-start(f32[3,6,16,128]{3,2,1,0:T(8,128)S(1)} %shard_map.133.near), channel_id=1, source_target_pairs={{0,1},{1,0},{2,3},{3,2},{4,5},{5,4},{6,7},{7,6},{8,9},{9,8},{10,11... | collective-permute-start | bytes 442376 | tf_op jit(solution)/shard_map/ppermute | solution.py:501
  77.9 1.0 %collective-permute-done.9.other = f32[3,6,16,128]{3,2,1,0:T(8,128)S(1)} collective-permute-done((f32[3,6,16,128]{3,2,1,0:T(8,128)S(1)}, f32[3,6,16,128]{3,2,1,0:T(8,128)S(1)}, u32[]{:S(2)}, u32[]{:S(2)}) %collective-permute-start.9) | collective-permute-done | bytes 147488 | tf_op jit(solution)/shard_map/ppermute | solution.py:501
  78.9 0.3 shard_map.134
  79.3 5.7 %shard_map.135 = (f32[3,32,128]{2,1,0:T(8,128)}, f32[3,32,128]{2,1,0:T(8,128)}) custom-call(f32[896,128]{1,0:T(8,128)S(1)} %bitcast.25, f32[896,128]{1,0:T(8,128)S(1)} %copy-done, f32[768,128]{1,0:T(8,128)S(1)} %bitcast.23, s32[128,128]{1,0:T(8,128)S(1)} %get-tuple-element.29.face_row, s32[128,128]{1,0:T(8,128)S(1)} %get-tuple-element.30.face_lane, ...), custom_call_target="tpu_custom_call" | custom-call | tf_op jit(solution)/shard_map/pallas_call | solution.py:475
  (24 shorter events, 0.1 us)
Async XLA Ops:
  4.8 24.6 %all-to-all-start = ((f32[64,1,1536]{2,1,0:T(1,128)}), f32[64,1,1536]{2,1,0:T(1,128)S(1)}, u32[]{:S(2)}, u32[]{:S(2)}) async-start(f32[64,1,1536]{2,1,0:T(1,128)} %bitcast.48), calls=%async_computation | async-start | bytes 786432 | tf_op jit(solution)/shard_map/all_to_all | solution.py:507
  17.6 8.0 %collective-permute-start = (f32[5,8,128]{2,1,0:T(8,128)S(1)}, f32[5,8,128]{2,1,0:T(8,128)S(1)}, u32[]{:S(2)}, u32[]{:S(2)}) collective-permute-start(f32[5,8,128]{2,1,0:T(8,128)S(1)} %get-tuple-element.32), channel_id=1, source_target_pairs={{0,8},{8,16},{16,24},{24,32},{32,40},{40,48},{48,56},{56,64},{64,7... | collective-permute-start | bytes 61448 | tf_op jit(solution)/shard_map/ppermute | solution.py:488
  18.6 6.9 %collective-permute-start.1 = (f32[5,8,128]{2,1,0:T(8,128)S(1)}, f32[5,8,128]{2,1,0:T(8,128)S(1)}, u32[]{:S(2)}, u32[]{:S(2)}) collective-permute-start(f32[5,8,128]{2,1,0:T(8,128)S(1)} %get-tuple-element.33), channel_id=1, source_target_pairs={{8,0},{16,8},{24,16},{32,24},{40,32},{48,40},{56,48},{64,56},{72,6... | collective-permute-start | bytes 61448 | tf_op jit(solution)/shard_map/ppermute | solution.py:489
  25.5 2.8 %copy-start.2 = (f32[3,4,8,128]{3,2,1,0:T(8,128)S(1)}, f32[3,4,8,128]{3,2,1,0:T(8,128)}, u32[]{:S(2)}) copy-start(f32[3,4,8,128]{3,2,1,0:T(8,128)} %disp.1) | copy-start | bytes 147460
  25.5 2.8 %copy-start.5 = (s32[1,1,1,32,128]{4,3,2,1,0:T(8,128)S(1)}, s32[1,1,1,32,128]{4,3,2,1,0:T(8,128)}, u32[]{:S(2)}) copy-start(s32[1,1,1,32,128]{4,3,2,1,0:T(8,128)} %param.21) | copy-start | bytes 49156
  25.6 11.4 %collective-permute-start.2 = (f32[5,8,128]{2,1,0:T(8,128)S(1)}, f32[5,8,128]{2,1,0:T(8,128)S(1)}, u32[]{:S(2)}, u32[]{:S(2)}) collective-permute-start(f32[5,8,128]{2,1,0:T(8,128)S(1)} %get-tuple-element.34), channel_id=1, source_target_pairs={{0,2},{2,4},{4,6},{6,0},{1,3},{3,5},{5,7},{7,1},{8,10},{10,12},{12... | collective-permute-start | bytes 61448 | tf_op jit(solution)/shard_map/ppermute | solution.py:488
  27.0 10.0 %collective-permute-start.3 = (f32[5,8,128]{2,1,0:T(8,128)S(1)}, f32[5,8,128]{2,1,0:T(8,128)S(1)}, u32[]{:S(2)}, u32[]{:S(2)}) collective-permute-start(f32[5,8,128]{2,1,0:T(8,128)S(1)} %get-tuple-element.35), channel_id=1, source_target_pairs={{2,0},{4,2},{6,4},{0,6},{3,1},{5,3},{7,5},{1,7},{10,8},{12,10},{14... | collective-permute-start | bytes 61448 | tf_op jit(solution)/shard_map/ppermute | solution.py:489
  30.5 16.1 %all-to-all-start.1 = ((f32[64,1,1024]{2,1,0:T(1,128)}), f32[64,1,1024]{2,1,0:T(1,128)S(1)}, u32[]{:S(2)}, u32[]{:S(2)}) async-start(f32[64,1,1024]{2,1,0:T(1,128)} %bitcast.26), calls=%async_computation.1 | async-start | bytes 524288 | tf_op jit(solution)/shard_map/all_to_all | solution.py:507
  37.1 4.7 %copy-start.1 = (f32[512,128]{1,0:T(8,128)S(1)}, f32[512,128]{1,0:T(8,128)}, u32[]{:S(2)}) copy-start(f32[512,128]{1,0:T(8,128)} %get-tuple-element.26.frames) | copy-start | bytes 786436
  37.1 4.3 %collective-permute-start.4 = (f32[5,6,16,128]{3,2,1,0:T(8,128)S(1)}, f32[5,6,16,128]{3,2,1,0:T(8,128)S(1)}, u32[]{:S(2)}, u32[]{:S(2)}) collective-permute-start(f32[5,6,16,128]{3,2,1,0:T(8,128)S(1)} %shard_map.128.near), channel_id=1, source_target_pairs={{0,1},{1,0},{2,3},{3,2},{4,5},{5,4},{6,7},{7,6},{8,9},{9,8},{10,11... | collective-permute-start | bytes 737288 | tf_op jit(solution)/shard_map/ppermute | solution.py:501
  41.8 4.8 %copy-start.3 = (s32[1,1,1,64,128]{4,3,2,1,0:T(8,128)S(1)}, s32[1,1,1,64,128]{4,3,2,1,0:T(8,128)}, u32[]{:S(2)}) copy-start(s32[1,1,1,64,128]{4,3,2,1,0:T(8,128)} %param.16) | copy-start | bytes 98308
  41.8 4.8 %copy-start.4 = (f32[1,1,1,64,128]{4,3,2,1,0:T(8,128)S(1)}, f32[1,1,1,64,128]{4,3,2,1,0:T(8,128)}, u32[]{:S(2)}) copy-start(f32[1,1,1,64,128]{4,3,2,1,0:T(8,128)} %param.17) | copy-start | bytes 98308
  41.8 4.8 %copy-start.6 = (f32[4,8,128]{2,1,0:T(8,128)S(1)}, f32[4,8,128]{2,1,0:T(8,128)}, u32[]{:S(2)}) copy-start(f32[4,8,128]{2,1,0:T(8,128)} %param.15) | copy-start | bytes 49156
  41.8 4.8 %copy-start.7 = (f32[3,4,8,128]{3,2,1,0:T(8,128)S(1)}, f32[3,4,8,128]{3,2,1,0:T(8,128)}, u32[]{:S(2)}) copy-start(f32[3,4,8,128]{3,2,1,0:T(8,128)} %param.12) | copy-start | bytes 147460
  52.7 26.6 %all-to-all-start.2 = ((f32[64,1,1792]{2,1,0:T(1,128)}), f32[64,1,1792]{2,1,0:T(1,128)S(1)}, u32[]{:S(2)}, u32[]{:S(2)}) async-start(f32[64,1,1792]{2,1,0:T(1,128)} %bitcast.24), calls=%async_computation.2 | async-start | bytes 917504 | tf_op jit(solution)/shard_map/all_to_all | solution.py:507
  61.3 17.9 %copy-start = (f32[896,128]{1,0:T(8,128)S(1)}, f32[896,128]{1,0:T(8,128)}, u32[]{:S(2)}) copy-start(f32[896,128]{1,0:T(8,128)} %get-tuple-element.38.sent) | copy-start | bytes 1376260
  61.3 9.5 %collective-permute-start.5 = (f32[3,8,128]{2,1,0:T(8,128)S(1)}, f32[3,8,128]{2,1,0:T(8,128)S(1)}, u32[]{:S(2)}, u32[]{:S(2)}) collective-permute-start(f32[3,8,128]{2,1,0:T(8,128)S(1)} %get-tuple-element.40), channel_id=1, source_target_pairs={{0,8},{8,16},{16,24},{24,32},{32,40},{40,48},{48,56},{56,64},{64,7... | collective-permute-start | bytes 36872 | tf_op jit(solution)/shard_map/ppermute | solution.py:488
  62.4 8.4 %collective-permute-start.6 = (f32[3,8,128]{2,1,0:T(8,128)S(1)}, f32[3,8,128]{2,1,0:T(8,128)S(1)}, u32[]{:S(2)}, u32[]{:S(2)}) collective-permute-start(f32[3,8,128]{2,1,0:T(8,128)S(1)} %get-tuple-element.41), channel_id=1, source_target_pairs={{8,0},{16,8},{24,16},{32,24},{40,32},{48,40},{56,48},{64,56},{72,6... | collective-permute-start | bytes 36872 | tf_op jit(solution)/shard_map/ppermute | solution.py:489
  70.8 3.8 %collective-permute-start.7 = (f32[3,8,128]{2,1,0:T(8,128)S(1)}, f32[3,8,128]{2,1,0:T(8,128)S(1)}, u32[]{:S(2)}, u32[]{:S(2)}) collective-permute-start(f32[3,8,128]{2,1,0:T(8,128)S(1)} %get-tuple-element.42), channel_id=1, source_target_pairs={{0,2},{2,4},{4,6},{6,0},{1,3},{3,5},{5,7},{7,1},{8,10},{10,12},{12... | collective-permute-start | bytes 36872 | tf_op jit(solution)/shard_map/ppermute | solution.py:488
  72.1 2.5 %collective-permute-start.8 = (f32[3,8,128]{2,1,0:T(8,128)S(1)}, f32[3,8,128]{2,1,0:T(8,128)S(1)}, u32[]{:S(2)}, u32[]{:S(2)}) collective-permute-start(f32[3,8,128]{2,1,0:T(8,128)S(1)} %get-tuple-element.43), channel_id=1, source_target_pairs={{2,0},{4,2},{6,4},{0,6},{3,1},{5,3},{7,5},{1,7},{10,8},{12,10},{14... | collective-permute-start | bytes 36872 | tf_op jit(solution)/shard_map/ppermute | solution.py:489
  74.7 4.2 %collective-permute-start.9 = (f32[3,6,16,128]{3,2,1,0:T(8,128)S(1)}, f32[3,6,16,128]{3,2,1,0:T(8,128)S(1)}, u32[]{:S(2)}, u32[]{:S(2)}) collective-permute-start(f32[3,6,16,128]{3,2,1,0:T(8,128)S(1)} %shard_map.133.near), channel_id=1, source_target_pairs={{0,1},{1,0},{2,3},{3,2},{4,5},{5,4},{6,7},{7,6},{8,9},{9,8},{10,11... | collective-permute-start | bytes 442376 | tf_op jit(solution)/shard_map/ppermute | solution.py:501

commit v3 on v2

--- a/solution.py
+++ b/solution.py
@@ -46,23 +46,30 @@
     return out + jnp.dot(onehot, high, preferred_element_type=F32)
 
 
-def gather_nodes(u_ref, nodes):
-    row = nodes >> 7
-    lane = nodes & 127
-    out = [jnp.zeros((PAIRS, PATCH), F32) for _ in range(3)]
-    for r in range(ROWS):
-        here = row == r
+def gather_nodes(u_ref, slaves, out_ref):
+    def body(i, carry):
+        start = pl.multiple_of(i * 8, 8)
+        nodes = slaves[pl.ds(start, 8), :]
+        row = nodes >> 7
+        lane = nodes & 127
+        out = [jnp.zeros((8, PATCH), F32) for _ in range(3)]
+        for r in range(ROWS):
+            here = row == r
+            for c in range(3):
+                source = jnp.broadcast_to(u_ref[c, r : r + 1, :], (8, PATCH))
+                out[c] = jnp.where(here, lane_pick(source, lane), out[c])
         for c in range(3):
-            source = jnp.broadcast_to(u_ref[c, r : r + 1, :], (PAIRS, PATCH))
-            out[c] = jnp.where(here, lane_pick(source, lane), out[c])
-    return out
+            out_ref[c, pl.ds(start, 8), :] = out[c]
+        return carry
+
+    lax.fori_loop(0, PAIRS // 8, body, 0)
 
 
 def up(x, amount):
     return pltpu.roll(x, x.shape[0] - amount, 0)
 
 
-def patch_table(u_ref, faces):
+def patch_table(u_ref, faces, normals):
     frames = []
     one = [u_ref[c] for c in range(3)]
     two = [up(x, 8) for x in one]
@@ -80,16 +87,23 @@
     normal = [x / length for x in normal]
     offset = centroid[0] * normal[0] + centroid[1] * normal[1] + centroid[2] * normal[2]
     frames = normal + [offset]
-    row = faces >> 7
-    lane = faces & 127
-    out = [jnp.zeros((PATCHES, PATCH), F32) for _ in range(4)]
-    for r in range((NI - 1) * NJ):
-        if r % NJ == NJ - 1:
-            continue
-        here = row == r
+    for c in range(3):
+        normals[c] = normal[c]
+    out = [[] for _ in range(4)]
+    for start in range(0, PATCHES, 8):
+        row = faces[start : start + 8] >> 7
+        lane = faces[start : start + 8] & 127
+        best = [jnp.zeros((8, PATCH), F32) for _ in range(4)]
+        for r in range((NI - 1) * NJ):
+            if r % NJ == NJ - 1:
+                continue
+            here = row == r
+            for c in range(4):
+                source = jnp.broadcast_to(frames[c][r : r + 1, :], (8, PATCH))
+                best[c] = jnp.where(here, lane_pick(source, lane), best[c])
         for c in range(4):
-            source = jnp.broadcast_to(frames[c][r : r + 1, :], (PATCHES, PATCH))
-            out[c] = jnp.where(here, lane_pick(source, lane), out[c])
+            out[c].append(best[c])
+    out = [jnp.concatenate(x, axis=0) for x in out]
     table = jnp.concatenate(out, axis=1)
     high, mid, low = parts_3(table)
     return jnp.concatenate([high, mid, low, jnp.zeros_like(high)], axis=0)
@@ -100,6 +114,8 @@
 
 
 def scatter_nodes(count, row_lane, forces_ref):
+    pieces_count = forces_ref.shape[0]
+    parts_count = pieces_count // 2
     half = ROWS // 2
     row_at = iota((half, PATCH), 0).astype(F32).astype(BF16)
     lane_at = iota((2 * PATCH, PATCH), 0).astype(F32).astype(BF16)
@@ -110,7 +126,7 @@
         rows, lanes = row_lane(start)
         lanes = (lanes + (rows >> 4) * PATCH).astype(F32)
         rows = (rows & (half - 1)).astype(F32)
-        parts = [forces_ref[c, pl.ds(start, 32), :] for c in range(6)]
+        parts = [forces_ref[c, pl.ds(start, 32), :] for c in range(pieces_count)]
         left = []
         right = []
         for q in range(32):
@@ -125,10 +141,10 @@
             left, right, (((1,), (1,)), ((), ())), preferred_element_type=F32
         )
 
-    acc = lax.fori_loop(0, count // 32, body, jnp.zeros((6 * half, 2 * PATCH), F32))
-    acc = acc[0 : 3 * half] + acc[3 * half : 6 * half]
+    acc = lax.fori_loop(0, count // 32, body, jnp.zeros((pieces_count * half, 2 * PATCH), F32))
+    acc = acc[0 : parts_count * half] + acc[parts_count * half : pieces_count * half]
     out = []
-    for c in range(3):
+    for c in range(parts_count):
         part = acc[c * half : (c + 1) * half]
         out.append(jnp.concatenate([part[:, 0:PATCH], part[:, PATCH:]], axis=0))
     return out
@@ -137,7 +153,8 @@
 def store_parts(forces_ref, c, start, force):
     high = force.astype(BF16).astype(F32)
     forces_ref[c, start : start + force.shape[0], :] = high
-    forces_ref[c + 3, start : start + force.shape[0], :] = force - high
+    low = c + forces_ref.shape[0] // 2
+    forces_ref[low, start : start + force.shape[0], :] = force - high
 
 
 def down_rows(x, amount):
@@ -145,47 +162,89 @@
     return jnp.where(iota(x.shape, 0) >= amount, moved, 0.0)
 
 
-def pair_force(u, normal, offset, gap):
+def pair_push(u, normal, offset, gap):
     now = gap + (u[0] * normal[0] + u[1] * normal[1] + u[2] * normal[2]) - offset
-    push = -PENALTY * jnp.minimum(now, 0.0)
-    return [push * normal[c] for c in range(3)]
+    return -PENALTY * jnp.minimum(now, 0.0)
 
 
 def every(ref, start, stride):
     return ref[pl.ds(start, GROUPS, stride=stride), :]
 
 
-def slabs_kernel(disp, lame, shear, five, low, high):
+def is_even(axis):
+    return lax.axis_index(axis) % 2 == 0
+
+
+def store_faces(axis, first, second, at, low, high):
+    even = is_even(axis)
+    first[at] = jnp.where(even, high, low)
+    second[at] = jnp.where(even, low, high)
+
+
+def low_high(axis, first, second):
+    even = is_even(axis)
+    return jnp.where(even, second, first), jnp.where(even, first, second)
+
+
+def slabs_kernel(
+    disp, lame, shear, vel, mass, faces, five, first, second, vel_out, mass_out, faces_out
+):
+    vel_out[...] = vel[...]
+    mass_out[...] = mass[...]
+    faces_out[...] = faces[...]
     for c in range(5):
         block = disp[c] if c < 3 else (lame[...] if c == 3 else shear[...])
         five[c] = block
-        low[c] = block[0]
-        high[c] = block[NI - 1]
-
-
-def rim_kernel(block, x_low, x_high, y_low, y_high):
+        store_faces("len", first, second, c, block[0], block[NI - 1])
+
+
+def widen_kernel(block, x_first, x_second, out):
     for c in range(block.shape[0]):
-        for out, j in ((y_low, 0), (y_high, NJ - 1)):
-            out[c, 0:1, :] = x_low[c, j : j + 1, :]
-            for i in range(NI):
-                out[c, i + 1 : i + 2, :] = block[c, i, j : j + 1, :]
-            out[c, 5:6, :] = x_high[c, j : j + 1, :]
-            out[c, 6:8, :] = jnp.zeros((2, NK), F32)
-
-
-def extend_kernel(block, x_low, x_high, y_low, y_high, out):
+        out[c, 0], out[c, NI + 1] = low_high("len", x_first[c], x_second[c])
+        for i in range(NI):
+            out[c, i + 1] = block[c, i]
+
+
+def face_rows(planes, j):
+    rows = [x[j : j + 1, :] for x in planes]
+    return jnp.concatenate(rows + [jnp.zeros((8 - len(rows), NK), F32)], axis=0)
+
+
+def rim_kernel(near, other, first, second):
+    for half, source in enumerate((near, other)):
+        for c in range(source.shape[0]):
+            planes = [source[c, i] for i in range(NI + 2)]
+            low, high = face_rows(planes, 0), face_rows(planes, NJ - 1)
+            store_faces("wid", first, second, half * source.shape[0] + c, low, high)
+
+
+def ring_kernel(block, x_first, x_second, first, second):
     for c in range(block.shape[0]):
-        for i in range(NI + 2):
-            if i == 0:
-                middle = x_low[c]
-            elif i == NI + 1:
-                middle = x_high[c]
-            else:
-                middle = block[c, i - 1]
-            out[c, i, 1:9, :] = middle
-            out[c, i, 0:1, :] = y_low[c, i : i + 1, :]
-            out[c, i, 9:10, :] = y_high[c, i : i + 1, :]
-            out[c, i, 10:16, :] = jnp.zeros((6, NK), F32)
+        x_low, x_high = low_high("len", x_first[c], x_second[c])
+        planes = [x_low] + [block[c, i] for i in range(NI)] + [x_high]
+        store_faces("wid", first, second, c, face_rows(planes, 0), face_rows(planes, NJ - 1))
+
+
+def put_planes(out, c, planes, first, second):
+    low, high = low_high("wid", first, second)
+    for i, plane in enumerate(planes):
+        out[c, i, 1:9, :] = plane
+        out[c, i, 0:1, :] = low[i : i + 1, :]
+        out[c, i, 9:10, :] = high[i : i + 1, :]
+        out[c, i, 10:16, :] = jnp.zeros((6, NK), F32)
+
+
+def extend(source, first, second, half, out):
+    for c in range(source.shape[0]):
+        at = half * source.shape[0] + c
+        put_planes(out, c, [source[c, i] for i in range(NI + 2)], first[at], second[at])
+
+
+def extend_kernel(block, x_first, x_second, y_first, y_second, out):
+    for c in range(block.shape[0]):
+        x_low, x_high = low_high("len", x_first[c], x_second[c])
+        planes = [x_low] + [block[c, i] for i in range(NI)] + [x_high]
+        put_planes(out, c, planes, y_first[c], y_second[c])
 
 
 def far_plane(near, other):
@@ -269,17 +328,14 @@
     return out
 
 
-def internal_first_kernel(near, other, out, moduli):
-    lame = element_moduli(near[3], other[3])
-    shear = element_moduli(near[4], other[4])
+def internal_first_kernel(near, other, y_low, y_high, out, moduli, here, there):
+    extend(near, y_low, y_high, 0, here)
+    extend(other, y_low, y_high, 1, there)
+    lame = element_moduli(here[3], there[3])
+    shear = element_moduli(here[4], there[4])
     moduli[0] = lame
     moduli[1] = shear
-    for c, force in enumerate(internal_force(near, other, lame, shear)):
-        out[c] = force
-
-
-def internal_kernel(near, other, moduli, out):
-    for c, force in enumerate(internal_force(near, other, moduli[0], moduli[1])):
+    for c, force in enumerate(internal_force(here, there, lame, shear)):
         out[c] = force
 
 
@@ -295,7 +351,11 @@
     return jnp.sum(jnp.where(eye, row, 0.0), axis=1, keepdims=True)
 
 
-def request_kernel(u, slaves, gaps, chosen, owners, wanted, send, slot_of, at_slaves):
+def request_kernel(
+    u, slaves, gaps, chosen, owners, wanted, send, slot_of, at_slaves, slaves_out, gaps_out
+):
+    slaves_out[...] = slaves[...]
+    gaps_out[...] = gaps[...]
     owner_row = owners[...].astype(F32)
     owner = row_to_column(owner_row)
     same = (owner == owner_row) & (iota((PAIRS, PAIRS), 1) < iota((PAIRS, PAIRS), 0))
@@ -304,9 +364,8 @@
     slot_row = column_to_row(slot)
     slot_of[...] = jnp.where(slot == iota((PAIRS, SLOTS), 1).astype(F32), 1.0, 0.0)
     place = jnp.where(slot_row == iota((SLOTS, PAIRS), 0).astype(F32), 1.0, 0.0).astype(BF16)
-    values = gather_nodes(u, slaves[...])
-    for c in range(3):
-        at_slaves[c] = values[c]
+    gather_nodes(u, slaves, at_slaves)
+    values = [at_slaves[c] for c in range(3)]
     exact = jnp.concatenate(values + [gaps[...]], axis=1)
     moved = select_dot(place, exact)
     patch = jnp.broadcast_to(row_to_column(wanted[...].astype(F32) + 1.0), (PAIRS, PATCH))
@@ -330,8 +389,8 @@
     return onehot, cand.astype(I32)
 
 
-def table_kernel(u, faces, table):
-    table[...] = patch_table(u, faces[...])
+def table_kernel(u, faces, table, normals):
+    table[...] = patch_table(u, faces[...], normals)
 
 
 def reply_kernel(arrived, table, faces, send, face_row, face_lane):
@@ -355,17 +414,20 @@
         u = [every(values, t * offset + c, stride) for c in range(3)]
         gap = every(gap_source, t * 4 + 3, 12)
         frame = [every(frames, t * frame_offset[1] + frame_offset[0] + c, frame_stride) for c in range(4)]
-        force = pair_force(u, frame[0:3], frame[3], gap)
-        for c in range(3):
-            store_parts(scratch, c, t * GROUPS, -0.25 * force[c])
-
-
-def face_contact(face_row, face_lane, scratch):
+        push = pair_push(u, frame[0:3], frame[3], gap)
+        store_parts(scratch, 0, t * GROUPS, -0.25 * push)
+
+
+def face_contact(face_row, face_lane, normals, scratch):
     def row_lane(start):
         return face_row[pl.ds(start, 32), :], face_lane[pl.ds(start, 32), :]
 
-    faces = scatter_nodes(SLOTS, row_lane, scratch)
-    return [x + down_rows(x, 8) + down_rows(x, 9) + down_rows(x, 1) for x in faces]
+    (push,) = scatter_nodes(SLOTS, row_lane, scratch)
+    out = []
+    for c in range(3):
+        x = jnp.where(push == 0.0, 0.0, push * normals[c])
+        out.append(x + down_rows(x, 8) + down_rows(x, 9) + down_rows(x, 1))
+    return out
 
 
 def slave_contact(arrived, stride, offset, slot_of, at_slaves, gaps, slaves, scratch):
@@ -379,9 +441,9 @@
         )
     mine = select_dot(onehot, jnp.concatenate(slots, axis=1))
     frame = [mine[:, c * 128 : (c + 1) * 128] for c in range(4)]
-    force = pair_force([at_slaves[c] for c in range(3)], frame[0:3], frame[3], gaps[...])
+    push = pair_push([at_slaves[c] for c in range(3)], frame[0:3], frame[3], gaps[...])
     for c in range(3):
-        store_parts(scratch, c, 0, force[c])
+        store_parts(scratch, c, 0, push * frame[c])
 
     def row_lane(start):
         nodes = slaves[pl.ds(start, 32), :]
@@ -390,9 +452,9 @@
     return scatter_nodes(PAIRS, row_lane, scratch)
 
 
-def reaction_kernel(arrived, frames, face_row, face_lane, out, scratch):
+def reaction_kernel(arrived, frames, face_row, face_lane, normals, out, scratch):
     owner_forces(arrived, arrived, frames, 12, 4, 8, (0, 4), scratch)
-    for c, force in enumerate(face_contact(face_row, face_lane, scratch)):
+    for c, force in enumerate(face_contact(face_row, face_lane, normals, scratch)):
         out[c] = force
 
 
@@ -406,27 +468,25 @@
 
 def middle_kernel(
     arrived, slot_of, at_slaves, gaps, slaves, reaction, internal, disp, vel, mass,
-    new_disp, new_vel, low, high, scratch,
+    new_disp, new_vel, first, second, scratch,
 ):
     contact = slave_contact(arrived, 8, (0, 4), slot_of, at_slaves, gaps, slaves, scratch)
     for c in range(3):
         force = internal[c] + (contact[c] + reaction[c])
         place = advance(c, force, disp, vel, mass, new_disp, new_vel)
-        low[c] = place[0:NJ]
-        high[c] = place[ROWS - NJ : ROWS]
-
-
-def second_kernel(u, slaves, faces, slot_of, arrived, send, at_slaves):
-    values = gather_nodes(u, slaves[...])
-    for c in range(3):
-        at_slaves[c] = values[c]
+        store_faces("len", first, second, c, place[0:NJ], place[ROWS - NJ : ROWS])
+
+
+def second_kernel(u, slaves, faces, slot_of, arrived, send, at_slaves, normals):
+    gather_nodes(u, slaves, at_slaves)
+    values = [at_slaves[c] for c in range(3)]
     place = slot_of[...].astype(BF16)
     high, mid, low = parts_3(jnp.concatenate(values, axis=1))
     dims = (((0,), (0,)), ((), ()))
     moved = lax.dot_general(place, low, dims, preferred_element_type=F32)
     moved = moved + lax.dot_general(place, mid, dims, preferred_element_type=F32)
     moved = moved + lax.dot_general(place, high, dims, preferred_element_type=F32)
-    table = patch_table(u, faces[...])
+    table = patch_table(u, faces[...], normals)
     onehot, cand = wanted_rows(arrived)
     tiles = jnp.dot(onehot, table, preferred_element_type=F32)
     for t in range(CAP):
@@ -441,16 +501,22 @@
             ]
 
 
-def last_kernel(
-    arrived, sent, first, face_row, face_lane, slot_of, at_slaves, gaps, slaves, internal,
-    disp, vel, mass, new_disp, new_vel, scratch, slave_scratch,
+def contact_kernel(
+    arrived, sent, first, face_row, face_lane, normals, slot_of, at_slaves, gaps, slaves, out,
+    scratch, slave_scratch,
 ):
     owner_forces(arrived, first, sent, 14, 7, 14, (3, 7), scratch)
-    reaction = face_contact(face_row, face_lane, scratch)
+    reaction = face_contact(face_row, face_lane, normals, scratch)
     contact = slave_contact(arrived, 14, (3, 7), slot_of, at_slaves, gaps, slaves, slave_scratch)
     for c in range(3):
-        force = internal[c] + (contact[c] + reaction[c])
-        advance(c, force, disp, vel, mass, new_disp, new_vel)
+        out[c] = contact[c] + reaction[c]
+
+
+def finish_kernel(near, other, moduli, contact, disp, vel, mass, new_disp, new_vel):
+    for c, internal in enumerate(internal_force(near, other, moduli[0], moduli[1])):
+        moved = vel[c] + TIME_STEP * (internal + contact[c]) / mass[...]
+        new_vel[c] = moved
+        new_disp[c] = disp[c] + TIME_STEP * moved
 
 
 def f32(*shape):
@@ -483,21 +549,28 @@
     )(*inputs)
 
 
-def shift_pair(low, high, axis):
+def swap_pair(first, second, axis):
     count = lax.axis_size(axis)
-    from_low = lax.ppermute(high, axis, [(i, (i + 1) % count) for i in range(count)])
-    from_high = lax.ppermute(low, axis, [((i + 1) % count, i) for i in range(count)])
-    return from_low, from_high
+    mate = [(i, i ^ 1) for i in range(count)]
+    other = [(i, (i - 1 if i % 2 == 0 else i + 1) % count) for i in range(count)]
+    return lax.ppermute(first, axis, mate), lax.ppermute(second, axis, other)
+
+
+def surroundings(block, low, high):
+    parts = block.shape[0]
+    x_low, x_high = swap_pair(low, high, "len")
+    near = call(widen_kernel, f32(parts, NI + 2, NJ, NK), block, x_low, x_high)
+    other = lax.ppermute(near, "lay", [(0, 1), (1, 0)])
+    low, high = call(rim_kernel, (f32(2 * parts, 8, NK), f32(2 * parts, 8, NK)), near, other)
+    y_low, y_high = swap_pair(low, high, "wid")
+    return near, other, y_low, y_high
 
 
 def extended(block, low, high):
-    parts = block.shape[0]
-    x_low, x_high = shift_pair(low, high, "len")
-    low, high = call(rim_kernel, (f32(parts, 8, NK), f32(parts, 8, NK)), block, x_low, x_high)
-    y_low, y_high = shift_pair(low, high, "wid")
-    near = call(
-        extend_kernel, f32(parts, NI + 2, 16, NK), block, x_low, x_high, y_low, y_high
-    )
+    x_low, x_high = swap_pair(low, high, "len")
+    low, high = call(ring_kernel, (f32(3, 8, NK), f32(3, 8, NK)), block, x_low, x_high)
+    y_low, y_high = swap_pair(low, high, "wid")
+    near = call(extend_kernel, f32(3, NI + 2, 16, NK), block, x_low, x_high, y_low, y_high)
     other = lax.ppermute(near, "lay", [(0, 1), (1, 0)])
     return near, other
 
@@ -521,19 +594,27 @@
     u = displacement.reshape(3, ROWS, NK)
     v = velocity.reshape(3, ROWS, NK)
     mass = nodal_mass.reshape(ROWS, NK)
-    five, low, high = call(
+    five, low, high, v, mass, faces = call(
         slabs_kernel,
-        (f32(5, NI, NJ, NK), f32(5, NJ, NK), f32(5, NJ, NK)),
-        displacement, lame_first, shear_modulus, raw=3,
-    )
-    near, other = extended(five, low, high)
-    send, slot_of, at_slaves = call(
+        (
+            f32(5, NI, NJ, NK), f32(5, NJ, NK), f32(5, NJ, NK), f32(3, ROWS, NK), f32(ROWS, NK),
+            i32(PATCHES, PATCH),
+        ),
+        displacement, lame_first, shear_modulus, v, mass, faces, raw=6,
+    )
+    around = surroundings(five, low, high)
+    send, slot_of, at_slaves, slaves, gaps = call(
         request_kernel,
-        (plain(GROUPS * 12, PATCH), f32(PAIRS, SLOTS), f32(3, PAIRS, PATCH)),
+        (
+            plain(GROUPS * 12, PATCH), f32(PAIRS, SLOTS), f32(3, PAIRS, PATCH),
+            i32(PAIRS, PATCH), f32(PAIRS, PATCH),
+        ),
         u, slaves, gaps, chosen, owners, wanted, raw=6,
     )
     first = exchange(send)
-    table = call(table_kernel, pltpu.VMEM((128, 512), BF16), u, faces)
+    table, normals = call(
+        table_kernel, (pltpu.VMEM((128, 512), BF16), f32(3, ROWS, NK)), u, faces
+    )
     reply, face_row, face_lane = call(
         reply_kernel,
         (plain(GROUPS * 8, PATCH), i32(SLOTS, PATCH), i32(SLOTS, PATCH)),
@@ -541,11 +622,12 @@
     )
     arrived = exchange(reply)
     reaction = call(
-        reaction_kernel, f32(3, ROWS, NK), first, reply, face_row, face_lane,
-        scratch=[(6, SLOTS, PATCH)],
+        reaction_kernel, f32(3, ROWS, NK), first, reply, face_row, face_lane, normals,
+        scratch=[(2, SLOTS, PATCH)],
     )
     internal, moduli = call(
-        internal_first_kernel, (f32(3, NI, NJ, NK), f32(2, 5, 16, NK)), near, other
+        internal_first_kernel, (f32(3, NI, NJ, NK), f32(2, 5, 16, NK)), *around,
+        scratch=[(5, NI + 2, 16, NK)] * 2,
     )
     u, v, low, high = call(
         middle_kernel,
@@ -555,19 +637,22 @@
         scratch=[(6, PAIRS, PATCH)],
     )
     near, other = extended(u.reshape(3, NI, NJ, NK), low, high)
-    sent, at_slaves = call(
+    sent, at_slaves, next_normals = call(
         second_kernel,
-        (plain(GROUPS * 14, PATCH), f32(3, PAIRS, PATCH)),
+        (plain(GROUPS * 14, PATCH), f32(3, PAIRS, PATCH), f32(3, ROWS, NK)),
         u, slaves, faces, slot_of, first,
     )
     arrived = exchange(sent)
-    internal = call(internal_kernel, f32(3, NI, NJ, NK), near, other, moduli)
+    contact = call(
+        contact_kernel, f32(3, ROWS, NK),
+        arrived, sent, first, face_row, face_lane, next_normals, slot_of, at_slaves, gaps, slaves,
+        scratch=[(2, SLOTS, PATCH), (6, PAIRS, PATCH)],
+    )
+    block = (3, NI, NJ, NK)
     u, v = call(
-        last_kernel,
-        (plain(3, ROWS, NK), plain(3, ROWS, NK)),
-        arrived, sent, first, face_row, face_lane, slot_of, at_slaves, gaps, slaves,
-        internal.reshape(3, ROWS, NK), u, v, mass,
-        scratch=[(6, SLOTS, PATCH), (6, PAIRS, PATCH)],
+        finish_kernel, (plain(*block), plain(*block)),
+        near, other, moduli, contact.reshape(block), u.reshape(block), v.reshape(block),
+        mass.reshape(NI, NJ, NK),
     )
     return u.reshape(displacement.shape), v.reshape(velocity.shape)
 

time: 85.4 us -> 90.5 us (1.060)
  waiting for transfers between devices: 12.5 us -> 19.6 us
  Pallas kernels: 23 us -> 19.9 us
  starting transfers between devices: 48.7 us -> 49.7 us
    all_to_all x3, waiting for transfers between devices: 1.49 us -> 9.53 us  [exchange(): lax.all_to_all(chunk, ('len', 'wid'), split_axis=0, concat_axis=0, tiled=...]
    ppermute x8 -> x9, starting transfers between devices: 15.2 us -> 20.5 us  [the longest x8 16.7 us: swap_pair(): return (lax.ppermute(first, axis, mate), lax.ppermute(second, axis, other))]
    pallas_call x14, Pallas kernels: 23 us -> 19.9 us  [call(): pl.pallas_call(kernel, out_shape=outs, in_specs=[whole if i < raw else lo...]
    all_to_all x3, starting transfers between devices: 27.1 us -> 24.6 us  [exchange(): lax.all_to_all(chunk, ('len', 'wid'), split_axis=0, concat_axis=0, tiled=...]
    ppermute x2 -> x1, waiting for transfers between devices: 2.15 us -> 0.01 us  [extended(): other = lax.ppermute(near, 'lay', [(0, 1), (1, 0)])]
    ppermute x2 -> x1, starting transfers between devices: 6.36 us -> 4.54 us  [extended(): other = lax.ppermute(near, 'lay', [(0, 1), (1, 0)])]
    ppermute x8 -> x9, waiting for transfers between devices: 8.87 us -> 10.1 us  [the longest x8 9.13 us: swap_pair(): return (lax.ppermute(first, axis, mate), lax.ppermute(second, axis, other))]
  transfers between devices with their start and end apart: 13 -> 13, of which waited for: 7 -> 6; matrix products, arithmetic and copies ran while one was open for 0% -> 0% of each run, Pallas kernels for 8% -> 11%
where the time goes in v3:
time: 90.5 us; the launch traced here: 90 us
  starting transfers between devices  49.7 us (55%)
  Pallas kernels  19.9 us (22%)
  waiting for transfers between devices  19.6 us (22%)
    all_to_all x3, starting transfers between devices, exchange(): lax.all_to_all(chunk, ('len', 'wid'), split_axis=0, concat_axis=0, tiled=...  24.6 us
    pallas_call x14, Pallas kernels, call(): pl.pallas_call(kernel, out_shape=outs, in_specs=[whole if i < raw else lo...  19.9 us
    ppermute x8, starting transfers between devices, swap_pair(): return (lax.ppermute(first, axis, mate), lax.ppermute(second, axis, other))  16.7 us
    all_to_all x3, waiting for transfers between devices, exchange(): lax.all_to_all(chunk, ('len', 'wid'), split_axis=0, concat_axis=0, tiled=...  9.53 us
    ppermute x8, waiting for transfers between devices, swap_pair(): return (lax.ppermute(first, axis, mate), lax.ppermute(second, axis, other))  9.13 us
    ppermute x1, starting transfers between devices, extended(): other = lax.ppermute(near, 'lay', [(0, 1), (1, 0)])  4.54 us
    ppermute x1, starting transfers between devices, surroundings(): other = lax.ppermute(near, 'lay', [(0, 1), (1, 0)])  3.83 us
  transfers between devices with their start and end apart: 13, of which 6 were waited for; matrix products, arithmetic and copies ran while one was open for 0% of the time, Pallas kernels for 11%

profile of v3, /device:TPU:1, one launch (start us, length us, event | category | flops | bytes accessed | tf_op | source)
XLA Modules:
  0.0 90.0 jit_solution(1216602756643835125)
XLA Ops:
  0.6 3.4 %shard_map.122 = (f32[768,128]{1,0:T(8,128)}, f32[64,128]{1,0:T(8,128)S(1)}, f32[3,64,128]{2,1,0:T(8,128)S(1)}, s32[64,128]{1,0:T(8,128)S(1)}, f32[64,128]{1,0:T(8,128)S(1)}) custom-call(f32[3,32,128]{2,1,0:T(8,128)} %bitcast.31, s32[64,128]{1,0:T(8,128)} %bitcast.40, f32[64,128]{1,0:T(8,128)} %bitcast.41, s32[64,128]{1,0:T(8,128)} %bitcast.42, ...), custom_call_target="tpu_custom_call" | custom-call | tf_op jit(solution)/shard_map/pallas_call | solution.py:541
  4.1 12.0 %all-to-all-start = ((f32[64,1,1536]{2,1,0:T(1,128)}), f32[64,1,1536]{2,1,0:T(1,128)S(1)}, u32[]{:S(2)}, u32[]{:S(2)}) async-start(f32[64,1,1536]{2,1,0:T(1,128)} %bitcast.38), calls=%async_computation | async-start | bytes 786432 | tf_op jit(solution)/shard_map/all_to_all | solution.py:580
  16.0 0.0 copy-start.2
  16.0 0.9 shard_map.123
  16.9 0.5 shard_map.124
  17.4 9.5 %all-to-all-done = f32[64,1,1536]{2,1,0:T(1,128)S(1)} async-done(((f32[64,1,1536]{2,1,0:T(1,128)}), f32[64,1,1536]{2,1,0:T(1,128)S(1)}, u32[]{:S(2)}, u32[]{:S(2)}) %all-to-all-start) | async-done | bytes 393248 | tf_op jit(solution)/shard_map/all_to_all | solution.py:580
  26.9 1.1 %shard_map.125 = (f32[512,128]{1,0:T(8,128)}, s32[128,128]{1,0:T(8,128)S(1)}, s32[128,128]{1,0:T(8,128)S(1)}) custom-call(f32[768,128]{1,0:T(8,128)S(1)} %bitcast.20, bf16[128,512]{1,0:T(8,128)(2,1)S(1)} %get-tuple-element.33.table, s32[32,128]{1,0:T(8,128)S(1)} %get-tuple-element.32.faces), custom_call_target="tpu_custom_call" | custom-call | tf_op jit(solution)/shard_map/pallas_call | solution.py:541
  28.0 4.6 %all-to-all-start.1 = ((f32[64,1,1024]{2,1,0:T(1,128)}), f32[64,1,1024]{2,1,0:T(1,128)S(1)}, u32[]{:S(2)}, u32[]{:S(2)}) async-start(f32[64,1,1024]{2,1,0:T(1,128)} %bitcast.26), calls=%async_computation.1 | async-start | bytes 524288 | tf_op jit(solution)/shard_map/all_to_all | solution.py:580
  32.7 1.0 %collective-permute-start = (f32[5,8,128]{2,1,0:T(8,128)S(1)}, f32[5,8,128]{2,1,0:T(8,128)S(1)}, u32[]{:S(2)}, u32[]{:S(2)}) collective-permute-start(f32[5,8,128]{2,1,0:T(8,128)S(1)} %get-tuple-element.43), channel_id=1, source_target_pairs={{0,8},{8,0},{16,24},{24,16},{32,40},{40,32},{48,56},{56,48},{64,72... | collective-permute-start | bytes 61448 | tf_op jit(solution)/shard_map/ppermute | solution.py:556
  33.7 4.3 %collective-permute-start.1 = (f32[5,8,128]{2,1,0:T(8,128)S(1)}, f32[5,8,128]{2,1,0:T(8,128)S(1)}, u32[]{:S(2)}, u32[]{:S(2)}) collective-permute-start(f32[5,8,128]{2,1,0:T(8,128)S(1)} %get-tuple-element.44), channel_id=1, source_target_pairs={{0,120},{8,16},{16,8},{24,32},{32,24},{40,48},{48,40},{56,64},{64,... | collective-permute-start | bytes 61448 | tf_op jit(solution)/shard_map/ppermute | solution.py:556
  37.9 0.0 collective-permute-done.x_first
  37.9 2.0 %collective-permute-done.1.x_second = f32[5,8,128]{2,1,0:T(8,128)S(1)} collective-permute-done((f32[5,8,128]{2,1,0:T(8,128)S(1)}, f32[5,8,128]{2,1,0:T(8,128)S(1)}, u32[]{:S(2)}, u32[]{:S(2)}) %collective-permute-start.1) | collective-permute-done | bytes 20512 | tf_op jit(solution)/shard_map/ppermute | solution.py:556
  40.0 3.8 %collective-permute-start.2 = (f32[5,6,8,128]{3,2,1,0:T(8,128)S(1)}, f32[5,6,8,128]{3,2,1,0:T(8,128)S(1)}, u32[]{:S(2)}, u32[]{:S(2)}) collective-permute-start(f32[5,6,8,128]{3,2,1,0:T(8,128)S(1)} %shard_map.127.near), channel_id=1, source_target_pairs={{0,1},{1,0},{2,3},{3,2},{4,5},{5,4},{6,7},{7,6},{8,9},{9,8},{10,11... | collective-permute-start | bytes 368648 | tf_op jit(solution)/shard_map/ppermute | solution.py:563
  43.8 1.0 %collective-permute-done.2.other = f32[5,6,8,128]{3,2,1,0:T(8,128)S(1)} collective-permute-done((f32[5,6,8,128]{3,2,1,0:T(8,128)S(1)}, f32[5,6,8,128]{3,2,1,0:T(8,128)S(1)}, u32[]{:S(2)}, u32[]{:S(2)}) %collective-permute-start.2) | collective-permute-done | bytes 122912 | tf_op jit(solution)/shard_map/ppermute | solution.py:563
  44.8 1.3 %collective-permute-start.3 = (f32[10,8,128]{2,1,0:T(8,128)S(1)}, f32[10,8,128]{2,1,0:T(8,128)S(1)}, u32[]{:S(2)}, u32[]{:S(2)}) collective-permute-start(f32[10,8,128]{2,1,0:T(8,128)S(1)} %get-tuple-element.45), channel_id=1, source_target_pairs={{0,2},{2,0},{4,6},{6,4},{1,3},{3,1},{5,7},{7,5},{8,10},{10,8},{12,... | collective-permute-start | bytes 122888 | tf_op jit(solution)/shard_map/ppermute | solution.py:556
  46.1 1.7 %collective-permute-start.4 = (f32[10,8,128]{2,1,0:T(8,128)S(1)}, f32[10,8,128]{2,1,0:T(8,128)S(1)}, u32[]{:S(2)}, u32[]{:S(2)}) collective-permute-start(f32[10,8,128]{2,1,0:T(8,128)S(1)} %get-tuple-element.46), channel_id=1, source_target_pairs={{0,6},{2,4},{4,2},{6,0},{1,7},{3,5},{5,3},{7,1},{8,14},{10,12},{12... | collective-permute-start | bytes 122888 | tf_op jit(solution)/shard_map/ppermute | solution.py:556
  47.8 0.0 collective-permute-done.3.y_low
  47.8 2.3 %collective-permute-done.4.y_high = f32[10,8,128]{2,1,0:T(8,128)S(1)} collective-permute-done((f32[10,8,128]{2,1,0:T(8,128)S(1)}, f32[10,8,128]{2,1,0:T(8,128)S(1)}, u32[]{:S(2)}, u32[]{:S(2)}) %collective-permute-start.4) | collective-permute-done | bytes 40992 | tf_op jit(solution)/shard_map/ppermute | solution.py:556
  50.1 0.4 shard_map.129
  50.5 3.0 %shard_map.126.reaction = f32[3,32,128]{2,1,0:T(8,128)S(1)} custom-call(f32[768,128]{1,0:T(8,128)S(1)} %bitcast.21, f32[512,128]{1,0:T(8,128)S(1)} %copy-done.1, s32[128,128]{1,0:T(8,128)S(1)} %get-tuple-element.39.face_row, s32[128,128]{1,0:T(8,128)S(1)} %get-tuple-element.40.face_lane, f32[3,32,128]{2,1,0:T(8,128)S(1)} %get-tuple-element.41.normals), custom_call_target="tpu_custom_call" | custom-call | tf_op jit(solution)/shard_map/pallas_call | solution.py:541
  53.5 1.9 %shard_map.130 = (f32[3,32,128]{2,1,0:T(8,128)S(1)}, f32[3,32,128]{2,1,0:T(8,128)S(1)}, f32[3,8,128]{2,1,0:T(8,128)S(1)}, f32[3,8,128]{2,1,0:T(8,128)S(1)}) custom-call(f32[512,128]{1,0:T(8,128)S(1)} %bitcast.27, f32[64,128]{1,0:T(8,128)S(1)} %get-tuple-element.35.slot_of, f32[3,64,128]{2,1,0:T(8,128)S(1)} %get-tuple-element.36.at_slaves, ...), custom_call_target="tpu_custom_call" | custom-call | tf_op jit(solution)/shard_map/pallas_call | solution.py:541
  55.4 3.0 %shard_map.133 = (f32[896,128]{1,0:T(8,128)}, f32[3,64,128]{2,1,0:T(8,128)S(1)}, f32[3,32,128]{2,1,0:T(8,128)S(1)}) custom-call(f32[3,32,128]{2,1,0:T(8,128)S(1)} %get-tuple-element.50.u, s32[64,128]{1,0:T(8,128)S(1)} %get-tuple-element.38.slaves, s32[32,128]{1,0:T(8,128)S(1)} %get-tuple-element.32.faces, f32[64,128]{1,0:T(8,128)S(1)} %get-tuple-element.35.slot_of, ...), custom_call_target="tpu_custom_call" | custom-call | tf_op jit(solution)/shard_map/pallas_call | solution.py:541
  58.4 8.1 %all-to-all-start.2 = ((f32[64,1,1792]{2,1,0:T(1,128)}), f32[64,1,1792]{2,1,0:T(1,128)S(1)}, u32[]{:S(2)}, u32[]{:S(2)}) async-start(f32[64,1,1792]{2,1,0:T(1,128)} %bitcast.24), calls=%async_computation.2 | async-start | bytes 917504 | tf_op jit(solution)/shard_map/all_to_all | solution.py:580
  66.4 1.1 %collective-permute-start.5 = (f32[3,8,128]{2,1,0:T(8,128)S(1)}, f32[3,8,128]{2,1,0:T(8,128)S(1)}, u32[]{:S(2)}, u32[]{:S(2)}) collective-permute-start(f32[3,8,128]{2,1,0:T(8,128)S(1)} %get-tuple-element.51), channel_id=1, source_target_pairs={{0,8},{8,0},{16,24},{24,16},{32,40},{40,32},{48,56},{56,48},{64,72... | collective-permute-start | bytes 36872 | tf_op jit(solution)/shard_map/ppermute | solution.py:556
  67.5 4.2 %collective-permute-start.6 = (f32[3,8,128]{2,1,0:T(8,128)S(1)}, f32[3,8,128]{2,1,0:T(8,128)S(1)}, u32[]{:S(2)}, u32[]{:S(2)}) collective-permute-start(f32[3,8,128]{2,1,0:T(8,128)S(1)} %get-tuple-element.52), channel_id=1, source_target_pairs={{0,120},{8,16},{16,8},{24,32},{32,24},{40,48},{48,40},{56,64},{64,... | collective-permute-start | bytes 36872 | tf_op jit(solution)/shard_map/ppermute | solution.py:556
  71.7 2.7 %collective-permute-done.6.x_second = f32[3,8,128]{2,1,0:T(8,128)S(1)} collective-permute-done((f32[3,8,128]{2,1,0:T(8,128)S(1)}, f32[3,8,128]{2,1,0:T(8,128)S(1)}, u32[]{:S(2)}, u32[]{:S(2)}) %collective-permute-start.6) | collective-permute-done | bytes 12320 | tf_op jit(solution)/shard_map/ppermute | solution.py:556
  74.4 1.6 %collective-permute-start.7 = (f32[3,8,128]{2,1,0:T(8,128)S(1)}, f32[3,8,128]{2,1,0:T(8,128)S(1)}, u32[]{:S(2)}, u32[]{:S(2)}) collective-permute-start(f32[3,8,128]{2,1,0:T(8,128)S(1)} %get-tuple-element.53), channel_id=1, source_target_pairs={{0,2},{2,0},{4,6},{6,4},{1,3},{3,1},{5,7},{7,5},{8,10},{10,8},{12,... | collective-permute-start | bytes 36872 | tf_op jit(solution)/shard_map/ppermute | solution.py:556
  75.9 1.6 %collective-permute-start.8 = (f32[3,8,128]{2,1,0:T(8,128)S(1)}, f32[3,8,128]{2,1,0:T(8,128)S(1)}, u32[]{:S(2)}, u32[]{:S(2)}) collective-permute-start(f32[3,8,128]{2,1,0:T(8,128)S(1)} %get-tuple-element.54), channel_id=1, source_target_pairs={{0,6},{2,4},{4,2},{6,0},{1,7},{3,5},{5,3},{7,1},{8,14},{10,12},{12... | collective-permute-start | bytes 36872 | tf_op jit(solution)/shard_map/ppermute | solution.py:556
  77.6 2.1 %collective-permute-done.8.y_second = f32[3,8,128]{2,1,0:T(8,128)S(1)} collective-permute-done((f32[3,8,128]{2,1,0:T(8,128)S(1)}, f32[3,8,128]{2,1,0:T(8,128)S(1)}, u32[]{:S(2)}, u32[]{:S(2)}) %collective-permute-start.8) | collective-permute-done | bytes 12320 | tf_op jit(solution)/shard_map/ppermute | solution.py:556
  79.7 4.5 %collective-permute-start.9 = (f32[3,6,16,128]{3,2,1,0:T(8,128)S(1)}, f32[3,6,16,128]{3,2,1,0:T(8,128)S(1)}, u32[]{:S(2)}, u32[]{:S(2)}) collective-permute-start(f32[3,6,16,128]{3,2,1,0:T(8,128)S(1)} %shard_map.132.near), channel_id=1, source_target_pairs={{0,1},{1,0},{2,3},{3,2},{4,5},{5,4},{6,7},{7,6},{8,9},{9,8},{10,11... | collective-permute-start | bytes 442376 | tf_op jit(solution)/shard_map/ppermute | solution.py:574
  84.3 4.7 %shard_map.134 = f32[3,32,128]{2,1,0:T(8,128)S(1)} custom-call(f32[896,128]{1,0:T(8,128)S(1)} %bitcast.25, f32[896,128]{1,0:T(8,128)S(1)} %copy-done, f32[768,128]{1,0:T(8,128)S(1)} %bitcast.23, s32[128,128]{1,0:T(8,128)S(1)} %get-tuple-element.39.face_row, s32[128,128]{1,0:T(8,128)S(1)} %get-tuple-element.40.face_lane, ...), custom_call_target="tpu_custom_call" | custom-call | tf_op jit(solution)/shard_map/pallas_call | solution.py:541
  89.1 1.0 %shard_map.135 = (f32[3,4,8,128]{3,2,1,0:T(8,128)}, f32[3,4,8,128]{3,2,1,0:T(8,128)}) custom-call(f32[3,6,16,128]{3,2,1,0:T(8,128)S(1)} %shard_map.132.near, f32[3,6,16,128]{3,2,1,0:T(8,128)S(1)} %collective-permute-done.9.other, f32[2,5,16,128]{3,2,1,0:T(8,128)S(1)} %get-tuple-element.55.moduli, f32[3,4,8,128]{3,2,1,0:T(8,128)S(1)} %bitcast.34, ...), custom_call_target="tpu_custom_call" | custom-call | tf_op jit(solution)/shard_map/pallas_call | solution.py:541
  (14 shorter events, 0.1 us)
Async XLA Ops:
  4.1 22.9 %all-to-all-start = ((f32[64,1,1536]{2,1,0:T(1,128)}), f32[64,1,1536]{2,1,0:T(1,128)S(1)}, u32[]{:S(2)}, u32[]{:S(2)}) async-start(f32[64,1,1536]{2,1,0:T(1,128)} %bitcast.38), calls=%async_computation | async-start | bytes 786432 | tf_op jit(solution)/shard_map/all_to_all | solution.py:580
  16.0 0.9 %copy-start.2 = (f32[3,4,8,128]{3,2,1,0:T(8,128)S(1)}, f32[3,4,8,128]{3,2,1,0:T(8,128)}, u32[]{:S(2)}) copy-start(f32[3,4,8,128]{3,2,1,0:T(8,128)} %disp.1) | copy-start | bytes 147460
  28.0 25.5 %all-to-all-start.1 = ((f32[64,1,1024]{2,1,0:T(1,128)}), f32[64,1,1024]{2,1,0:T(1,128)S(1)}, u32[]{:S(2)}, u32[]{:S(2)}) async-start(f32[64,1,1024]{2,1,0:T(1,128)} %bitcast.26), calls=%async_computation.1 | async-start | bytes 524288 | tf_op jit(solution)/shard_map/all_to_all | solution.py:580
  32.7 5.3 %collective-permute-start = (f32[5,8,128]{2,1,0:T(8,128)S(1)}, f32[5,8,128]{2,1,0:T(8,128)S(1)}, u32[]{:S(2)}, u32[]{:S(2)}) collective-permute-start(f32[5,8,128]{2,1,0:T(8,128)S(1)} %get-tuple-element.43), channel_id=1, source_target_pairs={{0,8},{8,0},{16,24},{24,16},{32,40},{40,32},{48,56},{56,48},{64,72... | collective-permute-start | bytes 61448 | tf_op jit(solution)/shard_map/ppermute | solution.py:556
  33.7 6.3 %collective-permute-start.1 = (f32[5,8,128]{2,1,0:T(8,128)S(1)}, f32[5,8,128]{2,1,0:T(8,128)S(1)}, u32[]{:S(2)}, u32[]{:S(2)}) collective-permute-start(f32[5,8,128]{2,1,0:T(8,128)S(1)} %get-tuple-element.44), channel_id=1, source_target_pairs={{0,120},{8,16},{16,8},{24,32},{32,24},{40,48},{48,40},{56,64},{64,... | collective-permute-start | bytes 61448 | tf_op jit(solution)/shard_map/ppermute | solution.py:556
  39.9 10.6 %copy-start.1 = (f32[512,128]{1,0:T(8,128)S(1)}, f32[512,128]{1,0:T(8,128)}, u32[]{:S(2)}) copy-start(f32[512,128]{1,0:T(8,128)} %get-tuple-element.34.frames) | copy-start | bytes 786436
  40.0 4.8 %collective-permute-start.2 = (f32[5,6,8,128]{3,2,1,0:T(8,128)S(1)}, f32[5,6,8,128]{3,2,1,0:T(8,128)S(1)}, u32[]{:S(2)}, u32[]{:S(2)}) collective-permute-start(f32[5,6,8,128]{3,2,1,0:T(8,128)S(1)} %shard_map.127.near), channel_id=1, source_target_pairs={{0,1},{1,0},{2,3},{3,2},{4,5},{5,4},{6,7},{7,6},{8,9},{9,8},{10,11... | collective-permute-start | bytes 368648 | tf_op jit(solution)/shard_map/ppermute | solution.py:563
  44.8 3.0 %collective-permute-start.3 = (f32[10,8,128]{2,1,0:T(8,128)S(1)}, f32[10,8,128]{2,1,0:T(8,128)S(1)}, u32[]{:S(2)}, u32[]{:S(2)}) collective-permute-start(f32[10,8,128]{2,1,0:T(8,128)S(1)} %get-tuple-element.45), channel_id=1, source_target_pairs={{0,2},{2,0},{4,6},{6,4},{1,3},{3,1},{5,7},{7,5},{8,10},{10,8},{12,... | collective-permute-start | bytes 122888 | tf_op jit(solution)/shard_map/ppermute | solution.py:556
  46.1 4.1 %collective-permute-start.4 = (f32[10,8,128]{2,1,0:T(8,128)S(1)}, f32[10,8,128]{2,1,0:T(8,128)S(1)}, u32[]{:S(2)}, u32[]{:S(2)}) collective-permute-start(f32[10,8,128]{2,1,0:T(8,128)S(1)} %get-tuple-element.46), channel_id=1, source_target_pairs={{0,6},{2,4},{4,2},{6,0},{1,7},{3,5},{5,3},{7,1},{8,14},{10,12},{12... | collective-permute-start | bytes 122888 | tf_op jit(solution)/shard_map/ppermute | solution.py:556
  58.4 25.9 %copy-start = (f32[896,128]{1,0:T(8,128)S(1)}, f32[896,128]{1,0:T(8,128)}, u32[]{:S(2)}) copy-start(f32[896,128]{1,0:T(8,128)} %get-tuple-element.56.sent) | copy-start | bytes 1376260
  58.4 25.9 %all-to-all-start.2 = ((f32[64,1,1792]{2,1,0:T(1,128)}), f32[64,1,1792]{2,1,0:T(1,128)S(1)}, u32[]{:S(2)}, u32[]{:S(2)}) async-start(f32[64,1,1792]{2,1,0:T(1,128)} %bitcast.24), calls=%async_computation.2 | async-start | bytes 917504 | tf_op jit(solution)/shard_map/all_to_all | solution.py:580
  66.4 5.3 %collective-permute-start.5 = (f32[3,8,128]{2,1,0:T(8,128)S(1)}, f32[3,8,128]{2,1,0:T(8,128)S(1)}, u32[]{:S(2)}, u32[]{:S(2)}) collective-permute-start(f32[3,8,128]{2,1,0:T(8,128)S(1)} %get-tuple-element.51), channel_id=1, source_target_pairs={{0,8},{8,0},{16,24},{24,16},{32,40},{40,32},{48,56},{56,48},{64,72... | collective-permute-start | bytes 36872 | tf_op jit(solution)/shard_map/ppermute | solution.py:556
  67.5 6.8 %collective-permute-start.6 = (f32[3,8,128]{2,1,0:T(8,128)S(1)}, f32[3,8,128]{2,1,0:T(8,128)S(1)}, u32[]{:S(2)}, u32[]{:S(2)}) collective-permute-start(f32[3,8,128]{2,1,0:T(8,128)S(1)} %get-tuple-element.52), channel_id=1, source_target_pairs={{0,120},{8,16},{16,8},{24,32},{32,24},{40,48},{48,40},{56,64},{64,... | collective-permute-start | bytes 36872 | tf_op jit(solution)/shard_map/ppermute | solution.py:556
  74.4 3.2 %collective-permute-start.7 = (f32[3,8,128]{2,1,0:T(8,128)S(1)}, f32[3,8,128]{2,1,0:T(8,128)S(1)}, u32[]{:S(2)}, u32[]{:S(2)}) collective-permute-start(f32[3,8,128]{2,1,0:T(8,128)S(1)} %get-tuple-element.53), channel_id=1, source_target_pairs={{0,2},{2,0},{4,6},{6,4},{1,3},{3,1},{5,7},{7,5},{8,10},{10,8},{12,... | collective-permute-start | bytes 36872 | tf_op jit(solution)/shard_map/ppermute | solution.py:556
  75.9 3.8 %collective-permute-start.8 = (f32[3,8,128]{2,1,0:T(8,128)S(1)}, f32[3,8,128]{2,1,0:T(8,128)S(1)}, u32[]{:S(2)}, u32[]{:S(2)}) collective-permute-start(f32[3,8,128]{2,1,0:T(8,128)S(1)} %get-tuple-element.54), channel_id=1, source_target_pairs={{0,6},{2,4},{4,2},{6,0},{1,7},{3,5},{5,3},{7,1},{8,14},{10,12},{12... | collective-permute-start | bytes 36872 | tf_op jit(solution)/shard_map/ppermute | solution.py:556
  79.7 9.3 %collective-permute-start.9 = (f32[3,6,16,128]{3,2,1,0:T(8,128)S(1)}, f32[3,6,16,128]{3,2,1,0:T(8,128)S(1)}, u32[]{:S(2)}, u32[]{:S(2)}) collective-permute-start(f32[3,6,16,128]{3,2,1,0:T(8,128)S(1)} %shard_map.132.near), channel_id=1, source_target_pairs={{0,1},{1,0},{2,3},{3,2},{4,5},{5,4},{6,7},{7,6},{8,9},{9,8},{10,11... | collective-permute-start | bytes 442376 | tf_op jit(solution)/shard_map/ppermute | solution.py:574

commit v4 on v3

--- a/solution.py
+++ b/solution.py
@@ -116,24 +116,27 @@
 def scatter_nodes(count, row_lane, forces_ref):
     pieces_count = forces_ref.shape[0]
     parts_count = pieces_count // 2
-    half = ROWS // 2
-    row_at = iota((half, PATCH), 0).astype(F32).astype(BF16)
-    lane_at = iota((2 * PATCH, PATCH), 0).astype(F32).astype(BF16)
-    none = jnp.zeros((half, PATCH), BF16)
+    size = 64
+    row_at = iota((ROWS, PATCH), 0).astype(F32).astype(BF16)
+    lane_at = iota((PATCH, PATCH), 0).astype(F32).astype(BF16)
+    none = jnp.zeros((ROWS, PATCH), BF16)
 
     def body(i, acc):
-        start = pl.multiple_of(i * 32, 32)
-        rows, lanes = row_lane(start)
-        lanes = (lanes + (rows >> 4) * PATCH).astype(F32)
-        rows = (rows & (half - 1)).astype(F32)
-        parts = [forces_ref[c, pl.ds(start, 32), :] for c in range(pieces_count)]
+        start = pl.multiple_of(i * size, size)
+        rows, lanes = row_lane(start, size)
+        rows = rows.astype(F32)
+        lanes = lanes.astype(F32)
+        parts = [forces_ref[c, pl.ds(start, size), :] for c in range(pieces_count)]
         left = []
         right = []
-        for q in range(32):
-            here = packed_row(rows, q) == row_at
-            pieces = [jnp.where(here, packed_row(part, q), none) for part in parts]
+        for q in range(size):
+            here = jnp.concatenate([packed_row(rows, q)] * 2, axis=0) == row_at
+            pieces = [
+                jnp.where(here, jnp.concatenate([packed_row(part, q)] * 2, axis=0), none)
+                for part in parts
+            ]
             left.append(jnp.concatenate(pieces, axis=0))
-            chosen = jnp.concatenate([packed_row(lanes, q)] * 16, axis=0) == lane_at
+            chosen = jnp.concatenate([packed_row(lanes, q)] * 8, axis=0) == lane_at
             right.append(jnp.where(chosen, jnp.ones_like(lane_at), jnp.zeros_like(lane_at)))
         left = jnp.concatenate(left, axis=1)
         right = jnp.concatenate(right, axis=1)
@@ -141,13 +144,9 @@
             left, right, (((1,), (1,)), ((), ())), preferred_element_type=F32
         )
 
-    acc = lax.fori_loop(0, count // 32, body, jnp.zeros((pieces_count * half, 2 * PATCH), F32))
-    acc = acc[0 : parts_count * half] + acc[parts_count * half : pieces_count * half]
-    out = []
-    for c in range(parts_count):
-        part = acc[c * half : (c + 1) * half]
-        out.append(jnp.concatenate([part[:, 0:PATCH], part[:, PATCH:]], axis=0))
-    return out
+    acc = lax.fori_loop(0, count // size, body, jnp.zeros((pieces_count * ROWS, PATCH), F32))
+    acc = acc[0 : parts_count * ROWS] + acc[parts_count * ROWS : pieces_count * ROWS]
+    return [acc[c * ROWS : (c + 1) * ROWS] for c in range(parts_count)]
 
 
 def store_parts(forces_ref, c, start, force):
@@ -418,11 +417,39 @@
         store_parts(scratch, 0, t * GROUPS, -0.25 * push)
 
 
+def scatter_faces(row_ref, lane_ref, push_ref, size):
+    row_at = iota((ROWS, PATCH), 0).astype(F32).astype(BF16)
+    lane_at = iota((PATCH, PATCH), 0).astype(F32).astype(BF16)
+    none = jnp.zeros((ROWS, PATCH), BF16)
+
+    def body(i, acc):
+        start = pl.multiple_of(i * size, size)
+        rows = row_ref[pl.ds(start, size), :].astype(F32)
+        lanes = lane_ref[pl.ds(start, size), :].astype(F32)
+        parts = [push_ref[c, pl.ds(start, size), :] for c in range(2)]
+        left = []
+        right = []
+        for q in range(size):
+            here = jnp.concatenate([packed_row(rows, q)] * 2, axis=0) == row_at
+            pieces = [
+                jnp.where(here, jnp.concatenate([packed_row(part, q)] * 2, axis=0), none)
+                for part in parts
+            ]
+            left.append(jnp.concatenate(pieces, axis=0))
+            chosen = jnp.concatenate([packed_row(lanes, q)] * 8, axis=0) == lane_at
+            right.append(jnp.where(chosen, jnp.ones_like(lane_at), jnp.zeros_like(lane_at)))
+        left = jnp.concatenate(left, axis=1)
+        right = jnp.concatenate(right, axis=1)
+        return acc + lax.dot_general(
+            left, right, (((1,), (1,)), ((), ())), preferred_element_type=F32
+        )
+
+    acc = lax.fori_loop(0, SLOTS // size, body, jnp.zeros((2 * ROWS, PATCH), F32))
+    return acc[0:ROWS] + acc[ROWS : 2 * ROWS]
+
+
 def face_contact(face_row, face_lane, normals, scratch):
-    def row_lane(start):
-        return face_row[pl.ds(start, 32), :], face_lane[pl.ds(start, 32), :]
-
-    (push,) = scatter_nodes(SLOTS, row_lane, scratch)
+    push = scatter_faces(face_row, face_lane, scratch, 128)
     out = []
     for c in range(3):
         x = jnp.where(push == 0.0, 0.0, push * normals[c])
@@ -445,8 +472,8 @@
     for c in range(3):
         store_parts(scratch, c, 0, push * frame[c])
 
-    def row_lane(start):
-        nodes = slaves[pl.ds(start, 32), :]
+    def row_lane(start, size):
+        nodes = slaves[pl.ds(start, size), :]
         return nodes >> 7, nodes & 127
 
     return scatter_nodes(PAIRS, row_lane, scratch)

time: 90.5 us -> 86.3 us (0.954)
  Pallas kernels: 19.9 us -> 15.7 us
    pallas_call x14, Pallas kernels: 19.9 us -> 15.7 us  [call(): pl.pallas_call(kernel, out_shape=outs, in_specs=[whole if i < raw else lo...]
  transfers between devices with their start and end apart: 13 -> 13, of which waited for: 6 -> 6; matrix products, arithmetic and copies ran while one was open for 0% -> 0% of each run, Pallas kernels for 11% -> 7%
where the time goes in v4:
time: 86.3 us; the launch traced here: 85.8 us
  starting transfers between devices  49.7 us (58%)
  waiting for transfers between devices  19.6 us (23%)
  Pallas kernels  15.7 us (18%)
    all_to_all x3, starting transfers between devices, exchange(): lax.all_to_all(chunk, ('len', 'wid'), split_axis=0, concat_axis=0, tiled=...  24.6 us
    ppermute x8, starting transfers between devices, swap_pair(): return (lax.ppermute(first, axis, mate), lax.ppermute(second, axis, other))  16.7 us
    pallas_call x14, Pallas kernels, call(): pl.pallas_call(kernel, out_shape=outs, in_specs=[whole if i < raw else lo...  15.7 us
    all_to_all x3, waiting for transfers between devices, exchange(): lax.all_to_all(chunk, ('len', 'wid'), split_axis=0, concat_axis=0, tiled=...  9.53 us
    ppermute x8, waiting for transfers between devices, swap_pair(): return (lax.ppermute(first, axis, mate), lax.ppermute(second, axis, other))  9.13 us
    ppermute x1, starting transfers between devices, extended(): other = lax.ppermute(near, 'lay', [(0, 1), (1, 0)])  4.56 us
    ppermute x1, starting transfers between devices, surroundings(): other = lax.ppermute(near, 'lay', [(0, 1), (1, 0)])  3.83 us
  transfers between devices with their start and end apart: 13, of which 6 were waited for; matrix products, arithmetic and copies ran while one was open for 0% of the time, Pallas kernels for 7%

profile of v4, /device:TPU:1, one launch (start us, length us, event | category | flops | bytes accessed | tf_op | source)
XLA Modules:
  0.0 85.8 jit_solution(7817000032624282806)
XLA Ops:
  0.6 3.4 %shard_map.122 = (f32[768,128]{1,0:T(8,128)}, f32[64,128]{1,0:T(8,128)S(1)}, f32[3,64,128]{2,1,0:T(8,128)S(1)}, s32[64,128]{1,0:T(8,128)S(1)}, f32[64,128]{1,0:T(8,128)S(1)}) custom-call(f32[3,32,128]{2,1,0:T(8,128)} %bitcast.31, s32[64,128]{1,0:T(8,128)} %bitcast.40, f32[64,128]{1,0:T(8,128)} %bitcast.41, s32[64,128]{1,0:T(8,128)} %bitcast.42, ...), custom_call_target="tpu_custom_call" | custom-call | tf_op jit(solution)/shard_map/pallas_call | solution.py:568
  4.1 12.0 %all-to-all-start = ((f32[64,1,1536]{2,1,0:T(1,128)}), f32[64,1,1536]{2,1,0:T(1,128)S(1)}, u32[]{:S(2)}, u32[]{:S(2)}) async-start(f32[64,1,1536]{2,1,0:T(1,128)} %bitcast.38), calls=%async_computation | async-start | bytes 786432 | tf_op jit(solution)/shard_map/all_to_all | solution.py:607
  16.0 0.0 copy-start.2
  16.0 0.9 %shard_map.123 = (f32[5,4,8,128]{3,2,1,0:T(8,128)S(1)}, f32[5,8,128]{2,1,0:T(8,128)S(1)}, f32[5,8,128]{2,1,0:T(8,128)S(1)}, f32[3,32,128]{2,1,0:T(8,128)S(1)}, f...) custom-call(f32[3,4,8,128]{3,2,1,0:T(8,128)} %disp.1, f32[4,8,128]{2,1,0:T(8,128)} %lame.1, f32[4,8,128]{2,1,0:T(8,128)} %shear.1, ...), custom_call_target="tpu_custom_call" | custom-call | tf_op jit(solution)/shard_map/pallas_call | solution.py:568
  16.9 0.5 shard_map.124
  17.4 9.5 %all-to-all-done = f32[64,1,1536]{2,1,0:T(1,128)S(1)} async-done(((f32[64,1,1536]{2,1,0:T(1,128)}), f32[64,1,1536]{2,1,0:T(1,128)S(1)}, u32[]{:S(2)}, u32[]{:S(2)}) %all-to-all-start) | async-done | bytes 393248 | tf_op jit(solution)/shard_map/all_to_all | solution.py:607
  26.9 1.1 %shard_map.125 = (f32[512,128]{1,0:T(8,128)}, s32[128,128]{1,0:T(8,128)S(1)}, s32[128,128]{1,0:T(8,128)S(1)}) custom-call(f32[768,128]{1,0:T(8,128)S(1)} %bitcast.20, bf16[128,512]{1,0:T(8,128)(2,1)S(1)} %get-tuple-element.33.table, s32[32,128]{1,0:T(8,128)S(1)} %get-tuple-element.32.faces), custom_call_target="tpu_custom_call" | custom-call | tf_op jit(solution)/shard_map/pallas_call | solution.py:568
  28.0 4.6 %all-to-all-start.1 = ((f32[64,1,1024]{2,1,0:T(1,128)}), f32[64,1,1024]{2,1,0:T(1,128)S(1)}, u32[]{:S(2)}, u32[]{:S(2)}) async-start(f32[64,1,1024]{2,1,0:T(1,128)} %bitcast.26), calls=%async_computation.1 | async-start | bytes 524288 | tf_op jit(solution)/shard_map/all_to_all | solution.py:607
  32.7 1.0 %collective-permute-start = (f32[5,8,128]{2,1,0:T(8,128)S(1)}, f32[5,8,128]{2,1,0:T(8,128)S(1)}, u32[]{:S(2)}, u32[]{:S(2)}) collective-permute-start(f32[5,8,128]{2,1,0:T(8,128)S(1)} %get-tuple-element.43), channel_id=1, source_target_pairs={{0,8},{8,0},{16,24},{24,16},{32,40},{40,32},{48,56},{56,48},{64,72... | collective-permute-start | bytes 61448 | tf_op jit(solution)/shard_map/ppermute | solution.py:583
  33.7 4.3 %collective-permute-start.1 = (f32[5,8,128]{2,1,0:T(8,128)S(1)}, f32[5,8,128]{2,1,0:T(8,128)S(1)}, u32[]{:S(2)}, u32[]{:S(2)}) collective-permute-start(f32[5,8,128]{2,1,0:T(8,128)S(1)} %get-tuple-element.44), channel_id=1, source_target_pairs={{0,120},{8,16},{16,8},{24,32},{32,24},{40,48},{48,40},{56,64},{64,... | collective-permute-start | bytes 61448 | tf_op jit(solution)/shard_map/ppermute | solution.py:583
  37.9 0.0 collective-permute-done.x_first
  37.9 2.0 %collective-permute-done.1.x_second = f32[5,8,128]{2,1,0:T(8,128)S(1)} collective-permute-done((f32[5,8,128]{2,1,0:T(8,128)S(1)}, f32[5,8,128]{2,1,0:T(8,128)S(1)}, u32[]{:S(2)}, u32[]{:S(2)}) %collective-permute-start.1) | collective-permute-done | bytes 20512 | tf_op jit(solution)/shard_map/ppermute | solution.py:583
  40.0 3.8 %collective-permute-start.2 = (f32[5,6,8,128]{3,2,1,0:T(8,128)S(1)}, f32[5,6,8,128]{3,2,1,0:T(8,128)S(1)}, u32[]{:S(2)}, u32[]{:S(2)}) collective-permute-start(f32[5,6,8,128]{3,2,1,0:T(8,128)S(1)} %shard_map.127.near), channel_id=1, source_target_pairs={{0,1},{1,0},{2,3},{3,2},{4,5},{5,4},{6,7},{7,6},{8,9},{9,8},{10,11... | collective-permute-start | bytes 368648 | tf_op jit(solution)/shard_map/ppermute | solution.py:590
  43.8 1.0 %collective-permute-done.2.other = f32[5,6,8,128]{3,2,1,0:T(8,128)S(1)} collective-permute-done((f32[5,6,8,128]{3,2,1,0:T(8,128)S(1)}, f32[5,6,8,128]{3,2,1,0:T(8,128)S(1)}, u32[]{:S(2)}, u32[]{:S(2)}) %collective-permute-start.2) | collective-permute-done | bytes 122912 | tf_op jit(solution)/shard_map/ppermute | solution.py:590
  44.8 1.3 %collective-permute-start.3 = (f32[10,8,128]{2,1,0:T(8,128)S(1)}, f32[10,8,128]{2,1,0:T(8,128)S(1)}, u32[]{:S(2)}, u32[]{:S(2)}) collective-permute-start(f32[10,8,128]{2,1,0:T(8,128)S(1)} %get-tuple-element.45), channel_id=1, source_target_pairs={{0,2},{2,0},{4,6},{6,4},{1,3},{3,1},{5,7},{7,5},{8,10},{10,8},{12,... | collective-permute-start | bytes 122888 | tf_op jit(solution)/shard_map/ppermute | solution.py:583
  46.1 1.7 %collective-permute-start.4 = (f32[10,8,128]{2,1,0:T(8,128)S(1)}, f32[10,8,128]{2,1,0:T(8,128)S(1)}, u32[]{:S(2)}, u32[]{:S(2)}) collective-permute-start(f32[10,8,128]{2,1,0:T(8,128)S(1)} %get-tuple-element.46), channel_id=1, source_target_pairs={{0,6},{2,4},{4,2},{6,0},{1,7},{3,5},{5,3},{7,1},{8,14},{10,12},{12... | collective-permute-start | bytes 122888 | tf_op jit(solution)/shard_map/ppermute | solution.py:583
  47.8 0.0 collective-permute-done.3.y_low
  47.8 2.3 %collective-permute-done.4.y_high = f32[10,8,128]{2,1,0:T(8,128)S(1)} collective-permute-done((f32[10,8,128]{2,1,0:T(8,128)S(1)}, f32[10,8,128]{2,1,0:T(8,128)S(1)}, u32[]{:S(2)}, u32[]{:S(2)}) %collective-permute-start.4) | collective-permute-done | bytes 40992 | tf_op jit(solution)/shard_map/ppermute | solution.py:583
  50.1 0.4 shard_map.129
  50.5 1.6 %shard_map.126.reaction = f32[3,32,128]{2,1,0:T(8,128)S(1)} custom-call(f32[768,128]{1,0:T(8,128)S(1)} %bitcast.21, f32[512,128]{1,0:T(8,128)S(1)} %copy-done.1, s32[128,128]{1,0:T(8,128)S(1)} %get-tuple-element.39.face_row, s32[128,128]{1,0:T(8,128)S(1)} %get-tuple-element.40.face_lane, f32[3,32,128]{2,1,0:T(8,128)S(1)} %get-tuple-element.41.normals), custom_call_target="tpu_custom_call" | custom-call | tf_op jit(solution)/shard_map/pallas_call | solution.py:568
  52.1 1.2 %shard_map.130 = (f32[3,32,128]{2,1,0:T(8,128)S(1)}, f32[3,32,128]{2,1,0:T(8,128)S(1)}, f32[3,8,128]{2,1,0:T(8,128)S(1)}, f32[3,8,128]{2,1,0:T(8,128)S(1)}) custom-call(f32[512,128]{1,0:T(8,128)S(1)} %bitcast.27, f32[64,128]{1,0:T(8,128)S(1)} %get-tuple-element.35.slot_of, f32[3,64,128]{2,1,0:T(8,128)S(1)} %get-tuple-element.36.at_slaves, ...), custom_call_target="tpu_custom_call" | custom-call | tf_op jit(solution)/shard_map/pallas_call | solution.py:568
  53.3 3.0 %shard_map.133 = (f32[896,128]{1,0:T(8,128)}, f32[3,64,128]{2,1,0:T(8,128)S(1)}, f32[3,32,128]{2,1,0:T(8,128)S(1)}) custom-call(f32[3,32,128]{2,1,0:T(8,128)S(1)} %get-tuple-element.50.u, s32[64,128]{1,0:T(8,128)S(1)} %get-tuple-element.38.slaves, s32[32,128]{1,0:T(8,128)S(1)} %get-tuple-element.32.faces, f32[64,128]{1,0:T(8,128)S(1)} %get-tuple-element.35.slot_of, ...), custom_call_target="tpu_custom_call" | custom-call | tf_op jit(solution)/shard_map/pallas_call | solution.py:568
  56.3 8.0 %all-to-all-start.2 = ((f32[64,1,1792]{2,1,0:T(1,128)}), f32[64,1,1792]{2,1,0:T(1,128)S(1)}, u32[]{:S(2)}, u32[]{:S(2)}) async-start(f32[64,1,1792]{2,1,0:T(1,128)} %bitcast.24), calls=%async_computation.2 | async-start | bytes 917504 | tf_op jit(solution)/shard_map/all_to_all | solution.py:607
  64.4 1.1 %collective-permute-start.5 = (f32[3,8,128]{2,1,0:T(8,128)S(1)}, f32[3,8,128]{2,1,0:T(8,128)S(1)}, u32[]{:S(2)}, u32[]{:S(2)}) collective-permute-start(f32[3,8,128]{2,1,0:T(8,128)S(1)} %get-tuple-element.51), channel_id=1, source_target_pairs={{0,8},{8,0},{16,24},{24,16},{32,40},{40,32},{48,56},{56,48},{64,72... | collective-permute-start | bytes 36872 | tf_op jit(solution)/shard_map/ppermute | solution.py:583
  65.5 4.2 %collective-permute-start.6 = (f32[3,8,128]{2,1,0:T(8,128)S(1)}, f32[3,8,128]{2,1,0:T(8,128)S(1)}, u32[]{:S(2)}, u32[]{:S(2)}) collective-permute-start(f32[3,8,128]{2,1,0:T(8,128)S(1)} %get-tuple-element.52), channel_id=1, source_target_pairs={{0,120},{8,16},{16,8},{24,32},{32,24},{40,48},{48,40},{56,64},{64,... | collective-permute-start | bytes 36872 | tf_op jit(solution)/shard_map/ppermute | solution.py:583
  69.7 2.7 %collective-permute-done.6.x_second = f32[3,8,128]{2,1,0:T(8,128)S(1)} collective-permute-done((f32[3,8,128]{2,1,0:T(8,128)S(1)}, f32[3,8,128]{2,1,0:T(8,128)S(1)}, u32[]{:S(2)}, u32[]{:S(2)}) %collective-permute-start.6) | collective-permute-done | bytes 12320 | tf_op jit(solution)/shard_map/ppermute | solution.py:583
  72.3 1.6 %collective-permute-start.7 = (f32[3,8,128]{2,1,0:T(8,128)S(1)}, f32[3,8,128]{2,1,0:T(8,128)S(1)}, u32[]{:S(2)}, u32[]{:S(2)}) collective-permute-start(f32[3,8,128]{2,1,0:T(8,128)S(1)} %get-tuple-element.53), channel_id=1, source_target_pairs={{0,2},{2,0},{4,6},{6,4},{1,3},{3,1},{5,7},{7,5},{8,10},{10,8},{12,... | collective-permute-start | bytes 36872 | tf_op jit(solution)/shard_map/ppermute | solution.py:583
  73.9 1.6 %collective-permute-start.8 = (f32[3,8,128]{2,1,0:T(8,128)S(1)}, f32[3,8,128]{2,1,0:T(8,128)S(1)}, u32[]{:S(2)}, u32[]{:S(2)}) collective-permute-start(f32[3,8,128]{2,1,0:T(8,128)S(1)} %get-tuple-element.54), channel_id=1, source_target_pairs={{0,6},{2,4},{4,2},{6,0},{1,7},{3,5},{5,3},{7,1},{8,14},{10,12},{12... | collective-permute-start | bytes 36872 | tf_op jit(solution)/shard_map/ppermute | solution.py:583
  75.6 2.1 %collective-permute-done.8.y_second = f32[3,8,128]{2,1,0:T(8,128)S(1)} collective-permute-done((f32[3,8,128]{2,1,0:T(8,128)S(1)}, f32[3,8,128]{2,1,0:T(8,128)S(1)}, u32[]{:S(2)}, u32[]{:S(2)}) %collective-permute-start.8) | collective-permute-done | bytes 12320 | tf_op jit(solution)/shard_map/ppermute | solution.py:583
  77.7 4.6 %collective-permute-start.9 = (f32[3,6,16,128]{3,2,1,0:T(8,128)S(1)}, f32[3,6,16,128]{3,2,1,0:T(8,128)S(1)}, u32[]{:S(2)}, u32[]{:S(2)}) collective-permute-start(f32[3,6,16,128]{3,2,1,0:T(8,128)S(1)} %shard_map.132.near), channel_id=1, source_target_pairs={{0,1},{1,0},{2,3},{3,2},{4,5},{5,4},{6,7},{7,6},{8,9},{9,8},{10,11... | collective-permute-start | bytes 442376 | tf_op jit(solution)/shard_map/ppermute | solution.py:601
  82.3 2.5 %shard_map.134 = f32[3,32,128]{2,1,0:T(8,128)S(1)} custom-call(f32[896,128]{1,0:T(8,128)S(1)} %bitcast.25, f32[896,128]{1,0:T(8,128)S(1)} %copy-done, f32[768,128]{1,0:T(8,128)S(1)} %bitcast.23, s32[128,128]{1,0:T(8,128)S(1)} %get-tuple-element.39.face_row, s32[128,128]{1,0:T(8,128)S(1)} %get-tuple-element.40.face_lane, ...), custom_call_target="tpu_custom_call" | custom-call | tf_op jit(solution)/shard_map/pallas_call | solution.py:568
  84.8 1.0 %shard_map.135 = (f32[3,4,8,128]{3,2,1,0:T(8,128)}, f32[3,4,8,128]{3,2,1,0:T(8,128)}) custom-call(f32[3,6,16,128]{3,2,1,0:T(8,128)S(1)} %shard_map.132.near, f32[3,6,16,128]{3,2,1,0:T(8,128)S(1)} %collective-permute-done.9.other, f32[2,5,16,128]{3,2,1,0:T(8,128)S(1)} %get-tuple-element.55.moduli, f32[3,4,8,128]{3,2,1,0:T(8,128)S(1)} %bitcast.34, ...), custom_call_target="tpu_custom_call" | custom-call | tf_op jit(solution)/shard_map/pallas_call | solution.py:568
  (14 shorter events, 0.1 us)
Async XLA Ops:
  4.1 22.9 %all-to-all-start = ((f32[64,1,1536]{2,1,0:T(1,128)}), f32[64,1,1536]{2,1,0:T(1,128)S(1)}, u32[]{:S(2)}, u32[]{:S(2)}) async-start(f32[64,1,1536]{2,1,0:T(1,128)} %bitcast.38), calls=%async_computation | async-start | bytes 786432 | tf_op jit(solution)/shard_map/all_to_all | solution.py:607
  16.0 0.9 %copy-start.2 = (f32[3,4,8,128]{3,2,1,0:T(8,128)S(1)}, f32[3,4,8,128]{3,2,1,0:T(8,128)}, u32[]{:S(2)}) copy-start(f32[3,4,8,128]{3,2,1,0:T(8,128)} %disp.1) | copy-start | bytes 147460
  28.0 24.1 %all-to-all-start.1 = ((f32[64,1,1024]{2,1,0:T(1,128)}), f32[64,1,1024]{2,1,0:T(1,128)S(1)}, u32[]{:S(2)}, u32[]{:S(2)}) async-start(f32[64,1,1024]{2,1,0:T(1,128)} %bitcast.26), calls=%async_computation.1 | async-start | bytes 524288 | tf_op jit(solution)/shard_map/all_to_all | solution.py:607
  32.7 5.3 %collective-permute-start = (f32[5,8,128]{2,1,0:T(8,128)S(1)}, f32[5,8,128]{2,1,0:T(8,128)S(1)}, u32[]{:S(2)}, u32[]{:S(2)}) collective-permute-start(f32[5,8,128]{2,1,0:T(8,128)S(1)} %get-tuple-element.43), channel_id=1, source_target_pairs={{0,8},{8,0},{16,24},{24,16},{32,40},{40,32},{48,56},{56,48},{64,72... | collective-permute-start | bytes 61448 | tf_op jit(solution)/shard_map/ppermute | solution.py:583
  33.7 6.3 %collective-permute-start.1 = (f32[5,8,128]{2,1,0:T(8,128)S(1)}, f32[5,8,128]{2,1,0:T(8,128)S(1)}, u32[]{:S(2)}, u32[]{:S(2)}) collective-permute-start(f32[5,8,128]{2,1,0:T(8,128)S(1)} %get-tuple-element.44), channel_id=1, source_target_pairs={{0,120},{8,16},{16,8},{24,32},{32,24},{40,48},{48,40},{56,64},{64,... | collective-permute-start | bytes 61448 | tf_op jit(solution)/shard_map/ppermute | solution.py:583
  39.9 10.6 %copy-start.1 = (f32[512,128]{1,0:T(8,128)S(1)}, f32[512,128]{1,0:T(8,128)}, u32[]{:S(2)}) copy-start(f32[512,128]{1,0:T(8,128)} %get-tuple-element.34.frames) | copy-start | bytes 786436
  40.0 4.8 %collective-permute-start.2 = (f32[5,6,8,128]{3,2,1,0:T(8,128)S(1)}, f32[5,6,8,128]{3,2,1,0:T(8,128)S(1)}, u32[]{:S(2)}, u32[]{:S(2)}) collective-permute-start(f32[5,6,8,128]{3,2,1,0:T(8,128)S(1)} %shard_map.127.near), channel_id=1, source_target_pairs={{0,1},{1,0},{2,3},{3,2},{4,5},{5,4},{6,7},{7,6},{8,9},{9,8},{10,11... | collective-permute-start | bytes 368648 | tf_op jit(solution)/shard_map/ppermute | solution.py:590
  44.8 3.0 %collective-permute-start.3 = (f32[10,8,128]{2,1,0:T(8,128)S(1)}, f32[10,8,128]{2,1,0:T(8,128)S(1)}, u32[]{:S(2)}, u32[]{:S(2)}) collective-permute-start(f32[10,8,128]{2,1,0:T(8,128)S(1)} %get-tuple-element.45), channel_id=1, source_target_pairs={{0,2},{2,0},{4,6},{6,4},{1,3},{3,1},{5,7},{7,5},{8,10},{10,8},{12,... | collective-permute-start | bytes 122888 | tf_op jit(solution)/shard_map/ppermute | solution.py:583
  46.1 4.1 %collective-permute-start.4 = (f32[10,8,128]{2,1,0:T(8,128)S(1)}, f32[10,8,128]{2,1,0:T(8,128)S(1)}, u32[]{:S(2)}, u32[]{:S(2)}) collective-permute-start(f32[10,8,128]{2,1,0:T(8,128)S(1)} %get-tuple-element.46), channel_id=1, source_target_pairs={{0,6},{2,4},{4,2},{6,0},{1,7},{3,5},{5,3},{7,1},{8,14},{10,12},{12... | collective-permute-start | bytes 122888 | tf_op jit(solution)/shard_map/ppermute | solution.py:583
  56.3 25.9 %copy-start = (f32[896,128]{1,0:T(8,128)S(1)}, f32[896,128]{1,0:T(8,128)}, u32[]{:S(2)}) copy-start(f32[896,128]{1,0:T(8,128)} %get-tuple-element.56.sent) | copy-start | bytes 1376260
  56.3 25.9 %all-to-all-start.2 = ((f32[64,1,1792]{2,1,0:T(1,128)}), f32[64,1,1792]{2,1,0:T(1,128)S(1)}, u32[]{:S(2)}, u32[]{:S(2)}) async-start(f32[64,1,1792]{2,1,0:T(1,128)} %bitcast.24), calls=%async_computation.2 | async-start | bytes 917504 | tf_op jit(solution)/shard_map/all_to_all | solution.py:607
  64.4 5.3 %collective-permute-start.5 = (f32[3,8,128]{2,1,0:T(8,128)S(1)}, f32[3,8,128]{2,1,0:T(8,128)S(1)}, u32[]{:S(2)}, u32[]{:S(2)}) collective-permute-start(f32[3,8,128]{2,1,0:T(8,128)S(1)} %get-tuple-element.51), channel_id=1, source_target_pairs={{0,8},{8,0},{16,24},{24,16},{32,40},{40,32},{48,56},{56,48},{64,72... | collective-permute-start | bytes 36872 | tf_op jit(solution)/shard_map/ppermute | solution.py:583
  65.5 6.8 %collective-permute-start.6 = (f32[3,8,128]{2,1,0:T(8,128)S(1)}, f32[3,8,128]{2,1,0:T(8,128)S(1)}, u32[]{:S(2)}, u32[]{:S(2)}) collective-permute-start(f32[3,8,128]{2,1,0:T(8,128)S(1)} %get-tuple-element.52), channel_id=1, source_target_pairs={{0,120},{8,16},{16,8},{24,32},{32,24},{40,48},{48,40},{56,64},{64,... | collective-permute-start | bytes 36872 | tf_op jit(solution)/shard_map/ppermute | solution.py:583
  72.3 3.2 %collective-permute-start.7 = (f32[3,8,128]{2,1,0:T(8,128)S(1)}, f32[3,8,128]{2,1,0:T(8,128)S(1)}, u32[]{:S(2)}, u32[]{:S(2)}) collective-permute-start(f32[3,8,128]{2,1,0:T(8,128)S(1)} %get-tuple-element.53), channel_id=1, source_target_pairs={{0,2},{2,0},{4,6},{6,4},{1,3},{3,1},{5,7},{7,5},{8,10},{10,8},{12,... | collective-permute-start | bytes 36872 | tf_op jit(solution)/shard_map/ppermute | solution.py:583
  73.9 3.8 %collective-permute-start.8 = (f32[3,8,128]{2,1,0:T(8,128)S(1)}, f32[3,8,128]{2,1,0:T(8,128)S(1)}, u32[]{:S(2)}, u32[]{:S(2)}) collective-permute-start(f32[3,8,128]{2,1,0:T(8,128)S(1)} %get-tuple-element.54), channel_id=1, source_target_pairs={{0,6},{2,4},{4,2},{6,0},{1,7},{3,5},{5,3},{7,1},{8,14},{10,12},{12... | collective-permute-start | bytes 36872 | tf_op jit(solution)/shard_map/ppermute | solution.py:583
  77.7 7.1 %collective-permute-start.9 = (f32[3,6,16,128]{3,2,1,0:T(8,128)S(1)}, f32[3,6,16,128]{3,2,1,0:T(8,128)S(1)}, u32[]{:S(2)}, u32[]{:S(2)}) collective-permute-start(f32[3,6,16,128]{3,2,1,0:T(8,128)S(1)} %shard_map.132.near), channel_id=1, source_target_pairs={{0,1},{1,0},{2,3},{3,2},{4,5},{5,4},{6,7},{7,6},{8,9},{9,8},{10,11... | collective-permute-start | bytes 442376 | tf_op jit(solution)/shard_map/ppermute | solution.py:601

commit v5 on v4

--- a/solution.py
+++ b/solution.py
@@ -41,14 +41,15 @@
 
 def select_dot(onehot, x):
     high, mid, low = parts_3(x)
-    out = jnp.dot(onehot, low, preferred_element_type=F32)
-    out = out + jnp.dot(onehot, mid, preferred_element_type=F32)
-    return out + jnp.dot(onehot, high, preferred_element_type=F32)
-
-
-def gather_nodes(u_ref, slaves, out_ref):
-    def body(i, carry):
-        start = pl.multiple_of(i * 8, 8)
+    return jnp.dot(
+        jnp.concatenate([onehot] * 3, axis=1),
+        jnp.concatenate([low, mid, high], axis=0),
+        preferred_element_type=F32,
+    )
+
+
+def gather_flat(u_ref, slaves, out_ref):
+    for start in range(0, PAIRS, 8):
         nodes = slaves[pl.ds(start, 8), :]
         row = nodes >> 7
         lane = nodes & 127
@@ -60,9 +61,6 @@
                 out[c] = jnp.where(here, lane_pick(source, lane), out[c])
         for c in range(3):
             out_ref[c, pl.ds(start, 8), :] = out[c]
-        return carry
-
-    lax.fori_loop(0, PAIRS // 8, body, 0)
 
 
 def up(x, amount):
@@ -351,7 +349,7 @@
 
 
 def request_kernel(
-    u, slaves, gaps, chosen, owners, wanted, send, slot_of, at_slaves, slaves_out, gaps_out
+    u, slaves, gaps, chosen, owners, wanted, send, slot_of, place_out, at_slaves, slaves_out, gaps_out
 ):
     slaves_out[...] = slaves[...]
     gaps_out[...] = gaps[...]
@@ -363,7 +361,8 @@
     slot_row = column_to_row(slot)
     slot_of[...] = jnp.where(slot == iota((PAIRS, SLOTS), 1).astype(F32), 1.0, 0.0)
     place = jnp.where(slot_row == iota((SLOTS, PAIRS), 0).astype(F32), 1.0, 0.0).astype(BF16)
-    gather_nodes(u, slaves, at_slaves)
+    place_out[...] = place
+    gather_flat(u, slaves, at_slaves)
     values = [at_slaves[c] for c in range(3)]
     exact = jnp.concatenate(values + [gaps[...]], axis=1)
     moved = select_dot(place, exact)
@@ -392,8 +391,10 @@
     table[...] = patch_table(u, faces[...], normals)
 
 
-def reply_kernel(arrived, table, faces, send, face_row, face_lane):
+def reply_kernel(arrived, table, faces, send, face_row, face_lane, patch_of, cand_of):
     onehot, cand = wanted_rows(arrived)
+    patch_of[...] = onehot
+    cand_of[...] = cand
     tiles = jnp.dot(onehot, table[...], preferred_element_type=F32)
     for c in range(4):
         picked = lane_pick(tiles[:, c * 128 : (c + 1) * 128], cand)
@@ -504,18 +505,13 @@
         store_faces("len", first, second, c, place[0:NJ], place[ROWS - NJ : ROWS])
 
 
-def second_kernel(u, slaves, faces, slot_of, arrived, send, at_slaves, normals):
-    gather_nodes(u, slaves, at_slaves)
+def second_kernel(u, slaves, faces, place, patch_of, cand_of, send, at_slaves, normals):
+    gather_flat(u, slaves, at_slaves)
     values = [at_slaves[c] for c in range(3)]
-    place = slot_of[...].astype(BF16)
-    high, mid, low = parts_3(jnp.concatenate(values, axis=1))
-    dims = (((0,), (0,)), ((), ()))
-    moved = lax.dot_general(place, low, dims, preferred_element_type=F32)
-    moved = moved + lax.dot_general(place, mid, dims, preferred_element_type=F32)
-    moved = moved + lax.dot_general(place, high, dims, preferred_element_type=F32)
+    moved = select_dot(place[...], jnp.concatenate(values, axis=1))
     table = patch_table(u, faces[...], normals)
-    onehot, cand = wanted_rows(arrived)
-    tiles = jnp.dot(onehot, table, preferred_element_type=F32)
+    cand = cand_of[...]
+    tiles = jnp.dot(patch_of[...], table, preferred_element_type=F32)
     for t in range(CAP):
         part = slice(t * GROUPS, (t + 1) * GROUPS)
         for c in range(3):
@@ -630,10 +626,11 @@
         displacement, lame_first, shear_modulus, v, mass, faces, raw=6,
     )
     around = surroundings(five, low, high)
-    send, slot_of, at_slaves, slaves, gaps = call(
+    send, slot_of, place, at_slaves, slaves, gaps = call(
         request_kernel,
         (
-            plain(GROUPS * 12, PATCH), f32(PAIRS, SLOTS), f32(3, PAIRS, PATCH),
+            plain(GROUPS * 12, PATCH), f32(PAIRS, SLOTS), pltpu.VMEM((SLOTS, PAIRS), BF16),
+            f32(3, PAIRS, PATCH),
             i32(PAIRS, PATCH), f32(PAIRS, PATCH),
         ),
         u, slaves, gaps, chosen, owners, wanted, raw=6,
@@ -642,9 +639,12 @@
     table, normals = call(
         table_kernel, (pltpu.VMEM((128, 512), BF16), f32(3, ROWS, NK)), u, faces
     )
-    reply, face_row, face_lane = call(
+    reply, face_row, face_lane, patch_of, cand_of = call(
         reply_kernel,
-        (plain(GROUPS * 8, PATCH), i32(SLOTS, PATCH), i32(SLOTS, PATCH)),
+        (
+            plain(GROUPS * 8, PATCH), i32(SLOTS, PATCH), i32(SLOTS, PATCH),
+            pltpu.VMEM((SLOTS, PATCH), BF16), i32(SLOTS, PATCH),
+        ),
         first, table, faces,
     )
     arrived = exchange(reply)
@@ -667,7 +667,7 @@
     sent, at_slaves, next_normals = call(
         second_kernel,
         (plain(GROUPS * 14, PATCH), f32(3, PAIRS, PATCH), f32(3, ROWS, NK)),
-        u, slaves, faces, slot_of, first,
+        u, slaves, faces, place, patch_of, cand_of,
     )
     arrived = exchange(sent)
     contact = call(

time: 86.3 us -> 85.1 us (0.986)
  Pallas kernels: 15.7 us -> 14.5 us
    pallas_call x14, Pallas kernels: 15.7 us -> 14.5 us  [call(): pl.pallas_call(kernel, out_shape=outs, in_specs=[whole if i < raw else lo...]
where the time goes in v5:
time: 85.1 us; the launch traced here: 84.7 us
  starting transfers between devices  49.7 us (58%)
  waiting for transfers between devices  19.6 us (23%)
  Pallas kernels  14.5 us (17%)
    all_to_all x3, starting transfers between devices, exchange(): lax.all_to_all(chunk, ('len', 'wid'), split_axis=0, concat_axis=0, tiled=...  24.6 us
    ppermute x8, starting transfers between devices, swap_pair(): return (lax.ppermute(first, axis, mate), lax.ppermute(second, axis, other))  16.7 us
    pallas_call x14, Pallas kernels, call(): pl.pallas_call(kernel, out_shape=outs, in_specs=[whole if i < raw else lo...  14.5 us
    all_to_all x3, waiting for transfers between devices, exchange(): lax.all_to_all(chunk, ('len', 'wid'), split_axis=0, concat_axis=0, tiled=...  9.53 us
    ppermute x8, waiting for transfers between devices, swap_pair(): return (lax.ppermute(first, axis, mate), lax.ppermute(second, axis, other))  9.13 us
    ppermute x1, starting transfers between devices, extended(): other = lax.ppermute(near, 'lay', [(0, 1), (1, 0)])  4.55 us
    ppermute x1, starting transfers between devices, surroundings(): other = lax.ppermute(near, 'lay', [(0, 1), (1, 0)])  3.83 us
  transfers between devices with their start and end apart: 13, of which 6 were waited for; matrix products, arithmetic and copies ran while one was open for 0% of the time, Pallas kernels for 7%

profile of v5, /device:TPU:1, one launch (start us, length us, event | category | flops | bytes accessed | tf_op | source)
XLA Modules:
  0.0 84.7 jit_solution(13574872674199998726)
XLA Ops:
  0.6 2.8 %shard_map.122 = (f32[768,128]{1,0:T(8,128)}, f32[64,128]{1,0:T(8,128)S(1)}, bf16[128,64]{1,0:T(8,128)(2,1)S(1)}, f32[3,64,128]{2,1,0:T(8,128)S(1)}, s32[64,128]{1,0:T(8,128)S(1)}, /*index=5*/f32[64,128]{1,0:T(8,128)S(1)}) custom-call(f32[3,32,128]{2,1,0:T(8,128)} %bitcast.30, s32[64,128]{1,0:T(8,128)} %bitcast.39, f32[64,128]{1,0:T(8,128)} %bitcast.40, ...), custom_call_target="tpu_custom_call" | custom-call | tf_op jit(solution)/shard_map/pallas_call | solution.py:564
  3.4 12.0 %all-to-all-start = ((f32[64,1,1536]{2,1,0:T(1,128)}), f32[64,1,1536]{2,1,0:T(1,128)S(1)}, u32[]{:S(2)}, u32[]{:S(2)}) async-start(f32[64,1,1536]{2,1,0:T(1,128)} %bitcast.37), calls=%async_computation | async-start | bytes 786432 | tf_op jit(solution)/shard_map/all_to_all | solution.py:603
  15.4 0.0 copy-start.2
  15.4 0.9 %shard_map.123 = (f32[5,4,8,128]{3,2,1,0:T(8,128)S(1)}, f32[5,8,128]{2,1,0:T(8,128)S(1)}, f32[5,8,128]{2,1,0:T(8,128)S(1)}, f32[3,32,128]{2,1,0:T(8,128)S(1)}, f...) custom-call(f32[3,4,8,128]{3,2,1,0:T(8,128)} %disp.1, f32[4,8,128]{2,1,0:T(8,128)} %lame.1, f32[4,8,128]{2,1,0:T(8,128)} %shear.1, ...), custom_call_target="tpu_custom_call" | custom-call | tf_op jit(solution)/shard_map/pallas_call | solution.py:564
  16.3 0.5 shard_map.124
  16.8 9.5 %all-to-all-done = f32[64,1,1536]{2,1,0:T(1,128)S(1)} async-done(((f32[64,1,1536]{2,1,0:T(1,128)}), f32[64,1,1536]{2,1,0:T(1,128)S(1)}, u32[]{:S(2)}, u32[]{:S(2)}) %all-to-all-start) | async-done | bytes 393248 | tf_op jit(solution)/shard_map/all_to_all | solution.py:603
  26.3 1.1 %shard_map.125 = (f32[512,128]{1,0:T(8,128)}, s32[128,128]{1,0:T(8,128)S(1)}, s32[128,128]{1,0:T(8,128)S(1)}, bf16[128,128]{1,0:T(8,128)(2,1)S(1)}, s32[128,128]{1,0:T(8,128)S(1)}) custom-call(f32[768,128]{1,0:T(8,128)S(1)} %bitcast.20, bf16[128,512]{1,0:T(8,128)(2,1)S(1)} %get-tuple-element.36.table, s32[32,128]{1,0:T(8,128)S(1)} %get-tuple-element.35.faces), custom_call_target="tpu_custom_call" | custom-call | tf_op jit(solution)/shard_map/pallas_call | solution.py:564
  27.4 4.6 %all-to-all-start.1 = ((f32[64,1,1024]{2,1,0:T(1,128)}), f32[64,1,1024]{2,1,0:T(1,128)S(1)}, u32[]{:S(2)}, u32[]{:S(2)}) async-start(f32[64,1,1024]{2,1,0:T(1,128)} %bitcast.25), calls=%async_computation.1 | async-start | bytes 524288 | tf_op jit(solution)/shard_map/all_to_all | solution.py:603
  32.0 1.0 %collective-permute-start = (f32[5,8,128]{2,1,0:T(8,128)S(1)}, f32[5,8,128]{2,1,0:T(8,128)S(1)}, u32[]{:S(2)}, u32[]{:S(2)}) collective-permute-start(f32[5,8,128]{2,1,0:T(8,128)S(1)} %get-tuple-element.46), channel_id=1, source_target_pairs={{0,8},{8,0},{16,24},{24,16},{32,40},{40,32},{48,56},{56,48},{64,72... | collective-permute-start | bytes 61448 | tf_op jit(solution)/shard_map/ppermute | solution.py:579
  33.0 4.3 %collective-permute-start.1 = (f32[5,8,128]{2,1,0:T(8,128)S(1)}, f32[5,8,128]{2,1,0:T(8,128)S(1)}, u32[]{:S(2)}, u32[]{:S(2)}) collective-permute-start(f32[5,8,128]{2,1,0:T(8,128)S(1)} %get-tuple-element.47), channel_id=1, source_target_pairs={{0,120},{8,16},{16,8},{24,32},{32,24},{40,48},{48,40},{56,64},{64,... | collective-permute-start | bytes 61448 | tf_op jit(solution)/shard_map/ppermute | solution.py:579
  37.3 2.0 %collective-permute-done.1.x_second = f32[5,8,128]{2,1,0:T(8,128)S(1)} collective-permute-done((f32[5,8,128]{2,1,0:T(8,128)S(1)}, f32[5,8,128]{2,1,0:T(8,128)S(1)}, u32[]{:S(2)}, u32[]{:S(2)}) %collective-permute-start.1) | collective-permute-done | bytes 20512 | tf_op jit(solution)/shard_map/ppermute | solution.py:579
  39.3 3.8 %collective-permute-start.2 = (f32[5,6,8,128]{3,2,1,0:T(8,128)S(1)}, f32[5,6,8,128]{3,2,1,0:T(8,128)S(1)}, u32[]{:S(2)}, u32[]{:S(2)}) collective-permute-start(f32[5,6,8,128]{3,2,1,0:T(8,128)S(1)} %shard_map.127.near), channel_id=1, source_target_pairs={{0,1},{1,0},{2,3},{3,2},{4,5},{5,4},{6,7},{7,6},{8,9},{9,8},{10,11... | collective-permute-start | bytes 368648 | tf_op jit(solution)/shard_map/ppermute | solution.py:586
  43.1 1.0 %collective-permute-done.2.other = f32[5,6,8,128]{3,2,1,0:T(8,128)S(1)} collective-permute-done((f32[5,6,8,128]{3,2,1,0:T(8,128)S(1)}, f32[5,6,8,128]{3,2,1,0:T(8,128)S(1)}, u32[]{:S(2)}, u32[]{:S(2)}) %collective-permute-start.2) | collective-permute-done | bytes 122912 | tf_op jit(solution)/shard_map/ppermute | solution.py:586
  44.1 1.3 %collective-permute-start.3 = (f32[10,8,128]{2,1,0:T(8,128)S(1)}, f32[10,8,128]{2,1,0:T(8,128)S(1)}, u32[]{:S(2)}, u32[]{:S(2)}) collective-permute-start(f32[10,8,128]{2,1,0:T(8,128)S(1)} %get-tuple-element.48), channel_id=1, source_target_pairs={{0,2},{2,0},{4,6},{6,4},{1,3},{3,1},{5,7},{7,5},{8,10},{10,8},{12,... | collective-permute-start | bytes 122888 | tf_op jit(solution)/shard_map/ppermute | solution.py:579
  45.4 1.7 %collective-permute-start.4 = (f32[10,8,128]{2,1,0:T(8,128)S(1)}, f32[10,8,128]{2,1,0:T(8,128)S(1)}, u32[]{:S(2)}, u32[]{:S(2)}) collective-permute-start(f32[10,8,128]{2,1,0:T(8,128)S(1)} %get-tuple-element.49), channel_id=1, source_target_pairs={{0,6},{2,4},{4,2},{6,0},{1,7},{3,5},{5,3},{7,1},{8,14},{10,12},{12... | collective-permute-start | bytes 122888 | tf_op jit(solution)/shard_map/ppermute | solution.py:579
  47.2 0.0 collective-permute-done.3.y_low
  47.2 2.3 %collective-permute-done.4.y_high = f32[10,8,128]{2,1,0:T(8,128)S(1)} collective-permute-done((f32[10,8,128]{2,1,0:T(8,128)S(1)}, f32[10,8,128]{2,1,0:T(8,128)S(1)}, u32[]{:S(2)}, u32[]{:S(2)}) %collective-permute-start.4) | collective-permute-done | bytes 40992 | tf_op jit(solution)/shard_map/ppermute | solution.py:579
  49.5 0.4 shard_map.129
  49.9 1.6 %shard_map.126.reaction = f32[3,32,128]{2,1,0:T(8,128)S(1)} custom-call(f32[768,128]{1,0:T(8,128)S(1)} %bitcast.21, f32[512,128]{1,0:T(8,128)S(1)} %copy-done.1, s32[128,128]{1,0:T(8,128)S(1)} %get-tuple-element.42.face_row, s32[128,128]{1,0:T(8,128)S(1)} %get-tuple-element.43.face_lane, f32[3,32,128]{2,1,0:T(8,128)S(1)} %get-tuple-element.44.normals), custom_call_target="tpu_custom_call" | custom-call | tf_op jit(solution)/shard_map/pallas_call | solution.py:564
  51.5 0.0 all-to-all-done.1
  51.5 1.2 %shard_map.130 = (f32[3,32,128]{2,1,0:T(8,128)S(1)}, f32[3,32,128]{2,1,0:T(8,128)S(1)}, f32[3,8,128]{2,1,0:T(8,128)S(1)}, f32[3,8,128]{2,1,0:T(8,128)S(1)}) custom-call(f32[512,128]{1,0:T(8,128)S(1)} %bitcast.26, f32[64,128]{1,0:T(8,128)S(1)} %get-tuple-element.38.slot_of, f32[3,64,128]{2,1,0:T(8,128)S(1)} %get-tuple-element.39.at_slaves, ...), custom_call_target="tpu_custom_call" | custom-call | tf_op jit(solution)/shard_map/pallas_call | solution.py:564
  52.7 2.5 %shard_map.133 = (f32[896,128]{1,0:T(8,128)}, f32[3,64,128]{2,1,0:T(8,128)S(1)}, f32[3,32,128]{2,1,0:T(8,128)S(1)}) custom-call(f32[3,32,128]{2,1,0:T(8,128)S(1)} %get-tuple-element.53.u, s32[64,128]{1,0:T(8,128)S(1)} %get-tuple-element.41.slaves, s32[32,128]{1,0:T(8,128)S(1)} %get-tuple-element.35.faces, bf16[128,64]{1,0:T(8,128)(2,1)S(1)} %get-tuple-element.59.place, ...), custom_call_target="tpu_custom_call" | custom-call | tf_op jit(solution)/shard_map/pallas_call | solution.py:564
  55.2 8.0 %all-to-all-start.2 = ((f32[64,1,1792]{2,1,0:T(1,128)}), f32[64,1,1792]{2,1,0:T(1,128)S(1)}, u32[]{:S(2)}, u32[]{:S(2)}) async-start(f32[64,1,1792]{2,1,0:T(1,128)} %bitcast.23), calls=%async_computation.2 | async-start | bytes 917504 | tf_op jit(solution)/shard_map/all_to_all | solution.py:603
  63.2 1.1 %collective-permute-start.5 = (f32[3,8,128]{2,1,0:T(8,128)S(1)}, f32[3,8,128]{2,1,0:T(8,128)S(1)}, u32[]{:S(2)}, u32[]{:S(2)}) collective-permute-start(f32[3,8,128]{2,1,0:T(8,128)S(1)} %get-tuple-element.54), channel_id=1, source_target_pairs={{0,8},{8,0},{16,24},{24,16},{32,40},{40,32},{48,56},{56,48},{64,72... | collective-permute-start | bytes 36872 | tf_op jit(solution)/shard_map/ppermute | solution.py:579
  64.3 4.2 %collective-permute-start.6 = (f32[3,8,128]{2,1,0:T(8,128)S(1)}, f32[3,8,128]{2,1,0:T(8,128)S(1)}, u32[]{:S(2)}, u32[]{:S(2)}) collective-permute-start(f32[3,8,128]{2,1,0:T(8,128)S(1)} %get-tuple-element.55), channel_id=1, source_target_pairs={{0,120},{8,16},{16,8},{24,32},{32,24},{40,48},{48,40},{56,64},{64,... | collective-permute-start | bytes 36872 | tf_op jit(solution)/shard_map/ppermute | solution.py:579
  68.5 2.7 %collective-permute-done.6.x_second = f32[3,8,128]{2,1,0:T(8,128)S(1)} collective-permute-done((f32[3,8,128]{2,1,0:T(8,128)S(1)}, f32[3,8,128]{2,1,0:T(8,128)S(1)}, u32[]{:S(2)}, u32[]{:S(2)}) %collective-permute-start.6) | collective-permute-done | bytes 12320 | tf_op jit(solution)/shard_map/ppermute | solution.py:579
  71.2 1.6 %collective-permute-start.7 = (f32[3,8,128]{2,1,0:T(8,128)S(1)}, f32[3,8,128]{2,1,0:T(8,128)S(1)}, u32[]{:S(2)}, u32[]{:S(2)}) collective-permute-start(f32[3,8,128]{2,1,0:T(8,128)S(1)} %get-tuple-element.56), channel_id=1, source_target_pairs={{0,2},{2,0},{4,6},{6,4},{1,3},{3,1},{5,7},{7,5},{8,10},{10,8},{12,... | collective-permute-start | bytes 36872 | tf_op jit(solution)/shard_map/ppermute | solution.py:579
  72.7 1.6 %collective-permute-start.8 = (f32[3,8,128]{2,1,0:T(8,128)S(1)}, f32[3,8,128]{2,1,0:T(8,128)S(1)}, u32[]{:S(2)}, u32[]{:S(2)}) collective-permute-start(f32[3,8,128]{2,1,0:T(8,128)S(1)} %get-tuple-element.57), channel_id=1, source_target_pairs={{0,6},{2,4},{4,2},{6,0},{1,7},{3,5},{5,3},{7,1},{8,14},{10,12},{12... | collective-permute-start | bytes 36872 | tf_op jit(solution)/shard_map/ppermute | solution.py:579
  74.4 2.1 %collective-permute-done.8.y_second = f32[3,8,128]{2,1,0:T(8,128)S(1)} collective-permute-done((f32[3,8,128]{2,1,0:T(8,128)S(1)}, f32[3,8,128]{2,1,0:T(8,128)S(1)}, u32[]{:S(2)}, u32[]{:S(2)}) %collective-permute-start.8) | collective-permute-done | bytes 12320 | tf_op jit(solution)/shard_map/ppermute | solution.py:579
  76.5 4.6 %collective-permute-start.9 = (f32[3,6,16,128]{3,2,1,0:T(8,128)S(1)}, f32[3,6,16,128]{3,2,1,0:T(8,128)S(1)}, u32[]{:S(2)}, u32[]{:S(2)}) collective-permute-start(f32[3,6,16,128]{3,2,1,0:T(8,128)S(1)} %shard_map.132.near), channel_id=1, source_target_pairs={{0,1},{1,0},{2,3},{3,2},{4,5},{5,4},{6,7},{7,6},{8,9},{9,8},{10,11... | collective-permute-start | bytes 442376 | tf_op jit(solution)/shard_map/ppermute | solution.py:597
  81.1 2.6 %shard_map.134 = f32[3,32,128]{2,1,0:T(8,128)S(1)} custom-call(f32[896,128]{1,0:T(8,128)S(1)} %bitcast.24, f32[896,128]{1,0:T(8,128)S(1)} %copy-done, f32[768,128]{1,0:T(8,128)S(1)} %bitcast.22, s32[128,128]{1,0:T(8,128)S(1)} %get-tuple-element.42.face_row, s32[128,128]{1,0:T(8,128)S(1)} %get-tuple-element.43.face_lane, ...), custom_call_target="tpu_custom_call" | custom-call | tf_op jit(solution)/shard_map/pallas_call | solution.py:564
  83.7 1.0 %shard_map.135 = (f32[3,4,8,128]{3,2,1,0:T(8,128)}, f32[3,4,8,128]{3,2,1,0:T(8,128)}) custom-call(f32[3,6,16,128]{3,2,1,0:T(8,128)S(1)} %shard_map.132.near, f32[3,6,16,128]{3,2,1,0:T(8,128)S(1)} %collective-permute-done.9.other, f32[2,5,16,128]{3,2,1,0:T(8,128)S(1)} %get-tuple-element.58.moduli, f32[3,4,8,128]{3,2,1,0:T(8,128)S(1)} %bitcast.33, ...), custom_call_target="tpu_custom_call" | custom-call | tf_op jit(solution)/shard_map/pallas_call | solution.py:564
  (14 shorter events, 0.1 us)
Async XLA Ops:
  3.4 22.9 %all-to-all-start = ((f32[64,1,1536]{2,1,0:T(1,128)}), f32[64,1,1536]{2,1,0:T(1,128)S(1)}, u32[]{:S(2)}, u32[]{:S(2)}) async-start(f32[64,1,1536]{2,1,0:T(1,128)} %bitcast.37), calls=%async_computation | async-start | bytes 786432 | tf_op jit(solution)/shard_map/all_to_all | solution.py:603
  15.4 0.9 %copy-start.2 = (f32[3,4,8,128]{3,2,1,0:T(8,128)S(1)}, f32[3,4,8,128]{3,2,1,0:T(8,128)}, u32[]{:S(2)}) copy-start(f32[3,4,8,128]{3,2,1,0:T(8,128)} %disp.1) | copy-start | bytes 147460
  27.4 24.1 %all-to-all-start.1 = ((f32[64,1,1024]{2,1,0:T(1,128)}), f32[64,1,1024]{2,1,0:T(1,128)S(1)}, u32[]{:S(2)}, u32[]{:S(2)}) async-start(f32[64,1,1024]{2,1,0:T(1,128)} %bitcast.25), calls=%async_computation.1 | async-start | bytes 524288 | tf_op jit(solution)/shard_map/all_to_all | solution.py:603
  32.0 5.3 %collective-permute-start = (f32[5,8,128]{2,1,0:T(8,128)S(1)}, f32[5,8,128]{2,1,0:T(8,128)S(1)}, u32[]{:S(2)}, u32[]{:S(2)}) collective-permute-start(f32[5,8,128]{2,1,0:T(8,128)S(1)} %get-tuple-element.46), channel_id=1, source_target_pairs={{0,8},{8,0},{16,24},{24,16},{32,40},{40,32},{48,56},{56,48},{64,72... | collective-permute-start | bytes 61448 | tf_op jit(solution)/shard_map/ppermute | solution.py:579
  33.0 6.3 %collective-permute-start.1 = (f32[5,8,128]{2,1,0:T(8,128)S(1)}, f32[5,8,128]{2,1,0:T(8,128)S(1)}, u32[]{:S(2)}, u32[]{:S(2)}) collective-permute-start(f32[5,8,128]{2,1,0:T(8,128)S(1)} %get-tuple-element.47), channel_id=1, source_target_pairs={{0,120},{8,16},{16,8},{24,32},{32,24},{40,48},{48,40},{56,64},{64,... | collective-permute-start | bytes 61448 | tf_op jit(solution)/shard_map/ppermute | solution.py:579
  39.3 10.6 %copy-start.1 = (f32[512,128]{1,0:T(8,128)S(1)}, f32[512,128]{1,0:T(8,128)}, u32[]{:S(2)}) copy-start(f32[512,128]{1,0:T(8,128)} %get-tuple-element.37.frames) | copy-start | bytes 786436
  39.3 4.8 %collective-permute-start.2 = (f32[5,6,8,128]{3,2,1,0:T(8,128)S(1)}, f32[5,6,8,128]{3,2,1,0:T(8,128)S(1)}, u32[]{:S(2)}, u32[]{:S(2)}) collective-permute-start(f32[5,6,8,128]{3,2,1,0:T(8,128)S(1)} %shard_map.127.near), channel_id=1, source_target_pairs={{0,1},{1,0},{2,3},{3,2},{4,5},{5,4},{6,7},{7,6},{8,9},{9,8},{10,11... | collective-permute-start | bytes 368648 | tf_op jit(solution)/shard_map/ppermute | solution.py:586
  44.1 3.0 %collective-permute-start.3 = (f32[10,8,128]{2,1,0:T(8,128)S(1)}, f32[10,8,128]{2,1,0:T(8,128)S(1)}, u32[]{:S(2)}, u32[]{:S(2)}) collective-permute-start(f32[10,8,128]{2,1,0:T(8,128)S(1)} %get-tuple-element.48), channel_id=1, source_target_pairs={{0,2},{2,0},{4,6},{6,4},{1,3},{3,1},{5,7},{7,5},{8,10},{10,8},{12,... | collective-permute-start | bytes 122888 | tf_op jit(solution)/shard_map/ppermute | solution.py:579
  45.4 4.1 %collective-permute-start.4 = (f32[10,8,128]{2,1,0:T(8,128)S(1)}, f32[10,8,128]{2,1,0:T(8,128)S(1)}, u32[]{:S(2)}, u32[]{:S(2)}) collective-permute-start(f32[10,8,128]{2,1,0:T(8,128)S(1)} %get-tuple-element.49), channel_id=1, source_target_pairs={{0,6},{2,4},{4,2},{6,0},{1,7},{3,5},{5,3},{7,1},{8,14},{10,12},{12... | collective-permute-start | bytes 122888 | tf_op jit(solution)/shard_map/ppermute | solution.py:579
  55.2 25.9 %copy-start = (f32[896,128]{1,0:T(8,128)S(1)}, f32[896,128]{1,0:T(8,128)}, u32[]{:S(2)}) copy-start(f32[896,128]{1,0:T(8,128)} %get-tuple-element.62.sent) | copy-start | bytes 1376260
  55.2 25.9 %all-to-all-start.2 = ((f32[64,1,1792]{2,1,0:T(1,128)}), f32[64,1,1792]{2,1,0:T(1,128)S(1)}, u32[]{:S(2)}, u32[]{:S(2)}) async-start(f32[64,1,1792]{2,1,0:T(1,128)} %bitcast.23), calls=%async_computation.2 | async-start | bytes 917504 | tf_op jit(solution)/shard_map/all_to_all | solution.py:603
  63.2 5.3 %collective-permute-start.5 = (f32[3,8,128]{2,1,0:T(8,128)S(1)}, f32[3,8,128]{2,1,0:T(8,128)S(1)}, u32[]{:S(2)}, u32[]{:S(2)}) collective-permute-start(f32[3,8,128]{2,1,0:T(8,128)S(1)} %get-tuple-element.54), channel_id=1, source_target_pairs={{0,8},{8,0},{16,24},{24,16},{32,40},{40,32},{48,56},{56,48},{64,72... | collective-permute-start | bytes 36872 | tf_op jit(solution)/shard_map/ppermute | solution.py:579
  64.3 6.8 %collective-permute-start.6 = (f32[3,8,128]{2,1,0:T(8,128)S(1)}, f32[3,8,128]{2,1,0:T(8,128)S(1)}, u32[]{:S(2)}, u32[]{:S(2)}) collective-permute-start(f32[3,8,128]{2,1,0:T(8,128)S(1)} %get-tuple-element.55), channel_id=1, source_target_pairs={{0,120},{8,16},{16,8},{24,32},{32,24},{40,48},{48,40},{56,64},{64,... | collective-permute-start | bytes 36872 | tf_op jit(solution)/shard_map/ppermute | solution.py:579
  71.2 3.2 %collective-permute-start.7 = (f32[3,8,128]{2,1,0:T(8,128)S(1)}, f32[3,8,128]{2,1,0:T(8,128)S(1)}, u32[]{:S(2)}, u32[]{:S(2)}) collective-permute-start(f32[3,8,128]{2,1,0:T(8,128)S(1)} %get-tuple-element.56), channel_id=1, source_target_pairs={{0,2},{2,0},{4,6},{6,4},{1,3},{3,1},{5,7},{7,5},{8,10},{10,8},{12,... | collective-permute-start | bytes 36872 | tf_op jit(solution)/shard_map/ppermute | solution.py:579
  72.7 3.8 %collective-permute-start.8 = (f32[3,8,128]{2,1,0:T(8,128)S(1)}, f32[3,8,128]{2,1,0:T(8,128)S(1)}, u32[]{:S(2)}, u32[]{:S(2)}) collective-permute-start(f32[3,8,128]{2,1,0:T(8,128)S(1)} %get-tuple-element.57), channel_id=1, source_target_pairs={{0,6},{2,4},{4,2},{6,0},{1,7},{3,5},{5,3},{7,1},{8,14},{10,12},{12... | collective-permute-start | bytes 36872 | tf_op jit(solution)/shard_map/ppermute | solution.py:579
  76.5 7.1 %collective-permute-start.9 = (f32[3,6,16,128]{3,2,1,0:T(8,128)S(1)}, f32[3,6,16,128]{3,2,1,0:T(8,128)S(1)}, u32[]{:S(2)}, u32[]{:S(2)}) collective-permute-start(f32[3,6,16,128]{3,2,1,0:T(8,128)S(1)} %shard_map.132.near), channel_id=1, source_target_pairs={{0,1},{1,0},{2,3},{3,2},{4,5},{5,4},{6,7},{7,6},{8,9},{9,8},{10,11... | collective-permute-start | bytes 442376 | tf_op jit(solution)/shard_map/ppermute | solution.py:597
